TPU v7x, 32 devices: a whole 2x2x4 slice. The times are simulated.
32 devices in a mesh: dp: 8 (over y, x, core), space: 4 (over z).
Axes of the slice: x: 2, y: 2, z: 4, core: 2. Of those that a mesh axis runs over, the one named last changes fastest.
Arguments:
- inputs: bfloat16 [64, 32, 32, 1024], P('dp', None, 'space'), may hold values from 0 to 2
- conv_in: bfloat16 [64, 864], replicated, may hold values from -0.21875 to 0.21875
- norm_gain: float32 [64], replicated, may hold values from 0.5 to 1.5
- norm_shift: float32 [64], replicated, may hold values from -3 to 3
- conv_out: bfloat16 [128, 1728], replicated, may hold values from -0.15625 to 0.15625
- dense_in: bfloat16 [65536, 128], replicated, may hold values from -0.0234375 to 0.0234375
- dense_out: bfloat16 [128, 4], replicated, may hold values from -0.5 to 0.5
- targets: float32 [64, 4], P(('dp', 'space')), may hold values from -6 to 6
Outputs:
- grad_conv_in: float32 [64, 864], replicated
- grad_norm: float32 [2, 64], replicated
- grad_conv_out: float32 [128, 1728], replicated
- grad_dense_in: float32 [65536, 128], P(('dp', 'space'))
- grad_dense_out: float32 [128, 4], replicated
- predictions: float32 [64, 4], P(('dp', 'space'))
All inputs are finite; a program needn't handle non-finite values.
Results may differ from a plain program's by a relative error of at most 0.015.
Values may be sent and summed in bfloat16 or wider, within the bound.
No kernel may reach another device: no remote copies, remote signals or barrier semaphores. Data moves between devices by JAX's collectives and lax.ppermute only.
A program may use at most 256 MiB of HBM per device.

v0:
```python
import jax
import jax.numpy as jnp
from jax import lax
from jax.sharding import PartitionSpec as P

C_OUT = 128
GRID = 32


norm_epsilon = 1e-05


def extended_2(cells, sides, width):
    for axis, dim in sides:
        count = lax.axis_size(axis)
        ends = count - 1
        head = lax.slice_in_dim(cells, 0, width, axis=dim)
        tail = lax.slice_in_dim(cells, cells.shape[dim] - width, cells.shape[dim], axis=dim)
        cells = jnp.concatenate(
            [
                lax.ppermute(tail, axis, [(i, (i + 1) % count) for i in range(ends)]),
                cells,
                lax.ppermute(head, axis, [((i + 1) % count, i) for i in range(ends)]),
            ],
            axis=dim,
        )
    return cells


def leaky_relu(values):
    return 0.65 * values + 0.35 * values * jnp.tanh(values)


def slope_of(values):
    bent = jnp.tanh(values)
    return 0.65 + 0.35 * (bent + values * (1.0 - bent * bent))


def plane_shift(volume, step_y, step_z, extent):
    plane_len = extent * extent
    offset = step_y * extent + step_z
    margin = extent + 1
    pad_widths = [(0, 0)] * (volume.ndim - 1) + [(margin, margin)]
    padded = jnp.pad(volume, pad_widths)
    shifted = lax.slice_in_dim(
        padded, margin + offset, margin + offset + plane_len, axis=volume.ndim - 1
    )
    column = lax.broadcasted_iota(jnp.int32, (plane_len,), 0) % extent
    inside = ((column + step_z >= 0) & (column + step_z < extent)).astype(volume.dtype)
    return shifted * inside


def columns(slab_ext, planes, extent):
    pieces = []
    for step_x in (-1, 0, 1):
        plane_set = lax.slice_in_dim(slab_ext, 1 + step_x, 1 + step_x + planes, axis=1)
        for step_y in (-1, 0, 1):
            for step_z in (-1, 0, 1):
                pieces.append(plane_shift(plane_set, step_y, step_z, extent))
    stacked = jnp.stack(pieces, 0)
    return stacked.reshape(len(pieces) * slab_ext.shape[0], planes * extent * extent)


def pad_planes(volume, extent):
    shaped = volume.reshape(volume.shape[0], extent, extent * extent)
    return jnp.pad(shaped, ((0, 0), (1, 1), (0, 0)))


def pool_slab(active, planes, extent):
    samples, channels = (active.shape[0], active.shape[1])
    blocks = active.reshape(samples, channels, planes // 2, 2, extent // 2, 2, extent // 2, 2)
    return (blocks.sum(axis=(3, 5, 7)) * 0.125).reshape(samples, channels, -1)


def unpool_slab(gradient, planes, extent):
    samples, channels = (gradient.shape[0], gradient.shape[1])
    blocks = gradient.reshape(samples, channels, planes // 2, 1, extent // 2, 1, extent // 2, 1)
    wide = jnp.broadcast_to(
        blocks, (samples, channels, planes // 2, 2, extent // 2, 2, extent // 2, 2)
    )
    return wide.reshape(samples, channels, planes * extent * extent) * 0.125


def shards(inputs, conv_in, norm_gain, norm_shift, conv_out, dense_in, dense_out, targets):
    half_grid = GRID // 2
    quarter = GRID // 4
    cell_count = inputs.shape[0] * GRID**3
    extended = extended_2(inputs, (("space", 2),), 1)
    planes = extended.shape[2] - 2

    def first_conv(slab_ext):
        return jnp.dot(conv_in, columns(slab_ext, planes, GRID), preferred_element_type=jnp.float32)

    first_out = lax.map(first_conv, extended)
    local_sum = jnp.sum(first_out, axis=(0, 2))
    average = lax.psum(local_sum, "space") / cell_count
    centred = first_out - average[None, :, None]
    variance = lax.psum(jnp.sum(centred * centred, axis=(0, 2)), "space") / cell_count
    inverse = lax.rsqrt(variance + norm_epsilon)
    whitened = centred * inverse[None, :, None]
    normed = norm_gain[None, :, None] * whitened + norm_shift[None, :, None]
    pooled = pool_slab(leaky_relu(normed), planes, GRID).astype(jnp.bfloat16)
    samples_pooled = lax.all_to_all(pooled, "space", split_axis=0, concat_axis=2, tiled=True)

    def second_conv(volume):
        return jnp.dot(
            conv_out,
            columns(pad_planes(volume, half_grid), half_grid, half_grid),
            preferred_element_type=jnp.float32,
        )

    second_out = lax.map(second_conv, samples_pooled)
    local_samples = second_out.shape[0]
    features = (
        pool_slab(leaky_relu(second_out), half_grid, half_grid)
        .reshape(local_samples, -1)
        .astype(jnp.bfloat16)
    )
    hidden_pre = jnp.dot(features, dense_in, preferred_element_type=jnp.float32)
    hidden = leaky_relu(hidden_pre).astype(jnp.bfloat16)
    predictions = jnp.dot(hidden, dense_out, preferred_element_type=jnp.float32)
    misfit = predictions - targets
    grad_out_local = jnp.dot(hidden.astype(jnp.float32).T, misfit, precision=lax.Precision.HIGHEST)
    back_hidden = (
        jnp.dot(misfit, dense_out.astype(jnp.float32).T, precision=lax.Precision.HIGHEST)
        * slope_of(hidden_pre)
    ).astype(jnp.bfloat16)
    partial_rows = lax.psum_scatter(
        lax.dot_general(
            features, back_hidden, (((0,), (0,)), ((), ())), preferred_element_type=jnp.float32
        ).astype(jnp.bfloat16),
        "dp",
        scatter_dimension=0,
        tiled=True,
    )
    grad_dense_in = lax.psum_scatter(partial_rows, "space", scatter_dimension=0, tiled=True).astype(
        jnp.float32
    )
    back_features = lax.dot_general(
        back_hidden, dense_in, (((1,), (1,)), ((), ())), preferred_element_type=jnp.float32
    )
    back_features = back_features.reshape(local_samples, C_OUT, quarter**3)
    back_second = (unpool_slab(back_features, half_grid, half_grid) * slope_of(second_out)).astype(
        jnp.bfloat16
    )

    def second_back(running, couple):
        volume, gradient = couple
        padded = pad_planes(volume, half_grid)
        patches = columns(padded, half_grid, half_grid)
        running = running + lax.dot_general(
            gradient, patches, (((1,), (1,)), ((), ())), preferred_element_type=jnp.float32
        )
        patch_grad = lax.dot_general(
            conv_out, gradient, (((0,), (0,)), ((), ())), preferred_element_type=jnp.float32
        )
        _, unfold = jax.vjp(
            lambda whole_pad: columns(whole_pad, half_grid, half_grid), padded.astype(jnp.float32)
        )
        volume_grad = unfold(patch_grad)[0][:, 1:-1, :]
        return (running, volume_grad.reshape(volume.shape).astype(jnp.bfloat16))

    grad_conv_out, back_pooled = lax.scan(
        second_back, jnp.zeros(conv_out.shape, jnp.float32), (samples_pooled, back_second)
    )
    back_slab = lax.all_to_all(back_pooled, "space", split_axis=2, concat_axis=0, tiled=True)
    back_active = unpool_slab(back_slab.astype(jnp.float32), planes, GRID) * slope_of(normed)
    sum_grad = jnp.sum(back_active, axis=(0, 2))
    sum_xgrad = jnp.sum(back_active * whitened, axis=(0, 2))
    group_grad, group_xgrad = lax.psum((sum_grad, sum_xgrad), "space")
    back_first = (norm_gain * inverse)[None, :, None] * (
        back_active
        - group_grad[None, :, None] / cell_count
        - whitened * group_xgrad[None, :, None] / cell_count
    )
    back_first = back_first.astype(jnp.bfloat16)

    def first_back(running, couple):
        slab_ext, gradient = couple
        patches = columns(slab_ext, planes, GRID)
        return (
            running
            + lax.dot_general(
                gradient, patches, (((1,), (1,)), ((), ())), preferred_element_type=jnp.float32
            ),
            None,
        )

    grad_conv_in, _ = lax.scan(
        first_back, jnp.zeros(conv_in.shape, jnp.float32), (extended, back_first)
    )
    grad_norm_local = jnp.stack([sum_xgrad, sum_grad])
    summed = lax.psum(
        (grad_conv_in, grad_norm_local, grad_conv_out, grad_out_local), ("dp", "space")
    )
    return (summed[0], summed[1], summed[2], grad_dense_in, summed[3], predictions)


def solution(mesh):
    placed = (P("dp", None, "space", None), P(), P(), P(), P(), P(), P(), P(("dp", "space"), None))
    return jax.shard_map(
        shards,
        mesh=mesh,
        in_specs=placed,
        out_specs=(P(), P(), P(), P(("dp", "space"), None), P(), P(("dp", "space"), None)),
        check_vma=False,
    )
```

profile of v0, /device:TPU:0, one launch (start us, length us, event | category | flops | bytes accessed | tf_op | source)
XLA Modules:
  0.0 1239.6 jit_solution(6425463289631794915)
XLA Ops:
  44.1 170.7 %while.52 = (s32[]{:T(128)}, f32[8,64,8192]{2,1,0:T(8,128)}, bf16[8,32,10,1024]{3,2,1,0:T(8,128)(2,1)}, bf16[64,864]{1,0:T(8,128)(2,1)S(1)}, s32[]{:T(128)}) while((s32[]{:T(128)}, f32[8,64,8192]{2,1,0:T(8,128)}, bf16[8,32,10,1024]{3,2,1,0:T(8,128)(2,1)}, bf16[64,864]{1,0:T(8,128)(2,1)S(1)}, s32[]{:T(128)}) %tuple.218), condition=%wide.region_1.2_spmd, body=%wide.region_0.1_spmd.sunk | while | flops 934313984 | bytes 77505088 | solution.py:94
  214.8 23.5 %copy.52 = f32[8,64,8192]{1,0,2:T(8,128)} copy(f32[8,64,8192]{2,1,0:T(8,128)} %get-tuple-element.251) | data formatting | bytes 33554432 | tf_op jit(solution)/shard_map/while | solution.py:94
  255.2 15.0 %multiply_reduce_fusion.1 = f32[64]{0:T(128)S(1)} fusion(f32[8,64,8192]{1,0,2:T(8,128)} %copy.52, f32[64]{0:T(128)S(1)} %broadcast_multiply_fusion.1), kind=kLoop, calls=%fused_computation.417 | loop fusion | flops 12582848 | bytes 16777728 | tf_op jit(solution)/shard_map/reduce_sum | solution.py:98
  279.8 25.5 %fusion.222 = f32[8,64,8192]{1,0,2:T(8,128)} fusion(f32[8,64,8192]{1,0,2:T(8,128)} %copy.52, f32[64]{0:T(128)S(1)} %copy-done.23, f32[64]{0:T(128)S(1)} %get-tuple-element.447, f32[64]{0:T(128)S(1)} %copy-done.19, f32[64]{0:T(128)S(1)} %broadcast_multiply_fusion.1), kind=kLoop, calls=%fused_computation.415 | loop fusion | flops 33554432 | bytes 33555456 | tf_op jit(solution)/shard_map/add | solution.py:31
  305.3 14.9 %reduce_sum.56 = f32[8,64,4,16,16]{1,0,4,3,2:T(8,128)} reduce(f32[8,64,4,2,16,2,16,2]{1,0,7,6,5,4,3,2:T(8,128)} %bitcast.865, f32[]{:T(128)} %constant.649.clone.1), dimensions={3,5,7}, to_apply=%region_6.7 | reduce | flops 3670016 | bytes 18874372 | tf_op jit(solution)/shard_map/reduce_sum | solution.py:72
  331.2 21.0 %all-to-all-done = bf16[8,64,1024]{2,1,0:T(8,128)(2,1)S(1)} async-done(((bf16[8,64,1024]{2,1,0:T(8,128)(2,1)}), bf16[8,64,1024]{2,1,0:T(8,128)(2,1)S(1)}, u32[]{:S(2)}, u32[]{:S(2)}) %all-to-all-start) | async-done | bytes 1048608 | tf_op jit(solution)/shard_map/all_to_all | solution.py:103
  352.4 35.7 %while.53 = (s32[]{:T(128)}, f32[2,128,4096]{1,2,0:T(8,128)}, bf16[2,64,4096]{2,1,0:T(8,128)(2,1)S(1)}, bf16[128,1728]{0,1:T(8,128)(2,1)S(1)}, s32[]{:T(128)}) while((s32[]{:T(128)}, f32[2,128,4096]{1,2,0:T(8,128)}, bf16[2,64,4096]{2,1,0:T(8,128)(2,1)S(1)}, bf16[128,1728]{0,1:T(8,128)(2,1)S(1)}, s32[]{:T(128)}) %tuple.217), condition=%wide.region_8.9_spmd, body=%wide.region_7.8_spmd.sunk | while | flops 1840259072 | bytes 77004352 | solution.py:112
  458.9 268.3 %while.54 = (s32[]{:T(128)}, f32[128,1728]{0,1:T(8,128)}, bf16[2,64,4096]{2,1,0:T(8,128)(2,1)}, bf16[2,128,4096]{1,2,0:T(8,128)(2,1)S(1)}, bf16[2,64,4096]{2,1,0...) while((s32[]{:T(128)}, f32[128,1728]{0,1:T(8,128)}, ...), condition=%wide.region_11.12_spmd.clone, body=%wide.region_10.11_spmd.clone.sunk | while | flops 3666803200 | bytes 362422176 | solution.py:163
  481.5 12.6 %convolution_bitcast_fusion.4 = f32[1728,4096]{1,0:T(8,128)} fusion(bf16[128,1728]{0,1:T(8,128)(2,1)} %get-tuple-element.749, bf16[2,128,4096]{1,2,0:T(8,128)(2,1)S(1)} %get-tuple-element.747, s32[]{:T(128)} %get-tuple-element.736), kind=kOutput, calls=%fused_computation.158.clone.1 | convolution fusion | flops 1811939328 | bytes 29802500 | tf_op jit(solution)/shard_map/while/body/eval_jaxpr/dot_general | solution.py:154
  602.1 12.2 convolution_bitcast_fusion.4
  738.6 23.6 %all-to-all-done.1 = bf16[4,2,65536]{2,1,0:T(2,128)(2,1)S(1)} async-done(((bf16[4,2,65536]{2,1,0:T(2,128)(2,1)}), bf16[4,2,65536]{2,1,0:T(2,128)(2,1)S(1)}, u32[]{:S(2)}, u32[]{:S(2)}) %all-to-all-start.1) | async-done | bytes 1048608 | tf_op jit(solution)/shard_map/all_to_all | solution.py:166
  778.5 22.3 %fusion.223 = (f32[64]{0:T(128)S(1)}, f32[64]{0:T(128)S(1)}) fusion(f32[8,64,8192]{1,0,2:T(8,128)} %copy.52, f32[8,64,4,16,16]{1,0,4,3,2:T(8,128)S(1)} %copy.62, f32[64]{0:T(128)S(1)} %copy-done.24, f32[64]{0:T(128)S(1)} %copy-done.22, f32[64]{0:T(128)S(1)} %copy-done.20, f32[64]{0:T(128)S(1)} %copy-done.18), kind=kLoop, calls=%fused_computation.419 | loop fusion | flops 58720128 | bytes 18875904 | tf_op jit(solution)/shard_map/reduce_sum | solution.py:168
  810.6 25.9 %multiply_convert_fusion = bf16[8,64,8192]{1,0,2:T(8,128)(2,1)} fusion(f32[8,64,8192]{1,0,2:T(8,128)} %copy.52, f32[64]{0:T(128)S(1)} %get-tuple-element.374, f32[64]{0:T(128)S(1)} %broadcast_multiply_fusion, f32[8,64,4,16,16]{1,0,4,3,2:T(8,128)} %copy-done.11, f32[64]{0:T(128)S(1)} %copy-done.24, f32[64]{0:T(128)S(1)} %copy-done.22, f32[64]{0:T(128)S(1)} %copy-done.20, ...), kind=kLoop, calls=%fused_computation.412 | loop fusion | flops 71303168 | bytes 27264768 | tf_op jit(solution)/shard_map/convert_element_type | solution.py:176
  836.5 18.4 %copy.63 = bf16[8,64,8192]{2,1,0:T(8,128)(2,1)} copy(bf16[8,64,8192]{1,0,2:T(8,128)(2,1)} %multiply_convert_fusion) | data formatting | bytes 16777216
  855.0 242.5 %while.55 = (s32[]{:T(128)}, f32[64,864]{1,0:T(8,128)S(1)}, bf16[8,64,8192]{2,1,0:T(8,128)(2,1)}, bf16[8,32,10,1024]{3,2,1,0:T(8,128)(2,1)}, s32[]{:T(128)}, /*index=5*/s32[]{:T(128)}) while((s32[]{:T(128)}, f32[64,864]{1,0:T(8,128)S(1)}, bf16[8,64,8192]{2,1,0:T(8,128)(2,1)}, bf16[8,32,10,1024]{3,2,1,0:T(8,128)(2,1)}, ...), condition=%wide.region_17.18_spmd.clone, body=%wide.region_16.17_spmd.clone.sunk | while | flops 934424576 | bytes 76788304 | solution.py:189
  863.6 12.1 copy.170
  894.0 12.1 copy.170
  924.3 12.1 copy.170
  954.6 12.1 copy.170
  984.9 12.1 copy.170
  1015.1 12.1 copy.170
  1045.4 12.1 copy.170
  1098.5 39.9 %all-reduce.41 = (f32[2,64]{1,0:T(2,128)}, f32[128,4]{0,1:T(4,128)}) all-reduce(f32[2,64]{1,0:T(2,128)S(1)} %pad_maximum_fusion.1, f32[128,4]{0,1:T(4,128)S(1)} %fusion.228), channel_id=1, replica_groups=mesh['dp'=8,'space'=4] {'dp','space'}, use_global_device_ids=true, to_apply=%region_19.20 | all-reduce | flops 640 | bytes 5120 | tf_op jit(solution)/shard_map/psum | solution.py:193
  1140.5 87.6 %all-reduce.46.cloned.1.call-done = (f32[64,864]{1,0:T(8,128)}, f32[128,1728]{0,1:T(8,128)}) async-done(((f32[64,864]{1,0:T(8,128)}, f32[128,1728]{0,1:T(8,128)}), (f32[64,864]{1,0:T(8,128)}, f32[128,1728]{0,1:T(8,128)})) %all-reduce.46.cloned.1.call-update) | async-done | bytes 1105936 | tf_op jit(solution)/shard_map/psum | solution.py:193
  (901 shorter events, 761.3 us)
Async XLA Ops:
  8.0 410.8 %copy-start = (bf16[128,4]{0,1:T(4,128)(2,1)S(1)}, bf16[128,4]{0,1:T(4,128)(2,1)}, u32[]{:S(2)}) copy-start(bf16[128,4]{0,1:T(4,128)(2,1)} %param.22) | copy-start | bytes 3076
  8.0 36.1 %copy-start.16 = (bf16[64,864]{1,0:T(8,128)(2,1)S(1)}, bf16[64,864]{1,0:T(8,128)(2,1)}, u32[]{:S(2)}) copy-start(bf16[64,864]{1,0:T(8,128)(2,1)} %param.17) | copy-start | bytes 331780
  13.6 16.1 %collective-permute-start = (bf16[8,32,1,1024]{3,1,2,0:T(8,128)(2,1)S(1)}, bf16[8,32,1,1024]{3,1,2,0:T(8,128)(2,1)S(1)}, u32[]{:S(2)}, u32[]{:S(2)}) collective-permute-start(bf16[8,32,1,1024]{3,1,2,0:T(8,128)(2,1)S(1)} %copy.67), channel_id=1, source_target_pairs={{0,1},{1,2},{2,3},{4,5},{5,6},{6,7},{8,9},{9,10},{10,11},{12,13},{... | collective-permute-start | bytes 1572872 | tf_op jit(solution)/shard_map/ppermute | solution.py:21
  18.7 15.3 %collective-permute-start.1 = (bf16[8,32,1,1024]{3,1,2,0:T(8,128)(2,1)S(1)}, bf16[8,32,1,1024]{3,1,2,0:T(8,128)(2,1)S(1)}, u32[]{:S(2)}, u32[]{:S(2)}) collective-permute-start(bf16[8,32,1,1024]{3,1,2,0:T(8,128)(2,1)S(1)} %copy.68), channel_id=1, source_target_pairs={{1,0},{2,1},{3,2},{5,4},{6,5},{7,6},{9,8},{10,9},{11,10},{13,12},{... | collective-permute-start | bytes 1572872 | tf_op jit(solution)/shard_map/ppermute | solution.py:23
  255.2 24.6 %copy-start.17 = (f32[64]{0:T(128)}, f32[64]{0:T(128)S(1)}, u32[]{:S(2)}) copy-start(f32[64]{0:T(128)S(1)} %broadcast_multiply_fusion.1) | copy-start | bytes 772
  255.2 24.1 %copy-start.19 = (f32[64]{0:T(128)S(1)}, f32[64]{0:T(128)}, u32[]{:S(2)}) copy-start(f32[64]{0:T(128)} %param.18) | copy-start | bytes 772
  255.2 24.6 %copy-start.23 = (f32[64]{0:T(128)S(1)}, f32[64]{0:T(128)}, u32[]{:S(2)}) copy-start(f32[64]{0:T(128)} %param.19) | copy-start | bytes 772
  279.8 25.5 %copy-start.21 = (f32[64]{0:T(128)}, f32[64]{0:T(128)S(1)}, u32[]{:S(2)}) copy-start(f32[64]{0:T(128)S(1)} %get-tuple-element.447) | copy-start | bytes 772
  305.3 47.0 %copy-start.14 = (bf16[128,1728]{0,1:T(8,128)(2,1)S(1)}, bf16[128,1728]{0,1:T(8,128)(2,1)}, u32[]{:S(2)}) copy-start(bf16[128,1728]{0,1:T(8,128)(2,1)} %param.20) | copy-start | bytes 1327108
  327.6 24.6 %all-to-all-start = ((bf16[8,64,1024]{2,1,0:T(8,128)(2,1)}), bf16[8,64,1024]{2,1,0:T(8,128)(2,1)S(1)}, u32[]{:S(2)}, u32[]{:S(2)}) async-start(bf16[8,64,1024]{2,1,0:T(8,128)(2,1)} %copy.54), calls=%async_computation | async-start | bytes 2097152 | tf_op jit(solution)/shard_map/all_to_all | solution.py:103
  331.2 523.7 %reduce-scatter.3.cloned.1.call-start = ((), (), s32[]{:S(2)}) async-start(), calls=%async_computation.4 | async-start | bytes 18874368 | tf_op jit(solution)/shard_map/reduce_scatter | solution.py:128
  734.9 27.2 %all-to-all-start.1 = ((bf16[4,2,65536]{2,1,0:T(2,128)(2,1)}), bf16[4,2,65536]{2,1,0:T(2,128)(2,1)S(1)}, u32[]{:S(2)}, u32[]{:S(2)}) async-start(bf16[4,2,65536]{2,1,0:T(2,128)(2,1)} %reshape.317), calls=%async_computation.1 | async-start | bytes 2097152 | tf_op jit(solution)/shard_map/all_to_all | solution.py:166
  738.5 400.0 %reduce-scatter.5.cloned.1.call-start = ((), (), s32[]{:S(2)}) async-start(), calls=%async_computation.5 | async-start | bytes 2621440 | tf_op jit(solution)/shard_map/reduce_scatter | solution.py:136
  738.5 39.9 %copy-start.18 = (f32[64]{0:T(128)S(1)}, f32[64]{0:T(128)}, u32[]{:S(2)}) copy-start(f32[64]{0:T(128)} %copy-done.17) | copy-start | bytes 772
  738.5 39.9 %copy-start.20 = (f32[64]{0:T(128)S(1)}, f32[64]{0:T(128)}, u32[]{:S(2)}) copy-start(f32[64]{0:T(128)} %param.18) | copy-start | bytes 772
  738.5 39.9 %copy-start.22 = (f32[64]{0:T(128)S(1)}, f32[64]{0:T(128)}, u32[]{:S(2)}) copy-start(f32[64]{0:T(128)} %copy-done.21) | copy-start | bytes 772
  738.6 39.9 %copy-start.24 = (f32[64]{0:T(128)S(1)}, f32[64]{0:T(128)}, u32[]{:S(2)}) copy-start(f32[64]{0:T(128)} %param.19) | copy-start | bytes 772
  778.5 22.3 %copy-start.11 = (f32[8,64,4,16,16]{1,0,4,3,2:T(8,128)}, f32[8,64,4,16,16]{1,0,4,3,2:T(8,128)S(1)}, u32[]{:S(2)}) copy-start(f32[8,64,4,16,16]{1,0,4,3,2:T(8,128)S(1)} %copy.62) | copy-start | bytes 6291460
  778.5 32.2 %copy-start.25 = (f32[64]{0:T(128)S(1)}, f32[64]{0:T(128)}, u32[]{:S(2)}) copy-start(f32[64]{0:T(128)} %get-tuple-element.446) | copy-start | bytes 772
  854.9 373.2 %all-reduce.46.cloned.1.call-start = ((), (), s32[]{:S(2)}) async-start(), calls=%async_computation.6 | async-start | bytes 2228224 | tf_op jit(solution)/shard_map/psum | solution.py:193
  855.0 243.3 %copy-start.27 = (bf16[2,128]{1,0:T(2,128)(2,1)S(1)}, bf16[2,128]{1,0:T(2,128)(2,1)}, u32[]{:S(2)}) copy-start(bf16[2,128]{1,0:T(2,128)(2,1)} %copy-done.26) | copy-start | bytes 1540
  855.0 243.3 %copy-start.29 = (f32[2,4]{1,0:T(2,128)S(1)}, f32[2,4]{1,0:T(2,128)}, u32[]{:S(2)}) copy-start(f32[2,4]{1,0:T(2,128)} %param.23) | copy-start | bytes 100
  855.0 243.3 %copy-start.31 = (f32[2,4]{1,0:T(2,128)S(1)}, f32[2,4]{1,0:T(2,128)}, u32[]{:S(2)}) copy-start(f32[2,4]{1,0:T(2,128)} %copy-done.30) | copy-start | bytes 100
  1097.6 134.3 %copy-start.1 = (bf16[128,4]{0,1:T(4,128)(2,1)S(1)}, bf16[128,4]{0,1:T(4,128)(2,1)}, u32[]{:S(2)}) copy-start(bf16[128,4]{0,1:T(4,128)(2,1)} %param.22) | copy-start | bytes 3076
  (26 other events, 209.5 us)
Sparse Core Ops, SparseCore 0:
  459.0 115.2 reduce-scatter.2
  855.0 42.4 reduce-scatter.4
Sparse Core Ops, SparseCore 1:
  1098.4 129.7 all-reduce.45
where the time goes:
time: 1250 us; the launch traced here: 1240 us
  local copies, waits for them, and re-layouts  443 us (35%)
  other arithmetic  328 us (26%)
  matrix products  190 us (15%)
  waiting for transfers between devices  145 us (12%)
  blocking collectives  68.7 us (5%)
  loops' own time  34.6 us (3%)
  between operations  16.2 us (1%)
  starting transfers between devices  13.4 us (1%)
    while x122, local copies, waits for them, and re-layouts  269 us
    while x520, other arithmetic  123 us
    psum x1, waiting for transfers between devices, shards(): lax.psum((grad_conv_in, grad_norm_local, grad_conv_out, grad_out_local),...  87.6 us
    dot_general x8, matrix products, first_back(): lax.dot_general(gradient, patches, (((1,), (1,)), ((), ())), preferred_el...  77.7 us
    psum x1, blocking collectives, shards(): lax.psum((grad_conv_in, grad_norm_local, grad_conv_out, grad_out_local),...  39.9 us
    dot_general x8, matrix products, first_conv(): jnp.dot(conv_in, columns(slab_ext, planes, GRID), preferred_element_type=...  32.8 us
    another operation x4, local copies, waits for them, and re-layouts, columns(): stacked = jnp.stack(pieces, 0)  31.5 us
    add x2, other arithmetic, leaky_relu(): return 0.65 * values + 0.35 * values * jnp.tanh(values)  30.5 us
  transfers between devices with their start and end apart: 7, of which 5 were waited for; matrix products, arithmetic and copies ran while one was open for 46% of the time, Pallas kernels for 0%

commit v1 on v0

v1 whole, which is shorter than its diff:
```python
import jax
import jax.numpy as jnp
import numpy as np
from jax import lax
from jax.experimental import pallas as pl
from jax.experimental.pallas import tpu as pltpu
from jax.sharding import PartitionSpec as P

GRID = 32
HALVES = 2
LANES = 128
norm_epsilon = 1e-05
INTERPRET = False

F32 = jnp.float32
BF16 = jnp.bfloat16


def leaky_relu(values):
    return values * (0.65 + 0.35 * jnp.tanh(values))


def slope_of(values):
    bent = jnp.tanh(values)
    return 0.65 + 0.35 * (bent + values * (1.0 - bent * bent))


def dot(a, b):
    return jnp.dot(a, b, preferred_element_type=F32)


def dot_rows(a, b):
    return lax.dot_general(a, b, (((0,), (0,)), ((), ())), preferred_element_type=F32)


def dot_lanes(a, b):
    return lax.dot_general(a, b, (((1,), (1,)), ((), ())), preferred_element_type=F32)


def low_half(shape):
    return lax.broadcasted_iota(jnp.int32, shape, len(shape) - 1) < LANES // 2


def roll_half(values):
    flat = values.reshape(-1, LANES)
    return pltpu.roll(flat, LANES // 2, 1).reshape(values.shape)


def both_halves(values):
    return values + roll_half(values)


def call(kernel, out_shape, **kwargs):
    return pl.pallas_call(kernel, out_shape=out_shape, interpret=INTERPRET, **kwargs)


def whole_spec(shape):
    return pl.BlockSpec(shape, lambda *_: (0,) * len(shape), pipeline_mode=pl.Buffered(1))


def first_weights(conv_in):
    co = conv_in.shape[0]
    c = conv_in.shape[1] // 27
    w = conv_in.reshape(co, 3, 3, 3, c).transpose(3, 1, 2, 4, 0)
    parts = [
        jnp.pad(w, ((0, 0), (px, 1 - px), (py, 1 - py), (0, 0), (0, 0)))
        for px in (0, 1)
        for py in (0, 1)
    ]
    w = jnp.stack(parts, axis=4).reshape(3, 2, 2, 2, 2, c, 4 * co)
    return w.transpose(0, 1, 3, 4, 2, 5, 6).reshape(3 * 16 * c, 4 * co)


def second_weights(conv_out):
    co = conv_out.shape[0]
    c = conv_out.shape[1] // 27
    w = conv_out.reshape(co, 3, 3, 3, c).transpose(2, 3, 1, 4, 0)
    parts = [jnp.pad(w, ((0, 0), (0, 0), (px, 1 - px), (0, 0), (0, 0))) for px in (0, 1)]
    return jnp.stack(parts, axis=4).reshape(9 * 4 * c, 2 * co)


def adjoint_weights(conv_out):
    co = conv_out.shape[0]
    c = conv_out.shape[1] // 27
    w = conv_out.reshape(co, 3, 3, 3, c)[:, ::-1, ::-1, ::-1].transpose(3, 1, 2, 0, 4)
    parts = [
        jnp.pad(w, ((0, 0), (px, 1 - px), (py, 1 - py), (0, 0), (0, 0)))
        for px in (0, 1)
        for py in (0, 1)
    ]
    return jnp.stack(parts, axis=4).reshape(48 * co, 4 * c)


def half_pads(before, after):
    zero = jnp.zeros_like(before[:, 0:8])
    return (
        jnp.concatenate([zero, before[:, 0:8]], axis=1),
        jnp.concatenate([after[:, 8:16], zero], axis=1),
    )


def first_kernel(planes, samples, refs):
    (x_ref, halo_ref, pa_ref, pb_ref, w_ref, f_ref, xb_ref, st_ref, z_ref, w_acc) = refs
    i = pl.program_id(0)
    pairs = planes // 2 + 1
    half_y = GRID // HALVES
    chunks = z_ref.shape[0]
    inner = HALVES * samples
    groups = GRID * GRID // LANES
    per_group = LANES // GRID

    @pl.when(i == 0)
    def _():
        def gather(t, carry):
            s = t % samples
            q = t // samples
            for h in range(HALVES):
                g = q + h * (groups // HALVES)
                lanes = pl.ds(pl.multiple_of(g * LANES, LANES), LANES)
                t_val = dot_rows(x_ref[s, :, lanes], pa_ref[...]) + dot_rows(
                    halo_ref[s, :, lanes], pb_ref[...]
                )
                start = (per_group * q + 1) * GRID * inner + h * samples + s
                for k in range(chunks):
                    z_ref[k, pl.ds(start, LANES, stride=inner), :] = t_val[
                        :, k * LANES : (k + 1) * LANES
                    ]
            return carry

        lax.fori_loop(0, samples * groups // HALVES, gather, 0)
        row = GRID * inner

        def plane_of(k, y):
            start = pl.multiple_of(y * row, row)
            return z_ref[k, pl.ds(start, row), :]

        for k in range(chunks):
            last = plane_of(k, half_y).reshape(GRID, inner, LANES)
            head = plane_of(k, 1).reshape(GRID, inner, LANES)
            lo, hi = half_pads(last, head)
            z_ref[k, 0:row, :] = lo.reshape(row, LANES)
            z_ref[k, (half_y + 1) * row : (half_y + 2) * row, :] = hi.reshape(row, LANES)

        def assemble(m, carry):
            mask = low_half((row, LANES))
            for k in range(pairs):
                a = plane_of(k // 2, 2 * m)
                b = plane_of(k // 2, 2 * m + 1)
                if k % 2 == 0:
                    b = roll_half(b)
                else:
                    a = roll_half(a)
                both = jnp.where(mask, a, b).astype(BF16)
                xb_ref[k, m, 1 : GRID + 1] = both.reshape(GRID, inner, LANES)
                zero = jnp.zeros((inner, LANES), BF16)
                xb_ref[k, m, 0] = zero
                xb_ref[k, m, GRID + 1] = zero
            return carry

        lax.fori_loop(0, half_y // 2 + 1, assemble, 0)
        w_acc[...] = jnp.zeros_like(w_acc)

    rows = GRID * inner
    blocks = half_y // 2
    per_block = rows // 8

    def conv(yb, carry):
        pieces = []
        for dz in range(3):
            for kk in range(2):
                for mm in range(2):
                    pieces.append(
                        xb_ref[i + kk, yb + mm, dz : dz + GRID].reshape(rows, LANES)
                    )
        out = dot(jnp.concatenate(pieces, axis=1), w_ref[...])
        f_ref[0, yb] = out.reshape(GRID, inner, 2 * LANES)
        stacked = out.reshape(per_block, 8, 2 * LANES)
        mean = jnp.sum(stacked, axis=0) * (1.0 / per_block)
        dev = stacked - mean[None]
        square = jnp.sum(dev * dev, axis=0)
        done = (i * blocks + yb).astype(F32)
        delta = mean - w_acc[0]
        w_acc[0] = w_acc[0] + delta / (done + 1.0)
        w_acc[1] = w_acc[1] + square + delta * delta * (per_block * done / (done + 1.0))
        return carry

    lax.fori_loop(0, blocks, conv, 0)

    @pl.when(i == pl.num_programs(0) - 1)
    def _():
        count = float(per_block * blocks * (planes // 2))
        mean = w_acc[0]
        m = jnp.mean(mean, axis=0, keepdims=True)
        m = both_halves((m[:, :LANES] + m[:, LANES:]) * 0.5) * 0.5
        wide = jnp.concatenate([m, m], axis=1)
        dev = mean - wide
        q = jnp.sum(w_acc[1] + count * dev * dev, axis=0, keepdims=True)
        q = both_halves(q[:, :LANES] + q[:, LANES:])
        st_ref[...] = jnp.concatenate([m, q], axis=0)


def first_conv(x, halo, w1, planes):
    samples = x.shape[0]
    c = halo.shape[1] // 2
    pairs = planes // 2 + 1
    used = pairs * 2 * c
    chunks = -(-used // LANES)
    inner = HALVES * samples
    half_y = GRID // HALVES
    pa = np.zeros((c * planes, chunks * LANES), np.float32)
    pb = np.zeros((2 * c, chunks * LANES), np.float32)
    for ch in range(c):
        for p in range(planes):
            pa[ch * planes + p, (p + 1) * c + ch] = 1.0
        pb[ch, ch] = 1.0
        pb[c + ch, (planes + 1) * c + ch] = 1.0
    pa = jnp.asarray(pa, BF16)
    pb = jnp.asarray(pb, BF16)
    nxb = planes // 2
    nyb = half_y // 2
    f_shape = (nxb, nyb, GRID, inner, 2 * LANES)
    xb_shape = (pairs, nyb + 1, GRID + 2, inner, LANES)
    return call(
        lambda *refs: first_kernel(planes, samples, refs),
        (
            jax.ShapeDtypeStruct(f_shape, F32),
            jax.ShapeDtypeStruct(xb_shape, BF16),
            jax.ShapeDtypeStruct((2, LANES), F32),
        ),
        grid=(nxb,),
        in_specs=[whole_spec(a.shape) for a in (x, halo, pa, pb, w1)],
        out_specs=(
            pl.BlockSpec((1,) + f_shape[1:], lambda i: (i, 0, 0, 0, 0)),
            whole_spec(xb_shape),
            whole_spec((2, LANES)),
        ),
        scratch_shapes=[
            pltpu.VMEM((chunks, (half_y + 2) * GRID * inner, LANES), F32),
            pltpu.VMEM((2, 8, 2 * LANES), F32),
        ],
        name="first_conv",
    )(x, halo, pa, pb, w1)


def group_stats(st, local_count, total_count):
    means = st[:, 0]
    mean = jnp.mean(means, axis=0, keepdims=True)
    dev = means - mean
    square = jnp.sum(st[:, 1] + local_count * dev * dev, axis=0, keepdims=True)
    inverse = lax.rsqrt(square / total_count + norm_epsilon)
    return mean, inverse


def wide(row):
    return jnp.concatenate([row, row], axis=1)


def pool_kernel(local_count, total_count, f_ref, st_ref, gs_ref, pd_ref, lo_ref, hi_ref):
    i = pl.program_id(0)
    mean, inverse = group_stats(st_ref[...], local_count, total_count)
    mean = wide(mean)
    inverse = wide(inverse)
    gain = wide(gs_ref[0:1])
    shift = wide(gs_ref[1:2])
    nyb = f_ref.shape[1]
    nz = f_ref.shape[2]
    inner = f_ref.shape[3]

    def step(yb, carry):
        f = f_ref[0, yb].reshape(nz * inner, 2 * LANES)
        act = leaky_relu(gain * ((f - mean) * inverse) + shift)
        act = act[:, :LANES] + act[:, LANES:]
        act = act.reshape(nz // 2, 2, inner, LANES)
        act = act[:, 0] + act[:, 1]
        pooled = both_halves(act) * 0.125
        pd_ref[0, yb] = pooled.astype(BF16)
        return carry

    lax.fori_loop(0, nyb, step, 0)
    half = nyb // 2

    def pack(ref):
        mask = low_half((nz // 2, inner, LANES))
        for y in range(half):
            ref[y] = jnp.where(mask, pd_ref[0, y].astype(F32), pd_ref[0, y + half].astype(F32)).astype(BF16)

    @pl.when(i == 0)
    def _():
        pack(lo_ref)

    @pl.when(i == pl.num_programs(0) - 1)
    def _():
        pack(hi_ref)


def normalise_pool(f, st, gs, local_count, total_count):
    nxb, nyb, nz, inner, _ = f.shape
    pd_shape = (nxb, nyb, nz // 2, inner, LANES)
    edge = (nyb // 2, nz // 2, inner, LANES)
    return call(
        lambda *refs: pool_kernel(local_count, total_count, *refs),
        (
            jax.ShapeDtypeStruct(pd_shape, BF16),
            jax.ShapeDtypeStruct(edge, BF16),
            jax.ShapeDtypeStruct(edge, BF16),
        ),
        grid=(nxb,),
        in_specs=[
            pl.BlockSpec((1,) + f.shape[1:], lambda i: (i, 0, 0, 0, 0)),
            whole_spec(st.shape),
            whole_spec(gs.shape),
        ],
        out_specs=(
            pl.BlockSpec((1,) + pd_shape[1:], lambda i: (i, 0, 0, 0, 0)),
            whole_spec(edge),
            whole_spec(edge),
        ),
        name="normalise_pool",
    )(f, st, gs)


def second_kernel(samples, j_ref, pd_ref, lo_ref, hi_ref, w_ref, d_ref, pp_ref, sec_ref, fc_ref, hid_ref, ft, fcs):
    planes, ny, nz, inner, _ = pd_ref.shape
    pairs = planes // 2 + 1
    half = ny // 2
    cells = fc_ref.shape[2]
    channels = fc_ref.shape[0]

    def unpack(ref, y):
        v = ref[y % half].astype(F32)
        return jnp.where(low_half(v.shape) == (y < half), v, roll_half(v))

    def assemble(y, carry):
        mask = low_half((nz, inner, LANES))
        for k in range(pairs):
            a = unpack(lo_ref, y) if k == 0 else pd_ref[2 * k - 1, y].astype(F32)
            b = unpack(hi_ref, y) if k == pairs - 1 else pd_ref[2 * k, y].astype(F32)
            pp_ref[k, y + 1, 1 : nz + 1] = jnp.where(mask, a, b).astype(BF16)
        return carry

    lax.fori_loop(0, ny, assemble, 0)
    zero = jnp.zeros((inner, LANES), BF16)
    for k in range(pairs):
        last = pp_ref[k, ny, 1 : nz + 1].astype(F32)
        head = pp_ref[k, 1, 1 : nz + 1].astype(F32)
        before, after = half_pads(last, head)
        pp_ref[k, 0, 1 : nz + 1] = before.astype(BF16)
        pp_ref[k, ny + 1, 1 : nz + 1] = after.astype(BF16)

        def zero_ends(y, carry, k=k):
            pp_ref[k, y, 0] = zero
            pp_ref[k, y, nz + 1] = zero
            return carry

        lax.fori_loop(0, ny + 2, zero_ends, 0)

    rows = 2 * nz * inner

    def conv(t, carry):
        xb = t // half
        y3 = t % half
        y = 2 * y3
        pieces = []
        for dy in range(3):
            for dz in range(3):
                for kk in range(2):
                    pieces.append(
                        pp_ref[xb + kk, pl.ds(y + dy, 2), dz : dz + nz].reshape(rows, LANES)
                    )
        out = dot(jnp.concatenate(pieces, axis=1), w_ref[...])
        sec_ref[xb, pl.ds(y, 2)] = out.reshape(2, nz, inner, 2 * LANES)
        act = leaky_relu(out)
        act = act[:, :LANES] + act[:, LANES:]
        act = act.reshape(2, nz // 2, 2, inner, LANES)
        act = (act[0, :, 0] + act[0, :, 1]) + (act[1, :, 0] + act[1, :, 1])
        act = (act * 0.125).astype(BF16).astype(F32)
        count = nz // 2 * inner
        start = pl.multiple_of((xb * half + y3) * count, count)
        ft[pl.ds(start, count), :] = act.reshape(count, LANES)
        return carry

    nxb = planes // 2
    lax.fori_loop(0, nxb * half, conv, 0)

    per_half = half * (nz // 2)

    def turn(s, carry):
        parts = []
        for xb in range(nxb):
            for h in range(HALVES):
                start = xb * per_half * inner + h * samples + s
                parts.append(ft[pl.ds(start, per_half, stride=inner), :])
        turned = jnp.concatenate(parts, axis=0).T
        fcs[pl.ds(s, channels, stride=samples), 0:cells] = turned
        return carry

    lax.fori_loop(0, samples, turn, 0)
    fc_ref[...] = fcs[:, 0:cells].reshape(channels, samples, cells).astype(BF16)

    def dense(t, acc):
        for u in range(8):
            ch = t * 8 + u
            acc[u % 4] = acc[u % 4] + dot(fc_ref[ch], d_ref[ch, 0])
        return acc

    zeros = [jnp.zeros((samples, LANES), F32) for _ in range(4)]
    acc = lax.fori_loop(0, channels // 8, dense, zeros)
    hid_ref[...] = (acc[0] + acc[1]) + (acc[2] + acc[3])


def second_conv(j, pd, lo, hi, w2, dense4, samples):
    planes, ny, nz, inner, _ = pd.shape
    channels, spaces, cells, units = dense4.shape
    pairs = planes // 2 + 1
    nxb = planes // 2
    pp_shape = (pairs, ny + 2, nz + 2, inner, LANES)
    sec_shape = (nxb, ny, nz, inner, 2 * LANES)
    fc_shape = (channels, samples, cells)

    def const(shape):
        return pl.BlockSpec(shape, lambda i, j_ref: (0,) * len(shape), pipeline_mode=pl.Buffered(1))

    return call(
        lambda *refs: second_kernel(samples, *refs),
        (
            jax.ShapeDtypeStruct(pp_shape, BF16),
            jax.ShapeDtypeStruct(sec_shape, F32),
            jax.ShapeDtypeStruct(fc_shape, BF16),
            jax.ShapeDtypeStruct((samples, units), F32),
        ),
        grid_spec=pltpu.PrefetchScalarGridSpec(
            num_scalar_prefetch=1,
            grid=(1,),
            in_specs=[const(pd.shape), const(lo.shape), const(hi.shape), const(w2.shape),
                      pl.BlockSpec((channels, 1, cells, units), lambda i, j_ref: (0, j_ref[0], 0, 0), pipeline_mode=pl.Buffered(1))],
            out_specs=(const(pp_shape), const(sec_shape), const(fc_shape), const((samples, units))),
            scratch_shapes=[
                pltpu.VMEM((nxb * (ny // 2) * (nz // 2) * inner, LANES), F32),
                pltpu.VMEM((channels * samples, LANES), F32),
            ],
        ),
        name="second_conv",
    )(j, pd, lo, hi, w2, dense4)


def dense_kernel(samples, own, targets_n, j_ref, hp_ref, tg_ref, do_ref, d_ref, sec_ref,
                 pred_ref, bh_ref, gdo_ref, bs_ref, bfc, bf):
    nxb, ny, nz, inner, _ = sec_ref.shape
    channels = d_ref.shape[0]
    cells = d_ref.shape[2]
    hp = hp_ref[...]
    hidden = leaky_relu(hp).astype(BF16).astype(F32)
    row = lax.broadcasted_iota(jnp.int32, (samples, 1), 0)
    mine = (row // own) == j_ref[0]
    lane = lax.broadcasted_iota(jnp.int32, (samples, LANES), 1)
    preds = jnp.zeros((samples, LANES), F32)
    back = jnp.zeros_like(hp)
    for t in range(targets_n):
        weight = do_ref[t : t + 1, :]
        pred = jnp.sum(hidden * weight, axis=1, keepdims=True)
        misfit = pred - tg_ref[:, t : t + 1]
        preds = jnp.where(lane == t, pred, preds)
        gdo_ref[t : t + 1, :] = jnp.sum(jnp.where(mine, hidden * misfit, 0.0), axis=0, keepdims=True)
        back = back + misfit * weight
    pred_ref[...] = preds
    bh = (back * slope_of(hp)).astype(BF16)
    bh_ref[...] = bh

    def features(t, carry):
        for u in range(8):
            ch = t * 8 + u
            out = dot_lanes(bh, d_ref[ch, 0])
            bfc[pl.ds(pl.multiple_of(ch * samples, samples), samples), 0:cells] = out
        return carry

    lax.fori_loop(0, channels // 8, features, 0)
    half = ny // 2
    per_half = half * (nz // 2)

    def turn(s, carry):
        turned = bfc[pl.ds(s, channels, stride=samples), 0:cells].T
        for xb in range(nxb):
            for h in range(HALVES):
                start = xb * per_half * inner + h * samples + s
                at = (xb * HALVES + h) * per_half
                bf[pl.ds(start, per_half, stride=inner), :] = turned[at : at + per_half]
        return carry

    lax.fori_loop(0, samples, turn, 0)
    count = nz // 2 * inner

    def spread(t, carry):
        xb = t // half
        y3 = t % half
        start = pl.multiple_of(t * count, count)
        g = bf[pl.ds(start, count), :].reshape(nz // 2, 1, inner, LANES) * 0.125
        g = jnp.broadcast_to(g, (nz // 2, 2, inner, LANES)).reshape(nz, inner, LANES)
        for dy in range(2):
            y = 2 * y3 + dy
            slope = slope_of(sec_ref[xb, y])
            for px in range(2):
                bs_ref[2 * xb + px, y] = (g * slope[:, :, px * LANES : (px + 1) * LANES]).astype(BF16)
        return carry

    lax.fori_loop(0, nxb * half, spread, 0)


def dense_layers(j, hp, targets, dense_out_t, dense4, sec, own):
    nxb, ny, nz, inner, _ = sec.shape
    channels, spaces, cells, units = dense4.shape
    samples, targets_n = targets.shape
    bs_shape = (2 * nxb, ny, nz, inner, LANES)

    def const(shape):
        return pl.BlockSpec(shape, lambda i, j_ref: (0,) * len(shape), pipeline_mode=pl.Buffered(1))

    return call(
        lambda *refs: dense_kernel(samples, own, targets_n, *refs),
        (
            jax.ShapeDtypeStruct((samples, LANES), F32),
            jax.ShapeDtypeStruct((samples, units), BF16),
            jax.ShapeDtypeStruct((targets_n, units), F32),
            jax.ShapeDtypeStruct(bs_shape, BF16),
        ),
        grid_spec=pltpu.PrefetchScalarGridSpec(
            num_scalar_prefetch=1,
            grid=(1,),
            in_specs=[const(hp.shape), const(targets.shape), const(dense_out_t.shape),
                      pl.BlockSpec((channels, 1, cells, units), lambda i, j_ref: (0, j_ref[0], 0, 0), pipeline_mode=pl.Buffered(1)),
                      const(sec.shape)],
            out_specs=(const((samples, LANES)), const((samples, units)), const((targets_n, units)), const(bs_shape)),
            scratch_shapes=[
                pltpu.VMEM((channels * samples, LANES), F32),
                pltpu.VMEM((nxb * (ny // 2) * (nz // 2) * inner, LANES), F32),
            ],
        ),
        name="dense_layers",
    )(j, hp, targets, dense_out_t, dense4, sec)


def dense_grad_kernel(f_ref, b_ref, o_ref):
    groups, spaces, chans, samples, cells = f_ref.shape
    b = b_ref[...].astype(F32).reshape(groups * samples, b_ref.shape[2]).astype(BF16)
    for ch in range(chans):
        for j in range(spaces):
            f = f_ref[:, j, ch].astype(F32).reshape(groups * samples, cells).astype(BF16)
            o_ref[ch, j] = dot_rows(f, b)


def dense_grad(feats, bh):
    groups, spaces, chans, samples, cells = feats.shape
    shape = (chans, spaces, cells, bh.shape[2])
    return call(dense_grad_kernel, jax.ShapeDtypeStruct(shape, F32), name="dense_grad")(feats, bh)


def second_grad_kernel(bs_ref, pp_ref, g_ref, acc):
    planes, ny, nz, inner, _ = bs_ref.shape
    nxb = planes // 2
    half = ny // 2
    rows = 2 * nz * inner
    acc[...] = jnp.zeros_like(acc)

    def step(t, carry):
        xb = t // half
        y = 2 * (t % half)
        left = jnp.concatenate(
            [bs_ref[2 * xb + px, pl.ds(y, 2)].reshape(rows, LANES) for px in range(2)], axis=1
        ).T
        for dy in range(3):
            for dz in range(3):
                right = jnp.concatenate(
                    [
                        pp_ref[xb + kk, pl.ds(y + dy, 2), dz : dz + nz].reshape(rows, LANES)
                        for kk in range(2)
                    ],
                    axis=1,
                )
                acc[dy * 3 + dz] = acc[dy * 3 + dz] + dot(left, right)
        return carry

    lax.fori_loop(0, nxb * half, step, 0)
    mid = LANES // 2
    for o in range(9):
        both = acc[o, :LANES, 0 : 3 * mid] + acc[o, LANES:, mid : 4 * mid]
        for a in range(3):
            at = (a * 9 + o) * mid
            g_ref[:, at : at + mid] = both[:, a * mid : (a + 1) * mid]


def second_grad(bs, pp):
    return call(
        second_grad_kernel,
        jax.ShapeDtypeStruct((LANES, 27 * LANES // 2), F32),
        scratch_shapes=[pltpu.VMEM((9, 2 * LANES, 2 * LANES), F32)],
        name="second_grad",
    )(bs, pp)


def second_back_kernel(bs_ref, lo_ref, hi_ref, w_ref, bp_ref, pad):
    planes, ny, nz, inner, _ = bs_ref.shape
    nxb = planes // 2
    zero = jnp.zeros((inner, LANES), BF16)
    for p in range(planes + 2):

        def fill(y, carry, p=p):
            if p == 0:
                v = lo_ref[y]
            elif p == planes + 1:
                v = hi_ref[y]
            else:
                v = bs_ref[p - 1, y]
            pad[p, y + 1, 1 : nz + 1] = v
            return carry

        lax.fori_loop(0, ny, fill, 0)
        before, after = half_pads(
            pad[p, ny, 1 : nz + 1].astype(F32), pad[p, 1, 1 : nz + 1].astype(F32)
        )
        pad[p, 0, 1 : nz + 1] = before.astype(BF16)
        pad[p, ny + 1, 1 : nz + 1] = after.astype(BF16)

        def zero_ends(y, carry, p=p):
            pad[p, y, 0] = zero
            pad[p, y, nz + 1] = zero
            return carry

        lax.fori_loop(0, ny + 2, zero_ends, 0)

    quarter = ny // 4
    rows = nz * inner
    depth = 16 * LANES

    def step(t, carry):
        xb = t // quarter
        y = 4 * (t % quarter)
        out = jnp.zeros((2 * rows, 2 * LANES), F32)
        for dz in range(3):
            pieces = []
            for jx in range(4):
                for jy in range(4):
                    pieces.append(
                        jnp.concatenate(
                            [
                                pad[2 * xb + jx, y + 2 * u + jy, dz : dz + nz].reshape(rows, LANES)
                                for u in range(2)
                            ],
                            axis=0,
                        )
                    )
            out = out + dot(
                jnp.concatenate(pieces, axis=1), w_ref[dz * depth : (dz + 1) * depth, :]
            )
        out = out.astype(BF16).astype(F32)
        mask = low_half((2 * rows, LANES))
        for px in range(2):
            v = out[:, px * LANES : (px + 1) * LANES]
            r = roll_half(v)
            for py in range(2):
                d = jnp.where(mask, v, r) if py == 0 else jnp.where(mask, r, v)
                d = d.astype(BF16).reshape(2, nz, inner, LANES)
                for u in range(2):
                    bp_ref[2 * xb + px, y + 2 * u + py] = d[u]
        return carry

    lax.fori_loop(0, nxb * quarter, step, 0)


def second_back(bs, lo, hi, w3):
    planes, ny, nz, inner, _ = bs.shape
    return call(
        second_back_kernel,
        jax.ShapeDtypeStruct(bs.shape, BF16),
        scratch_shapes=[pltpu.VMEM((planes + 2, ny + 2, nz + 2, inner, LANES), BF16)],
        name="second_back",
    )(bs, lo, hi, w3)


def active_of(f, bp, mean, inverse, gain, shift):
    nz, inner, _ = f.shape
    w = (f.reshape(nz * inner, 2 * LANES) - mean) * inverse
    slope = slope_of(gain * w + shift)
    g = bp.astype(F32).reshape(nz // 2, 1, inner, LANES) * 0.125
    g = jnp.broadcast_to(g, (nz // 2, 2, inner, LANES)).reshape(nz * inner, LANES)
    return w, slope * jnp.concatenate([g, g], axis=1)


def sums_kernel(local_count, total_count, f_ref, bp_ref, st_ref, gs_ref, o_ref, acc):
    i = pl.program_id(0)
    mean, inverse = group_stats(st_ref[...], local_count, total_count)
    mean, inverse = wide(mean), wide(inverse)
    gain, shift = wide(gs_ref[0:1]), wide(gs_ref[1:2])

    @pl.when(i == 0)
    def _():
        acc[...] = jnp.zeros_like(acc)

    def step(yb, carry):
        w, active = active_of(f_ref[0, yb], bp_ref[0, yb], mean, inverse, gain, shift)
        acc[0] = acc[0] + jnp.sum((active * w).reshape(-1, 8, 2 * LANES), axis=0)
        acc[1] = acc[1] + jnp.sum(active.reshape(-1, 8, 2 * LANES), axis=0)
        return carry

    lax.fori_loop(0, f_ref.shape[1], step, 0)

    @pl.when(i == pl.num_programs(0) - 1)
    def _():
        rows = [jnp.sum(acc[k], axis=0, keepdims=True) for k in range(2)]
        rows = [both_halves(r[:, :LANES] + r[:, LANES:]) for r in rows]
        o_ref[...] = jnp.concatenate(rows, axis=0)


def norm_sums(f, bp, st, gs, local_count, total_count):
    return call(
        lambda *refs: sums_kernel(local_count, total_count, *refs),
        jax.ShapeDtypeStruct((2, LANES), F32),
        grid=(f.shape[0],),
        in_specs=[
            pl.BlockSpec((1,) + f.shape[1:], lambda i: (i, 0, 0, 0, 0)),
            pl.BlockSpec((1,) + bp.shape[1:], lambda i: (i, 0, 0, 0, 0)),
            whole_spec(st.shape),
            whole_spec(gs.shape),
        ],
        out_specs=whole_spec((2, LANES)),
        scratch_shapes=[pltpu.VMEM((2, 8, 2 * LANES), F32)],
        name="norm_sums",
    )(f, bp, st, gs)


def first_grad_kernel(local_count, total_count, c, f_ref, bp_ref, st_ref, gs_ref, sum_ref, xa_ref, xc_ref, g_ref, acc):
    i = pl.program_id(0)
    mean, inverse = group_stats(st_ref[...], local_count, total_count)
    mean, inverse = wide(mean), wide(inverse)
    gain, shift = wide(gs_ref[0:1]), wide(gs_ref[1:2])
    cross = wide(sum_ref[0:1]) * (1.0 / total_count)
    plain = wide(sum_ref[1:2]) * (1.0 / total_count)
    scale = gain * inverse
    nz = f_ref.shape[2]
    inner = f_ref.shape[3]
    rows = nz * inner

    @pl.when(i == 0)
    def _():
        acc[...] = jnp.zeros_like(acc)

    def step(yb, carry):
        w, active = active_of(f_ref[0, yb], bp_ref[0, yb], mean, inverse, gain, shift)
        left = (scale * (active - plain - w * cross)).astype(BF16).T
        for dz in range(3):
            for kk, x_ref in enumerate((xa_ref, xc_ref)):
                right = jnp.concatenate(
                    [x_ref[0, yb + mm, dz : dz + nz].reshape(rows, LANES) for mm in range(2)],
                    axis=1,
                )
                acc[dz * 2 + kk] = acc[dz * 2 + kk] + dot(left, right)
        return carry

    lax.fori_loop(0, f_ref.shape[1], step, 0)

    @pl.when(i == pl.num_programs(0) - 1)
    def _():
        co = LANES // 2
        for a in range(3):
            for b in range(3):
                for d in range(3):
                    total = None
                    for px in range(2):
                        for py in range(2):
                            xw, yw = a + px, b + py
                            at = (yw // 2) * LANES + (yw % 2) * 2 * c + (xw % 2) * c
                            top = (px * 2 + py) * co
                            part = acc[d * 2 + xw // 2, top : top + co, at : at + c]
                            total = part if total is None else total + part
                    at = ((a * 3 + b) * 3 + d) * c
                    g_ref[:, at : at + c] = total


def first_grad(f, bp, st, gs, sums, xb, c, local_count, total_count):
    x_block = (1,) + xb.shape[1:]
    out = (LANES // 2, 27 * c)
    return call(
        lambda *refs: first_grad_kernel(local_count, total_count, c, *refs),
        jax.ShapeDtypeStruct(out, F32),
        grid=(f.shape[0],),
        in_specs=[
            pl.BlockSpec((1,) + f.shape[1:], lambda i: (i, 0, 0, 0, 0)),
            pl.BlockSpec((1,) + bp.shape[1:], lambda i: (i, 0, 0, 0, 0)),
            whole_spec(st.shape),
            whole_spec(gs.shape),
            whole_spec(sums.shape),
            pl.BlockSpec(x_block, lambda i: (i, 0, 0, 0, 0)),
            pl.BlockSpec(x_block, lambda i: (i + 1, 0, 0, 0, 0)),
        ],
        out_specs=whole_spec(out),
        scratch_shapes=[pltpu.VMEM((6, 2 * LANES, 2 * LANES), F32)],
        name="first_grad",
    )(f, bp, st, gs, sums, xb, xb)


def swap_edges(first, last, axis):
    count = lax.axis_size(axis)
    before = lax.ppermute(last, axis, [(i, i + 1) for i in range(count - 1)])
    after = lax.ppermute(first, axis, [(i + 1, i) for i in range(count - 1)])
    return before, after


def shards(inputs, conv_in, norm_gain, norm_shift, conv_out, dense_in, dense_out, targets):
    samples, c, planes, cells = inputs.shape
    spaces = lax.axis_size("space")
    groups = lax.axis_size("dp")
    units = dense_in.shape[1]
    channels = conv_out.shape[0]
    own = targets.shape[0]
    local_count = float(samples * planes * cells)
    total_count = local_count * spaces

    before, after = swap_edges(inputs[:, :, :1], inputs[:, :, planes - 1 :], "space")
    halo = jnp.concatenate([before, after], axis=1).reshape(samples, 2 * c, cells)
    w1 = first_weights(conv_in)
    w2 = second_weights(conv_out)
    w3 = adjoint_weights(conv_out)
    gs = jnp.stack([norm_gain, norm_shift])
    gs = jnp.concatenate([gs, gs], axis=1)
    j = lax.axis_index("space").astype(jnp.int32).reshape(1)
    dense4 = dense_in.reshape(channels, spaces, dense_in.shape[0] // (channels * spaces), units)
    group_targets = lax.all_gather(targets, "space", axis=0, tiled=True)

    f, xb, st = first_conv(inputs.reshape(samples, c * planes, cells), halo, w1, planes)
    stats = lax.all_gather(st, "space")
    pd, edge_lo, edge_hi = normalise_pool(f, stats, gs, local_count, total_count)
    lo, hi = swap_edges(edge_lo, edge_hi, "space")
    pp, sec, fc, partial = second_conv(j, pd, lo, hi, w2, dense4, samples)
    hp = lax.psum(partial, "space")
    preds, bh, gdo, bs = dense_layers(
        j, hp, group_targets, dense_out.astype(F32).T, dense4, sec, own
    )
    everyone = groups * spaces
    sent = fc.reshape((everyone, channels // everyone) + fc.shape[1:])
    feats = lax.all_to_all(sent, ("dp", "space"), split_axis=0, concat_axis=0, tiled=True)
    feats = feats.reshape((groups, spaces) + sent.shape[1:])
    all_bh = lax.all_gather(bh, "dp")
    bs_lo, bs_hi = swap_edges(bs[0], bs[-1], "space")
    grad_conv_out = lax.psum(second_grad(bs, pp), ("dp", "space"))
    bp = second_back(bs, bs_lo, bs_hi, w3)
    sums = norm_sums(f, bp, stats, gs, local_count, total_count)
    group_sums = lax.psum(sums, "space")
    grad_dense_in = dense_grad(feats, all_bh).reshape(-1, units)
    grad_conv_in = first_grad(f, bp, stats, gs, group_sums, xb, c, local_count, total_count)
    grad_conv_in, sums, gdo = lax.psum((grad_conv_in, sums, gdo), ("dp", "space"))
    first_row = lax.axis_index("space") * own
    predictions = lax.dynamic_slice_in_dim(preds, first_row, own, axis=0)[:, : targets.shape[1]]
    return (
        grad_conv_in,
        sums[:, : norm_gain.shape[0]],
        grad_conv_out,
        grad_dense_in,
        gdo.T,
        predictions,
    )


def solution(mesh):
    placed = (P("dp", None, "space", None), P(), P(), P(), P(), P(), P(), P(("dp", "space"), None))
    return jax.shard_map(
        shards,
        mesh=mesh,
        in_specs=placed,
        out_specs=(P(), P(), P(), P(("dp", "space"), None), P(), P(("dp", "space"), None)),
        check_vma=False,
    )
```

time: 1250 us -> 409 us (0.33)
  local copies, waits for them, and re-layouts: 443 us -> 39.7 us
  other arithmetic: 328 us -> 4.42 us
  matrix products: 190 us -> 0 us
  Pallas kernels: 0 us -> 156 us
  waiting for transfers between devices: 145 us -> 79.8 us
  loops' own time: 34.6 us -> 0 us
  blocking collectives: 68.7 us -> 93.6 us
    while x124 -> x0, local copies, waits for them, and re-layouts: 298 us -> none
    dot_general x28 -> x0, matrix products: 190 us -> none  [the longest x8 77.7 us: first_back(): lax.dot_general(gradient, patches, (((1,), (1,)), ((), ())), preferred_el...]
    pallas_call x0 -> x9, Pallas kernels: none -> 156 us  [the longest x1 44.5 us: first_conv(): call(lambda *refs: first_kernel(planes, samples, refs), (jax.ShapeDtypeSt...]
    while x520 -> x0, other arithmetic: 123 us -> none
    reduce_sum x5 -> x0, other arithmetic: 64.4 us -> none  [the longest x1 22.3 us: shards(): sum_grad = jnp.sum(back_active, axis=(0, 2))]
    all_to_all x2 -> x1, waiting for transfers between devices: 44.6 us -> 0.01 us  [shards(): lax.all_to_all(sent, ('dp', 'space'), split_axis=0, concat_axis=0, tiled=...]
    convert_element_type x69 -> x0, other arithmetic: 36.1 us -> none  [the longest x1 25.9 us: shards(): back_first = back_first.astype(jnp.bfloat16)]
    all_gather x0 -> x3, blocking collectives: none -> 34.7 us  [the longest x1 13.7 us: shards(): stats = lax.all_gather(st, 'space')]
  transfers between devices with their start and end apart: 7 -> 8, of which waited for: 5 -> 3; matrix products, arithmetic and copies ran while one was open for 46% -> 7% of each run, Pallas kernels for 0% -> 3%
where the time goes in v1:
time: 409 us; the launch traced here: 408 us
  Pallas kernels  156 us (38%)
  blocking collectives  93.6 us (23%)
  waiting for transfers between devices  79.8 us (20%)
  local copies, waits for them, and re-layouts  39.7 us (10%)
  starting transfers between devices  20.4 us (5%)
  between operations  14.2 us (3%)
  other arithmetic  4.42 us (1%)
    psum x1, waiting for transfers between devices, shards(): lax.psum((grad_conv_in, sums, gdo), ('dp', 'space'))  74.1 us
    pallas_call x1, Pallas kernels, first_conv(): call(lambda *refs: first_kernel(planes, samples, refs), (jax.ShapeDtypeSt...  44.5 us
    psum x1, blocking collectives, shards(): lax.psum((grad_conv_in, sums, gdo), ('dp', 'space'))  39.5 us
    pallas_call x1, Pallas kernels, first_grad(): call(lambda *refs: first_grad_kernel(local_count, total_count, c, *refs),...  33.2 us
    pallas_call x1, Pallas kernels, second_conv(): call(lambda *refs: second_kernel(samples, *refs), (jax.ShapeDtypeStruct(p...  17.2 us
    reshape x2, local copies, waits for them, and re-layouts, adjoint_weights(): return jnp.stack(parts, axis=4).reshape(48 * co, 4 * c)  16.8 us
    all_gather x1, blocking collectives, shards(): stats = lax.all_gather(st, 'space')  13.7 us
    pallas_call x1, Pallas kernels, norm_sums(): call(lambda *refs: sums_kernel(local_count, total_count, *refs), jax.Shap...  13.3 us
  transfers between devices with their start and end apart: 8, of which 3 were waited for; matrix products, arithmetic and copies ran while one was open for 7% of the time, Pallas kernels for 3%

profile of v1, /device:TPU:0, one launch (start us, length us, event | category | flops | bytes accessed | tf_op | source)
XLA Modules:
  0.0 408.3 jit_solution(12112114346451573126)
XLA Ops:
  7.2 5.4 %fusion = (bf16[8,32,1,1024]{3,2,1,0:T(2,128)(2,1)S(1)}, bf16[8,32,1,1024]{3,2,1,0:T(2,128)(2,1)S(1)}) fusion(bf16[8,32,8,1024]{3,2,1,0:T(8,128)(2,1)} %param.10), kind=kLoop, calls=%fused_computation.21 | loop fusion | bytes 2097152 | tf_op jit(solution)/shard_map/slice | solution.py:816
  15.1 6.4 %collective-permute-start = (bf16[8,32,1,1024]{3,1,0,2:T(8,128)(2,1)}, bf16[8,32,1,1024]{3,1,0,2:T(8,128)(2,1)}, u32[]{:S(2)}, u32[]{:S(2)}) collective-permute-start(bf16[8,32,1,1024]{3,1,0,2:T(8,128)(2,1)} %copy.66), channel_id=1, source_target_pairs={{0,1},{1,2},{2,3},{4,5},{5,6},{6,7},{8,9},{9,10},{10,11},{12,13},{... | collective-permute-start | bytes 1572872 | tf_op jit(solution)/shard_map/ppermute | solution.py:801
  26.5 3.3 collective-permute-done.1
  34.4 44.5 %first_conv.1 = (f32[4,8,32,16,256]{4,3,2,1,0:T(8,128)}, bf16[5,9,34,16,128]{4,3,2,1,0:T(8,128)(2,1)}, f32[2,128]{1,0:T(2,128)}) custom-call(bf16[8,256,1024]{2,1,0:T(8,128)(2,1)} %bitcast.60, bf16[8,64,1024]{2,1,0:T(8,128)(2,1)} %maximum_bitcast_fusion.refs_1_, bf16[256,384]{1,0:T(8,128)(2,1)} %constant.16.clone.refs_2_, ...), custom_call_target="tpu_custom_call" | custom-call | tf_op jit(solution)/shard_map/first_conv/pallas_call | solution.py:223
  78.9 13.7 %all-gather.2.refs_1_.refs_2_ = f32[4,2,128]{2,1,0:T(2,128)} all-gather(f32[1,2,128]{2,1,0:T(2,128)} %bitcast.74), channel_id=2, replica_groups=mesh['dp'=8,'space'=4] {'space'}, dimensions={0}, use_global_device_ids=true | all-gather | bytes 5120 | tf_op jit(solution)/shard_map/all_gather | solution.py:828
  92.6 11.4 %normalise_pool.1 = (bf16[4,8,16,16,128]{4,3,2,1,0:T(8,128)(2,1)}, bf16[4,16,16,128]{3,2,1,0:T(8,128)(2,1)}, bf16[4,16,16,128]{3,2,1,0:T(8,128)(2,1)}) custom-call(f32[4,8,32,16,256]{4,3,2,1,0:T(8,128)} %get-tuple-element.20.refs_0_, f32[4,2,128]{2,1,0:T(2,128)} %all-gather.2.refs_1_.refs_2_, f32[2,128]{1,0:T(2,128)} %maximum_maximum_fusion.refs_2_.refs_3_), custom_call_target="tpu_custom_call" | custom-call | tf_op jit(solution)/shard_map/normalise_pool/pallas_call | solution.py:300
  106.9 10.9 %all-gather.3 = f32[4,2,4]{2,1,0:T(2,128)} all-gather(f32[1,2,4]{2,1,0:T(2,128)S(1)} %bitcast.73), channel_id=1, replica_groups=mesh['dp'=8,'space'=4] {'space'}, dimensions={0}, use_global_device_ids=true | all-gather | bytes 160 | tf_op jit(solution)/shard_map/all_gather | solution.py:825
  121.6 17.2 %second_conv.1 = (bf16[3,10,18,16,128]{4,3,2,1,0:T(8,128)(2,1)}, f32[2,8,16,16,256]{4,3,2,1,0:T(8,128)}, bf16[128,8,128]{2,1,0:T(8,128)(2,1)}, f32[8,128]{1,0:T(8,128)}) custom-call(s32[1]{0:T(128)} %bitcast.11.refs_0_, bf16[4,8,16,16,128]{4,3,2,1,0:T(8,128)(2,1)} %get-tuple-element.22.refs_1_, bf16[4,16,16,128]{3,2,1,0:T(8,128)(2,1)} %copy-done.2, ...), custom_call_target="tpu_custom_call" | custom-call | tf_op jit(solution)/shard_map/second_conv/pallas_call | solution.py:423
  138.8 9.4 %psum.42.refs_1_ = f32[8,128]{1,0:T(8,128)} all-reduce(f32[8,128]{1,0:T(8,128)} %get-tuple-element.25), channel_id=1, replica_groups=mesh['dp'=8,'space'=4] {'space'}, use_global_device_ids=true, to_apply=%region_0.1 | all-reduce | flops 1024 | bytes 8192 | tf_op jit(solution)/shard_map/psum | solution.py:832
  148.2 11.3 %dense_layers.1 = (f32[8,128]{1,0:T(8,128)}, bf16[8,128]{1,0:T(8,128)(2,1)}, f32[4,128]{1,0:T(4,128)}, bf16[4,8,16,16,128]{4,3,2,1,0:T(8,128)(2,1)}) custom-call(s32[1]{0:T(128)} %bitcast.11.refs_0_, f32[8,128]{1,0:T(8,128)} %psum.42.refs_1_, f32[8,4]{1,0:T(8,128)} %bitcast.71, f32[4,128]{1,0:T(4,128)} %convert_bitcast_fusion.refs_3_, ...), custom_call_target="tpu_custom_call" | custom-call | tf_op jit(solution)/shard_map/dense_layers/pallas_call | solution.py:517
  159.5 2.4 slice_bitcast_fusion
  163.1 5.4 %collective-permute-start.4 = (bf16[8,16,16,128]{3,2,1,0:T(8,128)(2,1)}, bf16[8,16,16,128]{3,2,1,0:T(8,128)(2,1)}, u32[]{:S(2)}, u32[]{:S(2)}) collective-permute-start(bf16[8,16,16,128]{3,2,1,0:T(8,128)(2,1)} %get-tuple-element.65), channel_id=1, source_target_pairs={{0,1},{1,2},{2,3},{4,5},{5,6},{6,7},{8,9},{9,10},{10,11},{12,13},{... | collective-permute-start | bytes 1572872 | tf_op jit(solution)/shard_map/ppermute | solution.py:801
  169.8 6.8 %copy.64 = bf16[3,4,4,128,4,64]{5,4,3,2,1,0:T(4,128)(2,1)} copy(bf16[3,4,4,128,4,64]{3,5,0,2,1,4:T(8,128)(2,1)S(1)} %pad_maximum_fusion) | data formatting | bytes 6291456 | tf_op jit(solution)/shard_map/reshape | solution.py:91
  176.6 10.0 %reshape.72.w_ref = bf16[6144,256]{1,0:T(8,128)(2,1)} reshape(bf16[3,4,4,128,4,64]{5,4,3,2,1,0:T(4,128)(2,1)} %copy.64) | data formatting | bytes 6291456 | tf_op jit(solution)/shard_map/reshape | solution.py:91
  186.6 10.6 %second_grad.1 = f32[128,1728]{1,0:T(8,128)} custom-call(bf16[4,8,16,16,128]{4,3,2,1,0:T(8,128)(2,1)} %get-tuple-element.27.bs_ref, bf16[3,10,18,16,128]{4,3,2,1,0:T(8,128)(2,1)} %get-tuple-element.29.pp_ref), custom_call_target="tpu_custom_call" | custom-call | tf_op jit(solution)/shard_map/second_grad/pallas_call | solution.py:591
  197.3 12.3 %second_back.1.refs_1_ = bf16[4,8,16,16,128]{4,3,2,1,0:T(8,128)(2,1)} custom-call(bf16[4,8,16,16,128]{4,3,2,1,0:T(8,128)(2,1)} %get-tuple-element.27.bs_ref, bf16[8,16,16,128]{3,2,1,0:T(8,128)(2,1)} %collective-permute-done.4.lo_ref, bf16[8,16,16,128]{3,2,1,0:T(8,128)(2,1)} %collective-permute-done.5.hi_ref, bf16[6144,256]{1,0:T(8,128)(2,1)} %reshape.72.w_ref), custom_call_target="tpu_custom_call" | custom-call | tf_op jit(solution)/shard_map/second_back/pallas_call | solution.py:670
  209.6 13.3 %norm_sums.1 = f32[2,128]{1,0:T(2,128)} custom-call(f32[4,8,32,16,256]{4,3,2,1,0:T(8,128)} %get-tuple-element.20.refs_0_, bf16[4,8,16,16,128]{4,3,2,1,0:T(8,128)(2,1)} %second_back.1.refs_1_, f32[4,2,128]{2,1,0:T(2,128)} %all-gather.2.refs_1_.refs_2_, f32[2,128]{1,0:T(2,128)} %maximum_maximum_fusion.refs_2_.refs_3_), custom_call_target="tpu_custom_call" | custom-call | tf_op jit(solution)/shard_map/norm_sums/pallas_call | solution.py:713
  222.9 10.1 %psum.43.refs_4_ = f32[2,128]{1,0:T(2,128)} all-reduce(f32[2,128]{1,0:T(2,128)} %norm_sums.1), channel_id=1, replica_groups=mesh['dp'=8,'space'=4] {'space'}, use_global_device_ids=true, to_apply=%region_1.2 | all-reduce | flops 256 | bytes 2048 | tf_op jit(solution)/shard_map/psum | solution.py:845
  232.9 33.2 %first_grad.1 = f32[64,864]{1,0:T(8,128)} custom-call(f32[4,8,32,16,256]{4,3,2,1,0:T(8,128)} %get-tuple-element.20.refs_0_, bf16[4,8,16,16,128]{4,3,2,1,0:T(8,128)(2,1)} %second_back.1.refs_1_, f32[4,2,128]{2,1,0:T(2,128)} %all-gather.2.refs_1_.refs_2_, f32[2,128]{1,0:T(2,128)} %maximum_maximum_fusion.refs_2_.refs_3_, f32[2,128]{1,0:T(2,128)} %psum.43.refs_4_, ...), custom_call_target="tpu_custom_call" | custom-call | tf_op jit(solution)/shard_map/first_grad/pallas_call | solution.py:780
  266.2 3.3 all-to-all-start
  269.5 10.1 %all-gather.1 = bf16[64,128]{1,0:T(8,128)(2,1)} all-gather(bf16[8,128]{1,0:T(8,128)(2,1)S(1)} %copy-done.6), channel_id=3, replica_groups=mesh['dp'=8,'space'=4] {'dp'}, dimensions={0}, use_global_device_ids=true | all-gather | bytes 18432 | tf_op jit(solution)/shard_map/all_gather | solution.py:840
  283.9 39.5 %all-reduce.10 = (f32[2,128]{1,0:T(2,128)}, f32[128,4]{0,1:T(4,128)}) all-reduce(f32[2,128]{1,0:T(2,128)S(1)} %copy-done.5, f32[128,4]{0,1:T(4,128)S(1)} %bitcast.72), channel_id=1, replica_groups=mesh['dp'=8,'space'=4] {'dp','space'}, use_global_device_ids=true, to_apply=%region_3.4 | all-reduce | flops 768 | bytes 6144 | tf_op jit(solution)/shard_map/psum | solution.py:848
  323.3 74.1 %all-reduce.14.cloned.1.call-done = (f32[64,864]{1,0:T(8,128)}, f32[128,1728]{1,0:T(8,128)}) async-done(((f32[64,864]{1,0:T(8,128)}, f32[128,1728]{1,0:T(8,128)}), (f32[64,864]{1,0:T(8,128)}, f32[128,1728]{1,0:T(8,128)})) %all-reduce.14.cloned.1.call-update) | async-done | bytes 1105936 | tf_op jit(solution)/shard_map/psum | solution.py:848
  397.5 2.4 copy.61
  (57 shorter events, 27.0 us)
Async XLA Ops:
  7.2 390.3 %all-reduce.14.cloned.1.call-start = ((), (), s32[]{:S(2)}) async-start(), calls=%async_computation.1 | async-start | bytes 2293760 | tf_op jit(solution)/shard_map/psum | solution.py:848
  12.7 8.8 %copy-start.4 = (bf16[64,864]{1,0:T(8,128)(2,1)S(1)}, bf16[64,864]{1,0:T(8,128)(2,1)}, u32[]{:S(2)}) copy-start(bf16[64,864]{1,0:T(8,128)(2,1)} %param.11) | copy-start | bytes 331780
  12.9 17.0 %collective-permute-start.1 = (bf16[8,32,1,1024]{3,1,0,2:T(8,128)(2,1)S(1)}, bf16[8,32,1,1024]{3,1,0,2:T(8,128)(2,1)}, u32[]{:S(2)}, u32[]{:S(2)}) collective-permute-start(bf16[8,32,1,1024]{3,1,0,2:T(8,128)(2,1)S(1)} %copy.67), channel_id=1, source_target_pairs={{1,0},{2,1},{3,2},{5,4},{6,5},{7,6},{9,8},{10,9},{11,10},{13,12},{... | collective-permute-start | bytes 1572872 | tf_op jit(solution)/shard_map/ppermute | solution.py:802
  15.1 17.1 %collective-permute-start = (bf16[8,32,1,1024]{3,1,0,2:T(8,128)(2,1)}, bf16[8,32,1,1024]{3,1,0,2:T(8,128)(2,1)}, u32[]{:S(2)}, u32[]{:S(2)}) collective-permute-start(bf16[8,32,1,1024]{3,1,0,2:T(8,128)(2,1)} %copy.66), channel_id=1, source_target_pairs={{0,1},{1,2},{2,3},{4,5},{5,6},{6,7},{8,9},{9,10},{10,11},{12,13},{... | collective-permute-start | bytes 1572872 | tf_op jit(solution)/shard_map/ppermute | solution.py:801
  23.6 2.0 copy-start.10
  23.6 2.0 copy-start.11
  23.6 2.6 copy-start
  104.1 2.9 copy-start.8
  104.1 16.8 %collective-permute-start.2 = (bf16[4,16,16,128]{3,2,1,0:T(8,128)(2,1)}, bf16[4,16,16,128]{3,2,1,0:T(8,128)(2,1)S(1)}, u32[]{:S(2)}, u32[]{:S(2)}) collective-permute-start(bf16[4,16,16,128]{3,2,1,0:T(8,128)(2,1)} %get-tuple-element.23), channel_id=1, source_target_pairs={{0,1},{1,2},{2,3},{4,5},{5,6},{6,7},{8,9},{9,10},{10,11},{12,13},{... | collective-permute-start | bytes 786440 | tf_op jit(solution)/shard_map/ppermute | solution.py:801
  105.5 15.4 %collective-permute-start.3 = (bf16[4,16,16,128]{3,2,1,0:T(8,128)(2,1)}, bf16[4,16,16,128]{3,2,1,0:T(8,128)(2,1)S(1)}, u32[]{:S(2)}, u32[]{:S(2)}) collective-permute-start(bf16[4,16,16,128]{3,2,1,0:T(8,128)(2,1)} %get-tuple-element.24), channel_id=1, source_target_pairs={{1,0},{2,1},{3,2},{5,4},{6,5},{7,6},{9,8},{10,9},{11,10},{13,12},{... | collective-permute-start | bytes 786440 | tf_op jit(solution)/shard_map/ppermute | solution.py:802
  117.8 2.4 copy-start.9
  120.8 0.7 copy-start.2
  120.9 0.8 copy-start.3
  161.9 35.4 %collective-permute-start.5 = (bf16[8,16,16,128]{3,2,1,0:T(8,128)(2,1)}, bf16[8,16,16,128]{3,2,1,0:T(8,128)(2,1)}, u32[]{:S(2)}, u32[]{:S(2)}) collective-permute-start(bf16[8,16,16,128]{3,2,1,0:T(8,128)(2,1)} %get-tuple-element.64), channel_id=1, source_target_pairs={{1,0},{2,1},{3,2},{5,4},{6,5},{7,6},{9,8},{10,9},{11,10},{13,12},{... | collective-permute-start | bytes 1572872 | tf_op jit(solution)/shard_map/ppermute | solution.py:802
  163.1 34.1 %collective-permute-start.4 = (bf16[8,16,16,128]{3,2,1,0:T(8,128)(2,1)}, bf16[8,16,16,128]{3,2,1,0:T(8,128)(2,1)}, u32[]{:S(2)}, u32[]{:S(2)}) collective-permute-start(bf16[8,16,16,128]{3,2,1,0:T(8,128)(2,1)} %get-tuple-element.65), channel_id=1, source_target_pairs={{0,1},{1,2},{2,3},{4,5},{5,6},{6,7},{8,9},{9,10},{10,11},{12,13},{... | collective-permute-start | bytes 1572872 | tf_op jit(solution)/shard_map/ppermute | solution.py:801
  232.9 36.6 %copy-start.6 = (bf16[8,128]{1,0:T(8,128)(2,1)S(1)}, bf16[8,128]{1,0:T(8,128)(2,1)}, u32[]{:S(2)}) copy-start(bf16[8,128]{1,0:T(8,128)(2,1)} %get-tuple-element.31) | copy-start | bytes 6148
  266.2 17.7 %copy-start.5 = (f32[2,128]{1,0:T(2,128)S(1)}, f32[2,128]{1,0:T(2,128)}, u32[]{:S(2)}) copy-start(f32[2,128]{1,0:T(2,128)} %norm_sums.1) | copy-start | bytes 3076
  266.2 17.7 %copy-start.7 = (f32[4,128]{1,0:T(4,128)S(1)}, f32[4,128]{1,0:T(4,128)}, u32[]{:S(2)}) copy-start(f32[4,128]{1,0:T(4,128)} %get-tuple-element.32) | copy-start | bytes 6148
  266.2 14.7 %all-to-all-start = ((bf16[32,4,8,128]{3,2,1,0:T(8,128)(2,1)}), bf16[32,4,8,128]{3,2,1,0:T(8,128)(2,1)S(1)}, u32[]{:S(2)}, u32[]{:S(2)}) async-start(bf16[32,4,8,128]{3,2,1,0:T(8,128)(2,1)} %bitcast.31), calls=%async_computation | async-start | bytes 524288 | tf_op jit(solution)/shard_map/all_to_all | solution.py:838
  280.9 0.7 copy-start.1
Sparse Core Ops, SparseCore 0:
  266.3 131.0 all-reduce.13

commit v2 on v1

--- a/solution.py
+++ b/solution.py
@@ -6,6 +6,7 @@
 from jax.experimental.pallas import tpu as pltpu
 from jax.sharding import PartitionSpec as P
 
+
 GRID = 32
 HALVES = 2
 LANES = 128
@@ -50,45 +51,99 @@
     return values + roll_half(values)
 
 
-def call(kernel, out_shape, **kwargs):
-    return pl.pallas_call(kernel, out_shape=out_shape, interpret=INTERPRET, **kwargs)
+def call(kernel, out_shape, cost_us=1.0, **kwargs):
+    cost = pl.CostEstimate(
+        flops=int(cost_us * 1e9), bytes_accessed=int(cost_us * 3e6), transcendentals=0
+    )
+    return pl.pallas_call(
+        kernel, out_shape=out_shape, interpret=INTERPRET, cost_estimate=cost, **kwargs
+    )
 
 
 def whole_spec(shape):
     return pl.BlockSpec(shape, lambda *_: (0,) * len(shape), pipeline_mode=pl.Buffered(1))
 
 
-def first_weights(conv_in):
-    co = conv_in.shape[0]
-    c = conv_in.shape[1] // 27
-    w = conv_in.reshape(co, 3, 3, 3, c).transpose(3, 1, 2, 4, 0)
-    parts = [
-        jnp.pad(w, ((0, 0), (px, 1 - px), (py, 1 - py), (0, 0), (0, 0)))
-        for px in (0, 1)
-        for py in (0, 1)
-    ]
-    w = jnp.stack(parts, axis=4).reshape(3, 2, 2, 2, 2, c, 4 * co)
-    return w.transpose(0, 1, 3, 4, 2, 5, 6).reshape(3 * 16 * c, 4 * co)
-
-
-def second_weights(conv_out):
-    co = conv_out.shape[0]
-    c = conv_out.shape[1] // 27
-    w = conv_out.reshape(co, 3, 3, 3, c).transpose(2, 3, 1, 4, 0)
-    parts = [jnp.pad(w, ((0, 0), (0, 0), (px, 1 - px), (0, 0), (0, 0))) for px in (0, 1)]
-    return jnp.stack(parts, axis=4).reshape(9 * 4 * c, 2 * co)
-
-
-def adjoint_weights(conv_out):
-    co = conv_out.shape[0]
-    c = conv_out.shape[1] // 27
-    w = conv_out.reshape(co, 3, 3, 3, c)[:, ::-1, ::-1, ::-1].transpose(3, 1, 2, 0, 4)
-    parts = [
-        jnp.pad(w, ((0, 0), (px, 1 - px), (py, 1 - py), (0, 0), (0, 0)))
-        for px in (0, 1)
-        for py in (0, 1)
-    ]
-    return jnp.stack(parts, axis=4).reshape(48 * co, 4 * c)
+def weights_kernel(c_in, c_mid, ci_ref, co_ref, w1_ref, w2_ref, v3_ref, t1, t2):
+    def offset(a, b, d):
+        return (a * 3 + b) * 3 + d
+
+    for k in range(ci_ref.shape[1] // LANES):
+        lanes = slice(k * LANES, (k + 1) * LANES)
+        t1[lanes, :] = both_halves(ci_ref[:, lanes].astype(F32).T)
+    for k in range(co_ref.shape[1] // LANES):
+        lanes = slice(k * LANES, (k + 1) * LANES)
+        t2[lanes, :] = co_ref[:, lanes].astype(F32).T
+    mask = low_half((c_in, LANES))
+    zero = jnp.zeros((c_in, LANES), F32)
+    row = 0
+    for d in range(3):
+        for kk in range(2):
+            for mm in range(2):
+                for yo in range(2):
+                    for xo in range(2):
+                        for px in range(2):
+                            a = 2 * kk + xo - px
+                            parts = []
+                            for py in range(2):
+                                b = 2 * mm + yo - py
+                                if 0 <= a <= 2 and 0 <= b <= 2:
+                                    at = offset(a, b, d) * c_in
+                                    parts.append(t1[at : at + c_in, :])
+                                else:
+                                    parts.append(zero)
+                            w1_ref[row : row + c_in, px * LANES : (px + 1) * LANES] = jnp.where(
+                                mask, parts[0], parts[1]
+                            ).astype(BF16)
+                        row += c_in
+    row = 0
+    for b in range(3):
+        for d in range(3):
+            for xw in range(4):
+                for px in range(2):
+                    a = xw - px
+                    if 0 <= a <= 2:
+                        at = offset(a, b, d) * c_mid
+                        part = t2[at : at + c_mid, :].astype(BF16)
+                    else:
+                        part = jnp.zeros((c_mid, LANES), BF16)
+                    w2_ref[row : row + c_mid, px * LANES : (px + 1) * LANES] = part
+                row += c_mid
+    mask = low_half((LANES, LANES))
+    zero = jnp.zeros((LANES, LANES), F32)
+    for d in range(3):
+        for a in range(3):
+            for yw in range(4):
+                parts = []
+                for py in range(2):
+                    b = yw - py
+                    if 0 <= b <= 2:
+                        o = offset(2 - a, 2 - b, 2 - d)
+                        v = co_ref[:, o // 2 * LANES : (o // 2 + 1) * LANES].astype(F32)
+                        parts.append(v if o % 2 == py else roll_half(v))
+                    else:
+                        parts.append(zero)
+                v3_ref[d, a, yw] = jnp.where(mask, parts[0], parts[1]).astype(BF16)
+
+
+def make_weights(conv_in, conv_out):
+    c_in = conv_in.shape[1] // 27
+    c_mid = conv_out.shape[1] // 27
+    wide_in = -(-conv_in.shape[1] // LANES) * LANES
+    wide_out = -(-conv_out.shape[1] // LANES) * LANES
+    ci = jnp.pad(conv_in, ((0, LANES - conv_in.shape[0]), (0, wide_in - conv_in.shape[1])))
+    co = jnp.pad(conv_out, ((0, 0), (0, wide_out - conv_out.shape[1])))
+    return call(
+        lambda *refs: weights_kernel(c_in, c_mid, *refs),
+        (
+            jax.ShapeDtypeStruct((48 * c_in, 2 * LANES), BF16),
+            jax.ShapeDtypeStruct((36 * c_mid, 2 * LANES), BF16),
+            jax.ShapeDtypeStruct((3, 3, 4, LANES, LANES), BF16),
+        ),
+        5.0,
+        scratch_shapes=[pltpu.VMEM((wide_in, LANES), F32), pltpu.VMEM((wide_out, LANES), F32)],
+        name="weights",
+    )(ci, co)
 
 
 def half_pads(before, after):
@@ -99,70 +154,114 @@
     )
 
 
-def first_kernel(planes, samples, refs):
-    (x_ref, halo_ref, pa_ref, pb_ref, w_ref, f_ref, xb_ref, st_ref, z_ref, w_acc) = refs
-    i = pl.program_id(0)
-    pairs = planes // 2 + 1
+def gather_rows(src_ref, sel_ref, z_ref, samples):
     half_y = GRID // HALVES
     chunks = z_ref.shape[0]
     inner = HALVES * samples
     groups = GRID * GRID // LANES
     per_group = LANES // GRID
 
-    @pl.when(i == 0)
-    def _():
-        def gather(t, carry):
-            s = t % samples
-            q = t // samples
-            for h in range(HALVES):
-                g = q + h * (groups // HALVES)
-                lanes = pl.ds(pl.multiple_of(g * LANES, LANES), LANES)
-                t_val = dot_rows(x_ref[s, :, lanes], pa_ref[...]) + dot_rows(
-                    halo_ref[s, :, lanes], pb_ref[...]
-                )
-                start = (per_group * q + 1) * GRID * inner + h * samples + s
-                for k in range(chunks):
-                    z_ref[k, pl.ds(start, LANES, stride=inner), :] = t_val[
-                        :, k * LANES : (k + 1) * LANES
-                    ]
-            return carry
-
-        lax.fori_loop(0, samples * groups // HALVES, gather, 0)
-        row = GRID * inner
-
-        def plane_of(k, y):
-            start = pl.multiple_of(y * row, row)
-            return z_ref[k, pl.ds(start, row), :]
-
-        for k in range(chunks):
-            last = plane_of(k, half_y).reshape(GRID, inner, LANES)
-            head = plane_of(k, 1).reshape(GRID, inner, LANES)
-            lo, hi = half_pads(last, head)
-            z_ref[k, 0:row, :] = lo.reshape(row, LANES)
-            z_ref[k, (half_y + 1) * row : (half_y + 2) * row, :] = hi.reshape(row, LANES)
-
-        def assemble(m, carry):
-            mask = low_half((row, LANES))
-            for k in range(pairs):
-                a = plane_of(k // 2, 2 * m)
-                b = plane_of(k // 2, 2 * m + 1)
-                if k % 2 == 0:
-                    b = roll_half(b)
-                else:
-                    a = roll_half(a)
-                both = jnp.where(mask, a, b).astype(BF16)
-                xb_ref[k, m, 1 : GRID + 1] = both.reshape(GRID, inner, LANES)
-                zero = jnp.zeros((inner, LANES), BF16)
-                xb_ref[k, m, 0] = zero
-                xb_ref[k, m, GRID + 1] = zero
-            return carry
-
-        lax.fori_loop(0, half_y // 2 + 1, assemble, 0)
-        w_acc[...] = jnp.zeros_like(w_acc)
-
+    def gather(t, carry):
+        s = t % samples
+        q = t // samples
+        for h in range(HALVES):
+            g = q + h * (groups // HALVES)
+            lanes = pl.ds(pl.multiple_of(g * LANES, LANES), LANES)
+            val = dot_rows(src_ref[s, :, lanes], sel_ref[...])
+            start = (per_group * q + 1) * GRID * inner + h * samples + s
+            for k in range(chunks):
+                z_ref[k, pl.ds(start, LANES, stride=inner), :] = val[:, k * LANES : (k + 1) * LANES]
+        return carry
+
+    lax.fori_loop(0, samples * groups // HALVES, gather, 0)
+    row = GRID * inner
+    for k in range(chunks):
+        last = plane_of(z_ref, k, half_y, row).reshape(GRID, inner, LANES)
+        head = plane_of(z_ref, k, 1, row).reshape(GRID, inner, LANES)
+        lo, hi = half_pads(last, head)
+        z_ref[k, 0:row, :] = lo.reshape(row, LANES)
+        z_ref[k, (half_y + 1) * row : (half_y + 2) * row, :] = hi.reshape(row, LANES)
+
+
+def plane_of(z_ref, k, y, row):
+    return z_ref[k, pl.ds(pl.multiple_of(y * row, row), row), :]
+
+
+def prepare_kernel(planes, samples, x_ref, pa_ref, xb_ref, z_ref):
+    pairs = planes // 2 + 1
+    half_y = GRID // HALVES
+    inner = HALVES * samples
+    row = GRID * inner
+    gather_rows(x_ref, pa_ref, z_ref, samples)
+
+    def assemble(m, carry):
+        mask = low_half((row, LANES))
+        for k in range(pairs):
+            a = plane_of(z_ref, k // 2, 2 * m, row)
+            b = plane_of(z_ref, k // 2, 2 * m + 1, row)
+            if k % 2 == 0:
+                b = roll_half(b)
+            else:
+                a = roll_half(a)
+            both = jnp.where(mask, a, b).astype(BF16)
+            xb_ref[k, m, 1 : GRID + 1] = both.reshape(GRID, inner, LANES)
+            zero = jnp.zeros((inner, LANES), BF16)
+            xb_ref[k, m, 0] = zero
+            xb_ref[k, m, GRID + 1] = zero
+        return carry
+
+    lax.fori_loop(0, half_y // 2 + 1, assemble, 0)
+
+
+def prepare(x, planes, c):
+    samples = x.shape[0]
+    pairs = planes // 2 + 1
+    chunks = -(-pairs * 2 * c // LANES)
+    inner = HALVES * samples
+    half_y = GRID // HALVES
+    pa = np.zeros((c * planes, chunks * LANES), np.float32)
+    for ch in range(c):
+        for p in range(planes):
+            pa[ch * planes + p, (p + 1) * c + ch] = 1.0
+    return call(
+        lambda *refs: prepare_kernel(planes, samples, *refs),
+        jax.ShapeDtypeStruct((pairs, half_y // 2 + 1, GRID + 2, inner, LANES), BF16),
+        20.0,
+        scratch_shapes=[pltpu.VMEM((chunks, (half_y + 2) * GRID * inner, LANES), F32)],
+        name="prepare",
+    )(x, jnp.asarray(pa, BF16))
+
+
+def first_kernel(planes, samples, refs):
+    (xi_ref, halo_ref, pb_ref, w_ref, f_ref, xb_ref, st_ref, z_ref, w_acc) = refs
+    i = pl.program_id(0)
+    pairs = planes // 2 + 1
+    half_y = GRID // HALVES
+    inner = HALVES * samples
     rows = GRID * inner
     blocks = half_y // 2
     per_block = rows // 8
+
+    @pl.when(i == 0)
+    def _():
+        gather_rows(halo_ref, pb_ref, z_ref, samples)
+
+        def patch(m, carry):
+            lane = lax.broadcasted_iota(jnp.int32, (rows, LANES), 1)
+            a = plane_of(z_ref, 0, 2 * m, rows)
+            b = plane_of(z_ref, 0, 2 * m + 1, rows)
+            edge = jnp.where(lane < LANES // 2, a, b)
+            first = lane % (LANES // 2) < LANES // 4
+            for k in range(pairs):
+                xb_ref[k, m] = xi_ref[k, m]
+            for k in (0, pairs - 1):
+                own = xi_ref[k, m, 1 : GRID + 1].astype(F32).reshape(rows, LANES)
+                both = jnp.where(first, edge, own) if k == 0 else jnp.where(first, own, edge)
+                xb_ref[k, m, 1 : GRID + 1] = both.astype(BF16).reshape(GRID, inner, LANES)
+            return carry
+
+        lax.fori_loop(0, blocks + 1, patch, 0)
+        w_acc[...] = jnp.zeros_like(w_acc)
 
     def conv(yb, carry):
         pieces = []
@@ -192,54 +291,46 @@
         mean = w_acc[0]
         m = jnp.mean(mean, axis=0, keepdims=True)
         m = both_halves((m[:, :LANES] + m[:, LANES:]) * 0.5) * 0.5
-        wide = jnp.concatenate([m, m], axis=1)
-        dev = mean - wide
+        dev = mean - wide(m)
         q = jnp.sum(w_acc[1] + count * dev * dev, axis=0, keepdims=True)
         q = both_halves(q[:, :LANES] + q[:, LANES:])
-        st_ref[...] = jnp.concatenate([m, q], axis=0)
-
-
-def first_conv(x, halo, w1, planes):
-    samples = x.shape[0]
+        st = jnp.concatenate([m, q], axis=0)
+        st_ref[...] = st
+
+
+def first_conv(xi, halo, w1, planes):
+    samples = halo.shape[0]
     c = halo.shape[1] // 2
-    pairs = planes // 2 + 1
-    used = pairs * 2 * c
-    chunks = -(-used // LANES)
     inner = HALVES * samples
     half_y = GRID // HALVES
-    pa = np.zeros((c * planes, chunks * LANES), np.float32)
-    pb = np.zeros((2 * c, chunks * LANES), np.float32)
-    for ch in range(c):
-        for p in range(planes):
-            pa[ch * planes + p, (p + 1) * c + ch] = 1.0
+    pb = np.zeros((2 * c, LANES), np.float32)
+    for ch in range(2 * c):
         pb[ch, ch] = 1.0
-        pb[c + ch, (planes + 1) * c + ch] = 1.0
-    pa = jnp.asarray(pa, BF16)
+        pb[ch, LANES // 2 + ch] = 1.0
     pb = jnp.asarray(pb, BF16)
     nxb = planes // 2
-    nyb = half_y // 2
-    f_shape = (nxb, nyb, GRID, inner, 2 * LANES)
-    xb_shape = (pairs, nyb + 1, GRID + 2, inner, LANES)
+    f_shape = (nxb, half_y // 2, GRID, inner, 2 * LANES)
     return call(
         lambda *refs: first_kernel(planes, samples, refs),
         (
             jax.ShapeDtypeStruct(f_shape, F32),
-            jax.ShapeDtypeStruct(xb_shape, BF16),
+            jax.ShapeDtypeStruct(xi.shape, BF16),
             jax.ShapeDtypeStruct((2, LANES), F32),
         ),
+        25.0,
         grid=(nxb,),
-        in_specs=[whole_spec(a.shape) for a in (x, halo, pa, pb, w1)],
+        in_specs=[whole_spec(a.shape) for a in (xi, halo, pb, w1)],
         out_specs=(
             pl.BlockSpec((1,) + f_shape[1:], lambda i: (i, 0, 0, 0, 0)),
-            whole_spec(xb_shape),
+            whole_spec(xi.shape),
             whole_spec((2, LANES)),
         ),
         scratch_shapes=[
-            pltpu.VMEM((chunks, (half_y + 2) * GRID * inner, LANES), F32),
+            pltpu.VMEM((1, (half_y + 2) * GRID * inner, LANES), F32),
             pltpu.VMEM((2, 8, 2 * LANES), F32),
         ],
         name="first_conv",
-    )(x, halo, pa, pb, w1)
+    )(xi, halo, pb, w1)
 
 
 def group_stats(st, local_count, total_count):
@@ -255,8 +346,7 @@
     return jnp.concatenate([row, row], axis=1)
 
 
-def pool_kernel(local_count, total_count, f_ref, st_ref, gs_ref, pd_ref, lo_ref, hi_ref):
-    i = pl.program_id(0)
+def pool_kernel(local_count, total_count, f_ref, st_ref, gs_ref, pd_ref, edge_ref=None):
     mean, inverse = group_stats(st_ref[...], local_count, total_count)
     mean = wide(mean)
     inverse = wide(inverse)
@@ -277,50 +367,52 @@
         return carry
 
     lax.fori_loop(0, nyb, step, 0)
-    half = nyb // 2
-
-    def pack(ref):
+    if edge_ref is not None:
+        half = nyb // 2
         mask = low_half((nz // 2, inner, LANES))
         for y in range(half):
-            ref[y] = jnp.where(mask, pd_ref[0, y].astype(F32), pd_ref[0, y + half].astype(F32)).astype(BF16)
-
-    @pl.when(i == 0)
-    def _():
-        pack(lo_ref)
-
-    @pl.when(i == pl.num_programs(0) - 1)
-    def _():
-        pack(hi_ref)
-
-
-def normalise_pool(f, st, gs, local_count, total_count):
+            edge_ref[0, y] = jnp.where(
+                mask, pd_ref[0, y].astype(F32), pd_ref[0, y + half].astype(F32)
+            ).astype(BF16)
+
+
+def normalise_pool(f, st, gs, local_count, total_count, edges):
     nxb, nyb, nz, inner, _ = f.shape
-    pd_shape = (nxb, nyb, nz // 2, inner, LANES)
-    edge = (nyb // 2, nz // 2, inner, LANES)
+    count = 2 if edges else nxb - 2
+    stride, base = (nxb - 1, 0) if edges else (1, 1)
+    pd_shape = (count, nyb, nz // 2, inner, LANES)
+    edge = (2, nyb // 2, nz // 2, inner, LANES)
+    shapes = [jax.ShapeDtypeStruct(pd_shape, BF16)]
+    specs = [pl.BlockSpec((1,) + pd_shape[1:], lambda i: (i, 0, 0, 0, 0))]
+    if edges:
+        shapes.append(jax.ShapeDtypeStruct(edge, BF16))
+        specs.append(pl.BlockSpec((1,) + edge[1:], lambda i: (i, 0, 0, 0, 0)))
     return call(
         lambda *refs: pool_kernel(local_count, total_count, *refs),
-        (
-            jax.ShapeDtypeStruct(pd_shape, BF16),
-            jax.ShapeDtypeStruct(edge, BF16),
-            jax.ShapeDtypeStruct(edge, BF16),
-        ),
-        grid=(nxb,),
+        shapes,
+        3.0 * count,
+        grid=(count,),
         in_specs=[
-            pl.BlockSpec((1,) + f.shape[1:], lambda i: (i, 0, 0, 0, 0)),
+            pl.BlockSpec((1,) + f.shape[1:], lambda i: (i * stride + base, 0, 0, 0, 0)),
             whole_spec(st.shape),
             whole_spec(gs.shape),
         ],
-        out_specs=(
-            pl.BlockSpec((1,) + pd_shape[1:], lambda i: (i, 0, 0, 0, 0)),
-            whole_spec(edge),
-            whole_spec(edge),
-        ),
-        name="normalise_pool",
+        out_specs=specs,
+        name="pool_edges" if edges else "pool_inside",
     )(f, st, gs)
 
 
-def second_kernel(samples, j_ref, pd_ref, lo_ref, hi_ref, w_ref, d_ref, pp_ref, sec_ref, fc_ref, hid_ref, ft, fcs):
-    planes, ny, nz, inner, _ = pd_ref.shape
+def second_kernel(samples, refs):
+    (j_ref, pe_ref, *mid, lo_ref, hi_ref, w_ref, d_ref, tg_ref,
+     pp_ref, sec_ref, fc_ref, hid_ref, ft, fcs) = refs
+    edges, ny, nz, inner, _ = pe_ref.shape
+    planes = edges + (mid[0].shape[0] if mid else 0)
+
+    def plane(p, y):
+        if p == 0 or p == planes - 1:
+            return pe_ref[min(p, 1), y].astype(F32)
+        return mid[0][p - 1, y].astype(F32)
+
     pairs = planes // 2 + 1
     half = ny // 2
     cells = fc_ref.shape[2]
@@ -333,8 +425,8 @@
     def assemble(y, carry):
         mask = low_half((nz, inner, LANES))
         for k in range(pairs):
-            a = unpack(lo_ref, y) if k == 0 else pd_ref[2 * k - 1, y].astype(F32)
-            b = unpack(hi_ref, y) if k == pairs - 1 else pd_ref[2 * k, y].astype(F32)
+            a = unpack(lo_ref, y) if k == 0 else plane(2 * k - 1, y)
+            b = unpack(hi_ref, y) if k == pairs - 1 else plane(2 * k, y)
             pp_ref[k, y + 1, 1 : nz + 1] = jnp.where(mask, a, b).astype(BF16)
         return carry
 
@@ -405,12 +497,19 @@
 
     zeros = [jnp.zeros((samples, LANES), F32) for _ in range(4)]
     acc = lax.fori_loop(0, channels // 8, dense, zeros)
-    hid_ref[...] = (acc[0] + acc[1]) + (acc[2] + acc[3])
-
-
-def second_conv(j, pd, lo, hi, w2, dense4, samples):
-    planes, ny, nz, inner, _ = pd.shape
-    channels, spaces, cells, units = dense4.shape
+    total = (acc[0] + acc[1]) + (acc[2] + acc[3])
+    own, targets_n = tg_ref.shape
+    hid_ref[0:samples] = total
+    hid_ref[samples : 2 * samples] = jnp.zeros_like(total)
+    for q in range(own):
+        at = samples + j_ref[0] * own + q
+        hid_ref[pl.ds(at, 1), 0:targets_n] = tg_ref[q : q + 1, :]
+
+
+def second_conv(j, pds, lo, hi, w2, dense4, targets, samples):
+    _, ny, nz, inner, _ = pds[0].shape
+    planes = sum(p.shape[0] for p in pds)
+    channels, _, cells, units = dense4.shape
     pairs = planes // 2 + 1
     nxb = planes // 2
     pp_shape = (pairs, ny + 2, nz + 2, inner, LANES)
@@ -421,48 +520,57 @@
         return pl.BlockSpec(shape, lambda i, j_ref: (0,) * len(shape), pipeline_mode=pl.Buffered(1))
 
     return call(
-        lambda *refs: second_kernel(samples, *refs),
+        lambda *refs: second_kernel(samples, refs),
         (
             jax.ShapeDtypeStruct(pp_shape, BF16),
             jax.ShapeDtypeStruct(sec_shape, F32),
             jax.ShapeDtypeStruct(fc_shape, BF16),
-            jax.ShapeDtypeStruct((samples, units), F32),
+            jax.ShapeDtypeStruct((2 * samples, units), F32),
         ),
+        17.0,
         grid_spec=pltpu.PrefetchScalarGridSpec(
             num_scalar_prefetch=1,
             grid=(1,),
-            in_specs=[const(pd.shape), const(lo.shape), const(hi.shape), const(w2.shape),
-                      pl.BlockSpec((channels, 1, cells, units), lambda i, j_ref: (0, j_ref[0], 0, 0), pipeline_mode=pl.Buffered(1))],
-            out_specs=(const(pp_shape), const(sec_shape), const(fc_shape), const((samples, units))),
+            in_specs=[const(p.shape) for p in pds] + [const(lo.shape), const(hi.shape), const(w2.shape),
+                      pl.BlockSpec((channels, 1, cells, units), lambda i, j_ref: (0, j_ref[0], 0, 0), pipeline_mode=pl.Buffered(1)),
+                      const(targets.shape)],
+            out_specs=(const(pp_shape), const(sec_shape), const(fc_shape), const((2 * samples, units))),
             scratch_shapes=[
                 pltpu.VMEM((nxb * (ny // 2) * (nz // 2) * inner, LANES), F32),
                 pltpu.VMEM((channels * samples, LANES), F32),
             ],
         ),
         name="second_conv",
-    )(j, pd, lo, hi, w2, dense4)
-
-
-def dense_kernel(samples, own, targets_n, j_ref, hp_ref, tg_ref, do_ref, d_ref, sec_ref,
+    )(j, *pds, lo, hi, w2, dense4, targets)
+
+
+def dense_kernel(samples, own, targets_n, j_ref, hp_ref, do_ref, d_ref, sec_ref,
                  pred_ref, bh_ref, gdo_ref, bs_ref, bfc, bf):
     nxb, ny, nz, inner, _ = sec_ref.shape
     channels = d_ref.shape[0]
     cells = d_ref.shape[2]
-    hp = hp_ref[...]
+    both = hp_ref[0]
+    for t in range(1, hp_ref.shape[0]):
+        both = both + hp_ref[t]
+    hp = both[0:samples]
+    goals = both[samples:]
     hidden = leaky_relu(hp).astype(BF16).astype(F32)
     row = lax.broadcasted_iota(jnp.int32, (samples, 1), 0)
     mine = (row // own) == j_ref[0]
     lane = lax.broadcasted_iota(jnp.int32, (samples, LANES), 1)
     preds = jnp.zeros((samples, LANES), F32)
+    gdo_ref[...] = jnp.zeros_like(gdo_ref)
     back = jnp.zeros_like(hp)
     for t in range(targets_n):
         weight = do_ref[t : t + 1, :]
         pred = jnp.sum(hidden * weight, axis=1, keepdims=True)
-        misfit = pred - tg_ref[:, t : t + 1]
+        misfit = pred - goals[:, t : t + 1]
         preds = jnp.where(lane == t, pred, preds)
         gdo_ref[t : t + 1, :] = jnp.sum(jnp.where(mine, hidden * misfit, 0.0), axis=0, keepdims=True)
         back = back + misfit * weight
-    pred_ref[...] = preds
+    for q in range(own):
+        picked = jnp.where(row == j_ref[0] * own + q, preds, 0.0)
+        pred_ref[q : q + 1, :] = jnp.sum(picked, axis=0, keepdims=True)[:, :targets_n]
     bh = (back * slope_of(hp)).astype(BF16)
     bh_ref[...] = bh
 
@@ -505,10 +613,11 @@
     lax.fori_loop(0, nxb * half, spread, 0)
 
 
-def dense_layers(j, hp, targets, dense_out_t, dense4, sec, own):
+def dense_layers(j, hp, dense_out_t, dense4, sec, own):
     nxb, ny, nz, inner, _ = sec.shape
-    channels, spaces, cells, units = dense4.shape
-    samples, targets_n = targets.shape
+    channels, _, cells, units = dense4.shape
+    samples = hp.shape[1] // 2
+    targets_n = dense_out_t.shape[0]
     bs_shape = (2 * nxb, ny, nz, inner, LANES)
 
     def const(shape):
@@ -517,43 +626,67 @@
     return call(
         lambda *refs: dense_kernel(samples, own, targets_n, *refs),
         (
-            jax.ShapeDtypeStruct((samples, LANES), F32),
+            jax.ShapeDtypeStruct((own, targets_n), F32),
             jax.ShapeDtypeStruct((samples, units), BF16),
-            jax.ShapeDtypeStruct((targets_n, units), F32),
+            jax.ShapeDtypeStruct((8, units), F32),
             jax.ShapeDtypeStruct(bs_shape, BF16),
         ),
+        11.0,
         grid_spec=pltpu.PrefetchScalarGridSpec(
             num_scalar_prefetch=1,
             grid=(1,),
-            in_specs=[const(hp.shape), const(targets.shape), const(dense_out_t.shape),
+            in_specs=[const(hp.shape), const(dense_out_t.shape),
                       pl.BlockSpec((channels, 1, cells, units), lambda i, j_ref: (0, j_ref[0], 0, 0), pipeline_mode=pl.Buffered(1)),
                       const(sec.shape)],
-            out_specs=(const((samples, LANES)), const((samples, units)), const((targets_n, units)), const(bs_shape)),
+            out_specs=(const((own, targets_n)), const((samples, units)), const((8, units)), const(bs_shape)),
             scratch_shapes=[
                 pltpu.VMEM((channels * samples, LANES), F32),
                 pltpu.VMEM((nxb * (ny // 2) * (nz // 2) * inner, LANES), F32),
             ],
         ),
         name="dense_layers",
-    )(j, hp, targets, dense_out_t, dense4, sec)
-
-
-def dense_grad_kernel(f_ref, b_ref, o_ref):
-    groups, spaces, chans, samples, cells = f_ref.shape
-    b = b_ref[...].astype(F32).reshape(groups * samples, b_ref.shape[2]).astype(BF16)
+    )(j, hp, dense_out_t, dense4, sec)
+
+
+def collect_kernel(spaces, samples, at_bh, at_grad, r_ref, t_ref, o_ref):
+    everyone = r_ref.shape[0]
+    groups = everyone // spaces
+    chans, _, cells, _ = o_ref.shape
+    total = r_ref[0, at_grad:].astype(F32)
+    for t in range(1, everyone):
+        total = total + r_ref[t, at_grad:].astype(F32)
+    total = total.astype(BF16)
+    for t in range(everyone):
+        t_ref[t] = total
+
+    def stack(j, row):
+        rows = [
+            r_ref[g * spaces + j, row : row + samples].astype(F32) for g in range(groups)
+        ]
+        return jnp.concatenate(rows, axis=0).astype(BF16)
+
+    b = stack(0, at_bh)
     for ch in range(chans):
         for j in range(spaces):
-            f = f_ref[:, j, ch].astype(F32).reshape(groups * samples, cells).astype(BF16)
-            o_ref[ch, j] = dot_rows(f, b)
-
-
-def dense_grad(feats, bh):
-    groups, spaces, chans, samples, cells = feats.shape
-    shape = (chans, spaces, cells, bh.shape[2])
-    return call(dense_grad_kernel, jax.ShapeDtypeStruct(shape, F32), name="dense_grad")(feats, bh)
-
-
-def second_grad_kernel(bs_ref, pp_ref, g_ref, acc):
+            o_ref[ch, j] = dot_rows(stack(j, ch * samples)[:, 0:cells], b)
+
+
+def collect(received, spaces, fc_shape):
+    everyone = received.shape[0]
+    channels, samples, cells = fc_shape
+    at_bh, at_grad, end = message_rows(everyone, fc_shape)
+    return call(
+        lambda *refs: collect_kernel(spaces, samples, at_bh, at_grad, *refs),
+        (
+            jax.ShapeDtypeStruct((everyone, end - at_grad, LANES), BF16),
+            jax.ShapeDtypeStruct((channels // everyone, spaces, cells, LANES), F32),
+        ),
+        4.0,
+        name="collect",
+    )(received)
+
+
+def second_grad_kernel(bs_ref, pp_ref, fc_ref, bh_ref, m_ref, acc, flat):
     planes, ny, nz, inner, _ = bs_ref.shape
     nxb = planes // 2
     half = ny // 2
@@ -583,17 +716,44 @@
     for o in range(9):
         both = acc[o, :LANES, 0 : 3 * mid] + acc[o, LANES:, mid : 4 * mid]
         for a in range(3):
-            at = (a * 9 + o) * mid
-            g_ref[:, at : at + mid] = both[:, a * mid : (a + 1) * mid]
-
-
-def second_grad(bs, pp):
+            at = a * 9 + o
+            block = at // 2 * LANES
+            half_at = (at % 2) * mid
+            flat[block : block + LANES, half_at : half_at + mid] = both[:, a * mid : (a + 1) * mid]
+    flat[13 * LANES :, mid:] = jnp.zeros((LANES, mid), F32)
+    everyone = m_ref.shape[0]
+    chans = fc_ref.shape[0] // everyone
+    samples, cells = fc_ref.shape[1:]
+    at_bh, at_grad, _ = message_rows(everyone, fc_ref.shape)
+    piece = 14 * LANES // everyone
+    bh = bh_ref[...].astype(F32)
+    pad = jnp.zeros((at_grad - at_bh - samples, LANES), F32)
+    side = jnp.concatenate([bh, pad], axis=0).astype(BF16)
+    for t in range(everyone):
+        f = fc_ref[t * chans : (t + 1) * chans].astype(F32).reshape(chans * samples, cells)
+        m_ref[t, 0 : chans * samples, 0:cells] = f.astype(BF16)
+        m_ref[t, at_bh:at_grad] = side
+        m_ref[t, at_grad : at_grad + piece] = flat[t * piece : (t + 1) * piece].astype(BF16)
+
+
+def message_rows(everyone, fc_shape):
+    at_bh = -(-(fc_shape[0] // everyone * fc_shape[1]) // 16) * 16
+    at_grad = at_bh + -(-fc_shape[1] // 16) * 16
+    return at_bh, at_grad, at_grad + 14 * LANES // everyone
+
+
+def second_grad(bs, pp, fc, bh, everyone):
+    rows = message_rows(everyone, fc.shape)[2]
     return call(
         second_grad_kernel,
-        jax.ShapeDtypeStruct((LANES, 27 * LANES // 2), F32),
-        scratch_shapes=[pltpu.VMEM((9, 2 * LANES, 2 * LANES), F32)],
+        jax.ShapeDtypeStruct((everyone, rows, LANES), BF16),
+        12.0,
+        scratch_shapes=[
+            pltpu.VMEM((9, 2 * LANES, 2 * LANES), F32),
+            pltpu.VMEM((14 * LANES, LANES), F32),
+        ],
         name="second_grad",
-    )(bs, pp)
+    )(bs, pp, fc, bh)
 
 
 def second_back_kernel(bs_ref, lo_ref, hi_ref, w_ref, bp_ref, pad):
@@ -647,9 +807,16 @@
                             axis=0,
                         )
                     )
-            out = out + dot(
-                jnp.concatenate(pieces, axis=1), w_ref[dz * depth : (dz + 1) * depth, :]
-            )
+            sides = []
+            for px in range(2):
+                blocks = [
+                    w_ref[dz, jx - px].reshape(depth // 4, LANES)
+                    if 0 <= jx - px <= 2
+                    else jnp.zeros((depth // 4, LANES), BF16)
+                    for jx in range(4)
+                ]
+                sides.append(jnp.concatenate(blocks, axis=0))
+            out = out + dot(jnp.concatenate(pieces, axis=1), jnp.concatenate(sides, axis=1))
         out = out.astype(BF16).astype(F32)
         mask = low_half((2 * rows, LANES))
         for px in range(2):
@@ -670,6 +837,7 @@
     return call(
         second_back_kernel,
         jax.ShapeDtypeStruct(bs.shape, BF16),
+        12.0,
         scratch_shapes=[pltpu.VMEM((planes + 2, ny + 2, nz + 2, inner, LANES), BF16)],
         name="second_back",
     )(bs, lo, hi, w3)
@@ -713,6 +881,7 @@
     return call(
         lambda *refs: sums_kernel(local_count, total_count, *refs),
         jax.ShapeDtypeStruct((2, LANES), F32),
+        13.0,
         grid=(f.shape[0],),
         in_specs=[
             pl.BlockSpec((1,) + f.shape[1:], lambda i: (i, 0, 0, 0, 0)),
@@ -726,13 +895,14 @@
     )(f, bp, st, gs)
 
 
-def first_grad_kernel(local_count, total_count, c, f_ref, bp_ref, st_ref, gs_ref, sum_ref, xa_ref, xc_ref, g_ref, acc):
+def first_grad_kernel(local_count, total_count, c, f_ref, bp_ref, st_ref, gs_ref, sum_ref, own_ref, gdo_ref, xa_ref, xc_ref, g_ref, acc):
     i = pl.program_id(0)
     mean, inverse = group_stats(st_ref[...], local_count, total_count)
     mean, inverse = wide(mean), wide(inverse)
     gain, shift = wide(gs_ref[0:1]), wide(gs_ref[1:2])
-    cross = wide(sum_ref[0:1]) * (1.0 / total_count)
-    plain = wide(sum_ref[1:2]) * (1.0 / total_count)
+    group_sums = jnp.sum(sum_ref[...], axis=0)
+    cross = wide(group_sums[0:1]) * (1.0 / total_count)
+    plain = wide(group_sums[1:2]) * (1.0 / total_count)
     scale = gain * inverse
     nz = f_ref.shape[2]
     inner = f_ref.shape[3]
@@ -759,6 +929,10 @@
     @pl.when(i == pl.num_programs(0) - 1)
     def _():
         co = LANES // 2
+        blocks = -(-27 * c // LANES)
+        g_ref[(blocks - 1) * co :, :] = jnp.zeros((g_ref.shape[0] - (blocks - 1) * co, LANES), F32)
+        g_ref[blocks * co : blocks * co + 2, :] = own_ref[...]
+        g_ref[blocks * co + 8 : blocks * co + 16, :] = gdo_ref[...]
         for a in range(3):
             for b in range(3):
                 for d in range(3):
@@ -771,15 +945,17 @@
                             part = acc[d * 2 + xw // 2, top : top + co, at : at + c]
                             total = part if total is None else total + part
                     at = ((a * 3 + b) * 3 + d) * c
-                    g_ref[:, at : at + c] = total
-
-
-def first_grad(f, bp, st, gs, sums, xb, c, local_count, total_count):
+                    row = at // LANES * co
+                    g_ref[row : row + co, at % LANES : at % LANES + c] = total
+
+
+def first_grad(f, bp, st, gs, sums, own, gdo, xb, c, local_count, total_count, rows):
     x_block = (1,) + xb.shape[1:]
-    out = (LANES // 2, 27 * c)
+    out = (rows, LANES)
     return call(
         lambda *refs: first_grad_kernel(local_count, total_count, c, *refs),
         jax.ShapeDtypeStruct(out, F32),
+        33.0,
         grid=(f.shape[0],),
         in_specs=[
             pl.BlockSpec((1,) + f.shape[1:], lambda i: (i, 0, 0, 0, 0)),
@@ -787,13 +963,59 @@
             whole_spec(st.shape),
             whole_spec(gs.shape),
             whole_spec(sums.shape),
+            whole_spec(own.shape),
+            whole_spec(gdo.shape),
             pl.BlockSpec(x_block, lambda i: (i, 0, 0, 0, 0)),
             pl.BlockSpec(x_block, lambda i: (i + 1, 0, 0, 0, 0)),
         ],
         out_specs=whole_spec(out),
         scratch_shapes=[pltpu.VMEM((6, 2 * LANES, 2 * LANES), F32)],
         name="first_grad",
-    )(f, bp, st, gs, sums, xb, xb)
+    )(f, bp, st, gs, sums, own, gdo, xb, xb)
+
+
+def add_kernel(r_ref, o_ref):
+    total = r_ref[0]
+    for t in range(1, r_ref.shape[0]):
+        total = total + r_ref[t]
+    total = total.astype(BF16)
+    for t in range(o_ref.shape[0]):
+        o_ref[t] = total
+
+
+def add_parts(parts):
+    return call(add_kernel, jax.ShapeDtypeStruct(parts.shape, BF16), 2.0, name="add_parts")(parts)
+
+
+def gather_all(value, axis):
+    count = lax.axis_size(axis)
+    others = [
+        lax.ppermute(value, axis, [(i, (i + k) % count) for i in range(count)])
+        for k in range(1, count)
+    ]
+    return jnp.stack([value] + others)
+
+
+def swap(parts, axes):
+    return lax.all_to_all(parts, axes, split_axis=0, concat_axis=0, tiled=True)
+
+
+def finish_second_kernel(r_ref, g_ref):
+    columns = g_ref.shape[1]
+    for k in range(r_ref.shape[0]):
+        width = min(LANES, columns - k * LANES)
+        g_ref[:, k * LANES : k * LANES + width] = r_ref[k].astype(F32)[:, 0:width]
+
+
+def finish_first_kernel(r_ref, g_ref, n_ref, gdo_ref):
+    co, columns = g_ref.shape
+    blocks = -(-columns // LANES)
+    for k in range(blocks):
+        width = min(LANES, columns - k * LANES)
+        g_ref[:, k * LANES : k * LANES + width] = r_ref[k * co : (k + 1) * co].astype(F32)[:, 0:width]
+    tail = r_ref[blocks * co : blocks * co + 16].astype(F32)
+    n_ref[...] = tail[0:2, 0 : n_ref.shape[1]]
+    gdo_ref[...] = tail[8:16].T[:, 0 : gdo_ref.shape[1]]
 
 
 def swap_edges(first, last, axis):
@@ -813,47 +1035,66 @@
     local_count = float(samples * planes * cells)
     total_count = local_count * spaces
 
+    everyone = groups * spaces
+    world = ("dp", "space")
+
     before, after = swap_edges(inputs[:, :, :1], inputs[:, :, planes - 1 :], "space")
-    halo = jnp.concatenate([before, after], axis=1).reshape(samples, 2 * c, cells)
-    w1 = first_weights(conv_in)
-    w2 = second_weights(conv_out)
-    w3 = adjoint_weights(conv_out)
+    w1, w2, v3 = make_weights(conv_in, conv_out)
+    xi = prepare(inputs.reshape(samples, c * planes, cells), planes, c)
     gs = jnp.stack([norm_gain, norm_shift])
     gs = jnp.concatenate([gs, gs], axis=1)
     j = lax.axis_index("space").astype(jnp.int32).reshape(1)
     dense4 = dense_in.reshape(channels, spaces, dense_in.shape[0] // (channels * spaces), units)
-    group_targets = lax.all_gather(targets, "space", axis=0, tiled=True)
-
-    f, xb, st = first_conv(inputs.reshape(samples, c * planes, cells), halo, w1, planes)
-    stats = lax.all_gather(st, "space")
-    pd, edge_lo, edge_hi = normalise_pool(f, stats, gs, local_count, total_count)
-    lo, hi = swap_edges(edge_lo, edge_hi, "space")
-    pp, sec, fc, partial = second_conv(j, pd, lo, hi, w2, dense4, samples)
-    hp = lax.psum(partial, "space")
-    preds, bh, gdo, bs = dense_layers(
-        j, hp, group_targets, dense_out.astype(F32).T, dense4, sec, own
+    halo = jnp.concatenate([before, after], axis=1).reshape(samples, 2 * c, cells)
+
+    f, xb, st = first_conv(xi, halo, w1, planes)
+    stats = gather_all(st, "space")
+    outer, edge = normalise_pool(f, stats, gs, local_count, total_count, True)
+    lo, hi = swap_edges(edge[0], edge[1], "space")
+    pds = [outer]
+    if planes > 4:
+        pds += normalise_pool(f, stats, gs, local_count, total_count, False)
+    pp, sec, fc, partial = second_conv(j, pds, lo, hi, w2, dense4, targets, samples)
+    hp = gather_all(partial, "space")
+    predictions, bh, gdo, bs = dense_layers(j, hp, dense_out.astype(F32).T, dense4, sec, own)
+    bs_lo, bs_hi = swap_edges(bs[0], bs[-1], "space")
+    message = second_grad(bs, pp, fc, bh, everyone)
+    received = swap(message, world)
+    bp = second_back(bs, bs_lo, bs_hi, v3)
+    own_sums = norm_sums(f, bp, stats, gs, local_count, total_count)
+    sums = gather_all(own_sums, "space")
+    totals, grad_dense_in = collect(received, spaces, fc.shape)
+    totals = swap(totals, world)
+    used = -(-conv_in.shape[1] // LANES) * conv_in.shape[0] + 16
+    rows = -(-used // everyone)
+    rows = (-(-rows // 8) * 8 if rows > 8 else rows) * everyone
+    local_in = first_grad(
+        f, bp, stats, gs, sums, own_sums, gdo, xb, c, local_count, total_count, rows
     )
-    everyone = groups * spaces
-    sent = fc.reshape((everyone, channels // everyone) + fc.shape[1:])
-    feats = lax.all_to_all(sent, ("dp", "space"), split_axis=0, concat_axis=0, tiled=True)
-    feats = feats.reshape((groups, spaces) + sent.shape[1:])
-    all_bh = lax.all_gather(bh, "dp")
-    bs_lo, bs_hi = swap_edges(bs[0], bs[-1], "space")
-    grad_conv_out = lax.psum(second_grad(bs, pp), ("dp", "space"))
-    bp = second_back(bs, bs_lo, bs_hi, w3)
-    sums = norm_sums(f, bp, stats, gs, local_count, total_count)
-    group_sums = lax.psum(sums, "space")
-    grad_dense_in = dense_grad(feats, all_bh).reshape(-1, units)
-    grad_conv_in = first_grad(f, bp, stats, gs, group_sums, xb, c, local_count, total_count)
-    grad_conv_in, sums, gdo = lax.psum((grad_conv_in, sums, gdo), ("dp", "space"))
-    first_row = lax.axis_index("space") * own
-    predictions = lax.dynamic_slice_in_dim(preds, first_row, own, axis=0)[:, : targets.shape[1]]
+    parts = swap(local_in.reshape(everyone, -1, LANES), world)
+    grad_conv_out = call(
+        finish_second_kernel,
+        jax.ShapeDtypeStruct(conv_out.shape, F32),
+        2.0,
+        name="finish_second",
+    )(totals.reshape(14, LANES, LANES))
+    sent = add_parts(parts)
+    totals = swap(sent, world)
+    grad_conv_in, grad_norm, grad_dense_out = call(
+        finish_first_kernel,
+        (
+            jax.ShapeDtypeStruct(conv_in.shape, F32),
+            jax.ShapeDtypeStruct((2, norm_gain.shape[0]), F32),
+            jax.ShapeDtypeStruct(dense_out.shape, F32),
+        ),
+        name="finish_first",
+    )(totals.reshape(rows, LANES))
     return (
         grad_conv_in,
-        sums[:, : norm_gain.shape[0]],
+        grad_norm,
         grad_conv_out,
-        grad_dense_in,
-        gdo.T,
+        grad_dense_in.reshape(-1, units),
+        grad_dense_out,
         predictions,
     )
 

time: 409 us -> 307 us (0.75)
  blocking collectives: 93.6 us -> 0 us
  starting transfers between devices: 20.4 us -> 51.8 us
  waiting for transfers between devices: 79.8 us -> 50.5 us
  Pallas kernels: 156 us -> 180 us
  local copies, waits for them, and re-layouts: 39.7 us -> 16.1 us
  between operations: 14.2 us -> 0.82 us
    psum x1 -> x0, waiting for transfers between devices: 74.1 us -> none  [shards(): lax.psum((grad_conv_in, sums, gdo), ('dp', 'space'))]
    psum x3 -> x0, blocking collectives: 58.9 us -> none  [the longest x1 39.5 us: shards(): lax.psum((grad_conv_in, sums, gdo), ('dp', 'space'))]
    all_to_all x1 -> x4, waiting for transfers between devices: 0.01 us -> 34.8 us  [swap(): return lax.all_to_all(parts, axes, split_axis=0, concat_axis=0, tiled=True)]
    all_gather x3 -> x0, blocking collectives: 34.7 us -> none  [the longest x1 13.7 us: shards(): stats = lax.all_gather(st, 'space')]
    pallas_call x5 -> x11, Pallas kernels: 53.8 us -> 84.4 us  [the longest x1 19.6 us: prepare(): call(lambda *refs: prepare_kernel(planes, samples, *refs), jax.ShapeDtype...]
    ppermute x0 -> x9, starting transfers between devices: none -> 19.7 us  [gather_all(): lax.ppermute(value, axis, [(i, (i + k) % count) for i in range(count)])]
    reshape x3 -> x0, local copies, waits for them, and re-layouts: 17.8 us -> none  [the longest x2 16.8 us: adjoint_weights(): return jnp.stack(parts, axis=4).reshape(48 * co, 4 * c)]
    all_to_all x1 -> x4, starting transfers between devices: 3.3 us -> 19.2 us  [swap(): return lax.all_to_all(parts, axes, split_axis=0, concat_axis=0, tiled=True)]
  transfers between devices with their start and end apart: 8 -> 19, of which waited for: 3 -> 12; matrix products, arithmetic and copies ran while one was open for 7% -> 2% of each run, Pallas kernels for 3% -> 15%
where the time goes in v2:
time: 307 us; the launch traced here: 305 us
  Pallas kernels  180 us (59%)
  starting transfers between devices  51.8 us (17%)
  waiting for transfers between devices  50.5 us (16%)
  local copies, waits for them, and re-layouts  16.1 us (5%)
  other arithmetic  6.14 us (2%)
    pallas_call x1, Pallas kernels, first_conv(): call(lambda *refs: first_kernel(planes, samples, refs), (jax.ShapeDtypeSt...  37.2 us
    all_to_all x4, waiting for transfers between devices, swap(): return lax.all_to_all(parts, axes, split_axis=0, concat_axis=0, tiled=True)  34.8 us
    pallas_call x1, Pallas kernels, first_grad(): call(lambda *refs: first_grad_kernel(local_count, total_count, c, *refs),...  33.4 us
    ppermute x9, starting transfers between devices, gather_all(): lax.ppermute(value, axis, [(i, (i + k) % count) for i in range(count)])  19.7 us
    pallas_call x1, Pallas kernels, prepare(): call(lambda *refs: prepare_kernel(planes, samples, *refs), jax.ShapeDtype...  19.6 us
    all_to_all x4, starting transfers between devices, swap(): return lax.all_to_all(parts, axes, split_axis=0, concat_axis=0, tiled=True)  19.2 us
    pallas_call x1, Pallas kernels, second_conv(): call(lambda *refs: second_kernel(samples, refs), (jax.ShapeDtypeStruct(pp...  17.3 us
    pallas_call x2, Pallas kernels, normalise_pool(): call(lambda *refs: pool_kernel(local_count, total_count, *refs), shapes,...  13.7 us
  transfers between devices with their start and end apart: 19, of which 12 were waited for; matrix products, arithmetic and copies ran while one was open for 2% of the time, Pallas kernels for 15%

profile of v2, /device:TPU:0, one launch (start us, length us, event | category | flops | bytes accessed | tf_op | source)
XLA Modules:
  0.0 305.0 jit_solution(14356559775480381694)
XLA Ops:
  0.6 5.4 %fusion = (bf16[8,32,1,1024]{3,2,1,0:T(2,128)(2,1)S(1)}, bf16[8,32,1,1024]{3,2,1,0:T(2,128)(2,1)S(1)}) fusion(bf16[8,32,8,1024]{3,2,1,0:T(8,128)(2,1)} %param.10), kind=kLoop, calls=%fused_computation.10 | loop fusion | bytes 2097152 | tf_op jit(solution)/shard_map/slice | solution.py:1041
  6.3 5.0 %collective-permute-start = (bf16[8,32,1,1024]{3,1,0,2:T(8,128)(2,1)S(1)}, bf16[8,32,1,1024]{3,1,0,2:T(8,128)(2,1)S(1)}, u32[]{:S(2)}, u32[]{:S(2)}) collective-permute-start(bf16[8,32,1,1024]{3,1,0,2:T(8,128)(2,1)S(1)} %copy.21), channel_id=1, source_target_pairs={{0,1},{1,2},{2,3},{4,5},{5,6},{6,7},{8,9},{9,10},{10,11},{12,13},{... | collective-permute-start | bytes 1572872 | tf_op jit(solution)/shard_map/ppermute | solution.py:1023
  12.8 19.6 %prepare.1.refs_0_ = bf16[5,9,34,16,128]{4,3,2,1,0:T(8,128)(2,1)} custom-call(bf16[8,256,1024]{2,1,0:T(8,128)(2,1)} %bitcast.33, bf16[256,384]{1,0:T(8,128)(2,1)} %constant.11.clone.refs_1_), custom_call_target="tpu_custom_call" | custom-call | flops 20000000000 | bytes 60000000 | tf_op jit(solution)/shard_map/prepare/pallas_call | solution.py:226
  34.1 3.4 %weights.1 = (bf16[1536,256]{1,0:T(8,128)(2,1)}, bf16[2304,256]{1,0:T(8,128)(2,1)}, bf16[3,3,4,128,128]{4,3,2,1,0:T(8,128)(2,1)}) custom-call(bf16[128,896]{1,0:T(8,128)(2,1)} %pad.8.refs_0_, bf16[128,1792]{1,0:T(8,128)(2,1)} %pad.9.refs_1_), custom_call_target="tpu_custom_call" | custom-call | flops 5000000000 | bytes 15000000 | tf_op jit(solution)/shard_map/weights/pallas_call | solution.py:136
  38.6 37.2 %first_conv.1 = (f32[4,8,32,16,256]{4,3,2,1,0:T(8,128)}, bf16[5,9,34,16,128]{4,3,2,1,0:T(8,128)(2,1)}, f32[2,128]{1,0:T(2,128)}) custom-call(bf16[5,9,34,16,128]{4,3,2,1,0:T(8,128)(2,1)} %prepare.1.refs_0_, bf16[8,64,1024]{2,1,0:T(8,128)(2,1)} %maximum_bitcast_fusion.refs_1_, bf16[64,128]{1,0:T(8,128)(2,1)} %constant.12.clone.refs_2_, ...), custom_call_target="tpu_custom_call" | custom-call | flops 24999999488 | bytes 75000000 | tf_op jit(solution)/shard_map/first_conv/pallas_call | solution.py:313
  75.8 2.6 collective-permute-start.2
  86.1 6.9 %pool_edges.1 = (bf16[2,8,16,16,128]{4,3,2,1,0:T(8,128)(2,1)}, bf16[2,4,16,16,128]{4,3,2,1,0:T(8,128)(2,1)}) custom-call(f32[4,8,32,16,256]{4,3,2,1,0:T(8,128)} %get-tuple-element.28.refs_0_, f32[4,2,128]{2,1,0:T(2,128)} %pad_maximum_fusion.1.refs_1_.refs_2_, f32[2,128]{1,0:T(2,128)} %maximum_maximum_fusion.refs_2_.refs_3_), custom_call_target="tpu_custom_call" | custom-call | flops 6000000000 | bytes 18000000 | tf_op jit(solution)/shard_map/pool_edges/pallas_call | solution.py:390
  97.4 6.8 %pool_inside.1.refs_2_ = bf16[2,8,16,16,128]{4,3,2,1,0:T(8,128)(2,1)} custom-call(f32[4,8,32,16,256]{4,3,2,1,0:T(8,128)} %get-tuple-element.28.refs_0_, f32[4,2,128]{2,1,0:T(2,128)} %pad_maximum_fusion.1.refs_1_.refs_2_, f32[2,128]{1,0:T(2,128)} %maximum_maximum_fusion.refs_2_.refs_3_), custom_call_target="tpu_custom_call" | custom-call | flops 6000000000 | bytes 18000000 | tf_op jit(solution)/shard_map/pool_inside/pallas_call | solution.py:390
  105.0 17.3 %second_conv.1 = (bf16[3,10,18,16,128]{4,3,2,1,0:T(8,128)(2,1)}, f32[2,8,16,16,256]{4,3,2,1,0:T(8,128)}, bf16[128,8,128]{2,1,0:T(8,128)(2,1)}, f32[16,128]{1,0:T(8,128)}) custom-call(s32[1]{0:T(128)} %bitcast.2.refs_0_, bf16[2,8,16,16,128]{4,3,2,1,0:T(8,128)(2,1)} %get-tuple-element.30.refs_1_, bf16[2,8,16,16,128]{4,3,2,1,0:T(8,128)(2,1)} %pool_inside.1.refs_2_, ...), custom_call_target="tpu_custom_call" | custom-call | flops 16999999488 | bytes 51000000 | tf_op jit(solution)/shard_map/second_conv/pallas_call | solution.py:522
  124.9 3.6 %collective-permute-start.8 = (f32[16,128]{1,0:T(8,128)}, f32[16,128]{1,0:T(8,128)S(1)}, u32[]{:S(2)}, u32[]{:S(2)}) collective-permute-start(f32[16,128]{1,0:T(8,128)} %get-tuple-element.33), channel_id=1, source_target_pairs={{0,2},{1,3},{2,0},{3,1},{4,6},{5,7},{6,4},{7,5},{8,10},{9,11},{10,... | collective-permute-start | bytes 24584 | tf_op jit(solution)/shard_map/ppermute | solution.py:993
  133.7 11.3 %dense_layers.1 = (f32[2,4]{1,0:T(2,128)}, bf16[8,128]{1,0:T(8,128)(2,1)}, f32[8,128]{1,0:T(8,128)}, bf16[4,8,16,16,128]{4,3,2,1,0:T(8,128)(2,1)}) custom-call(s32[1]{0:T(128)} %bitcast.2.refs_0_, f32[4,16,128]{2,1,0:T(8,128)} %pad_maximum_fusion.refs_1_, f32[4,128]{1,0:T(4,128)} %convert_bitcast_fusion.refs_2_, bf16[128,4,128,128]{3,2,1,0:T(8,128)(2,1)} %bitcast.52, ...), custom_call_target="tpu_custom_call" | custom-call | flops 11000000512 | bytes 33000000 | tf_op jit(solution)/shard_map/dense_layers/pallas_call | solution.py:626
  149.6 5.6 %collective-permute-done.10.lo_ref = bf16[8,16,16,128]{3,2,1,0:T(8,128)(2,1)S(1)} collective-permute-done((bf16[8,16,16,128]{3,2,1,0:T(8,128)(2,1)S(1)}, bf16[8,16,16,128]{3,2,1,0:T(8,128)(2,1)S(1)}, u32[]{:S(2)}, u32[]{:S(2)}) %collective-permute-start.10) | collective-permute-done | bytes 524320 | tf_op jit(solution)/shard_map/ppermute | solution.py:1023
  155.2 4.2 %collective-permute-done.11.hi_ref = bf16[8,16,16,128]{3,2,1,0:T(8,128)(2,1)S(1)} collective-permute-done((bf16[8,16,16,128]{3,2,1,0:T(8,128)(2,1)S(1)}, bf16[8,16,16,128]{3,2,1,0:T(8,128)(2,1)S(1)}, u32[]{:S(2)}, u32[]{:S(2)}) %collective-permute-start.11) | collective-permute-done | bytes 524320 | tf_op jit(solution)/shard_map/ppermute | solution.py:1024
  160.2 11.8 %second_back.1.refs_1_ = bf16[4,8,16,16,128]{4,3,2,1,0:T(8,128)(2,1)} custom-call(bf16[4,8,16,16,128]{4,3,2,1,0:T(8,128)(2,1)} %get-tuple-element.35.bs_ref, bf16[8,16,16,128]{3,2,1,0:T(8,128)(2,1)} %copy-done.9, bf16[8,16,16,128]{3,2,1,0:T(8,128)(2,1)} %copy-done.10, bf16[3,3,4,128,128]{4,3,2,1,0:T(8,128)(2,1)} %get-tuple-element.36.w_ref), custom_call_target="tpu_custom_call" | custom-call | flops 12000000000 | bytes 36000000 | tf_op jit(solution)/shard_map/second_back/pallas_call | solution.py:837
  171.9 13.3 %norm_sums.1.refs_5_ = f32[2,128]{1,0:T(2,128)} custom-call(f32[4,8,32,16,256]{4,3,2,1,0:T(8,128)} %get-tuple-element.28.refs_0_, bf16[4,8,16,16,128]{4,3,2,1,0:T(8,128)(2,1)} %second_back.1.refs_1_, f32[4,2,128]{2,1,0:T(2,128)} %pad_maximum_fusion.1.refs_1_.refs_2_, f32[2,128]{1,0:T(2,128)} %maximum_maximum_fusion.refs_2_.refs_3_), custom_call_target="tpu_custom_call" | custom-call | flops 12999999488 | bytes 39000000 | tf_op jit(solution)/shard_map/norm_sums/pallas_call | solution.py:881
  188.4 2.9 collective-permute-start.14
  194.1 33.4 %first_grad.1 = f32[512,128]{1,0:T(8,128)} custom-call(f32[4,8,32,16,256]{4,3,2,1,0:T(8,128)} %get-tuple-element.28.refs_0_, bf16[4,8,16,16,128]{4,3,2,1,0:T(8,128)(2,1)} %second_back.1.refs_1_, f32[4,2,128]{2,1,0:T(2,128)} %pad_maximum_fusion.1.refs_1_.refs_2_, f32[2,128]{1,0:T(2,128)} %maximum_maximum_fusion.refs_2_.refs_3_, ...), custom_call_target="tpu_custom_call" | custom-call | flops 32999999488 | bytes 99000000 | tf_op jit(solution)/shard_map/first_grad/pallas_call | solution.py:955
  227.6 6.5 %all-to-all-start = ((f32[32,16,128]{2,1,0:T(8,128)}), f32[32,16,128]{2,1,0:T(8,128)S(1)}, u32[]{:S(2)}, u32[]{:S(2)}) async-start(f32[32,16,128]{2,1,0:T(8,128)} %bitcast.35), calls=%async_computation | async-start | bytes 524288 | tf_op jit(solution)/shard_map/all_to_all | solution.py:1000
  234.1 10.8 %second_grad.1 = bf16[32,104,128]{2,1,0:T(8,128)(2,1)} custom-call(bf16[4,8,16,16,128]{4,3,2,1,0:T(8,128)(2,1)} %get-tuple-element.35.bs_ref, bf16[3,10,18,16,128]{4,3,2,1,0:T(8,128)(2,1)} %get-tuple-element.41.pp_ref, bf16[128,8,128]{2,1,0:T(8,128)(2,1)} %get-tuple-element.42.fc_ref, bf16[8,128]{1,0:T(8,128)(2,1)} %get-tuple-element.43.bh_ref), custom_call_target="tpu_custom_call" | custom-call | flops 12000000000 | bytes 36000000 | tf_op jit(solution)/shard_map/second_grad/pallas_call | solution.py:747
  244.8 5.7 %all-to-all-start.2 = ((bf16[32,104,128]{2,1,0:T(8,128)(2,1)}), bf16[32,104,128]{2,1,0:T(8,128)(2,1)S(1)}, u32[]{:S(2)}, u32[]{:S(2)}) async-start(bf16[32,104,128]{2,1,0:T(8,128)(2,1)} %second_grad.1), calls=%async_computation.2 | async-start | bytes 1703936 | tf_op jit(solution)/shard_map/all_to_all | solution.py:1000
  252.2 19.2 %all-to-all-done.2.refs_0_ = bf16[32,104,128]{2,1,0:T(8,128)(2,1)S(1)} async-done(((bf16[32,104,128]{2,1,0:T(8,128)(2,1)}), bf16[32,104,128]{2,1,0:T(8,128)(2,1)S(1)}, u32[]{:S(2)}, u32[]{:S(2)}) %all-to-all-start.2) | async-done | bytes 852000 | tf_op jit(solution)/shard_map/all_to_all | solution.py:1000
  271.3 4.5 %all-to-all-start.1 = ((bf16[32,16,128]{2,1,0:T(8,128)(2,1)}), bf16[32,16,128]{2,1,0:T(8,128)(2,1)S(1)}, u32[]{:S(2)}, u32[]{:S(2)}) async-start(bf16[32,16,128]{2,1,0:T(8,128)(2,1)} %add_parts.1), calls=%async_computation.1 | async-start | bytes 262144 | tf_op jit(solution)/shard_map/all_to_all | solution.py:1000
  278.4 5.8 %all-to-all-done.1 = bf16[32,16,128]{2,1,0:T(8,128)(2,1)S(1)} async-done(((bf16[32,16,128]{2,1,0:T(8,128)(2,1)}), bf16[32,16,128]{2,1,0:T(8,128)(2,1)S(1)}, u32[]{:S(2)}, u32[]{:S(2)}) %all-to-all-start.1) | async-done | bytes 131104 | tf_op jit(solution)/shard_map/all_to_all | solution.py:1000
  290.0 9.8 %all-to-all-done.3 = bf16[32,56,128]{2,1,0:T(8,128)(2,1)S(1)} async-done(((bf16[32,56,128]{2,1,0:T(8,128)(2,1)}), bf16[32,56,128]{2,1,0:T(8,128)(2,1)S(1)}, u32[]{:S(2)}, u32[]{:S(2)}) %all-to-all-start.3) | async-done | bytes 458784 | tf_op jit(solution)/shard_map/all_to_all | solution.py:1000
  (71 shorter events, 51.6 us)
Async XLA Ops:
  6.3 31.2 %collective-permute-start = (bf16[8,32,1,1024]{3,1,0,2:T(8,128)(2,1)S(1)}, bf16[8,32,1,1024]{3,1,0,2:T(8,128)(2,1)S(1)}, u32[]{:S(2)}, u32[]{:S(2)}) collective-permute-start(bf16[8,32,1,1024]{3,1,0,2:T(8,128)(2,1)S(1)} %copy.21), channel_id=1, source_target_pairs={{0,1},{1,2},{2,3},{4,5},{5,6},{6,7},{8,9},{9,10},{10,11},{12,13},{... | collective-permute-start | bytes 1572872 | tf_op jit(solution)/shard_map/ppermute | solution.py:1023
  11.4 26.1 %collective-permute-start.1 = (bf16[8,32,1,1024]{3,1,0,2:T(8,128)(2,1)S(1)}, bf16[8,32,1,1024]{3,1,0,2:T(8,128)(2,1)S(1)}, u32[]{:S(2)}, u32[]{:S(2)}) collective-permute-start(bf16[8,32,1,1024]{3,1,0,2:T(8,128)(2,1)S(1)} %copy.22), channel_id=1, source_target_pairs={{1,0},{2,1},{3,2},{5,4},{6,5},{7,6},{9,8},{10,9},{11,10},{13,12},{... | collective-permute-start | bytes 1572872 | tf_op jit(solution)/shard_map/ppermute | solution.py:1024
  12.7 19.6 %copy-start.2 = (bf16[128,1728]{0,1:T(8,128)(2,1)S(1)}, bf16[128,1728]{0,1:T(8,128)(2,1)}, u32[]{:S(2)}) copy-start(bf16[128,1728]{0,1:T(8,128)(2,1)} %param.14) | copy-start | bytes 1327108
  12.7 20.6 %copy-start.5 = (bf16[64,864]{1,0:T(8,128)(2,1)S(1)}, bf16[64,864]{1,0:T(8,128)(2,1)}, u32[]{:S(2)}) copy-start(bf16[64,864]{1,0:T(8,128)(2,1)} %param.11) | copy-start | bytes 331780
  38.6 43.8 %copy-start.7 = (f32[64]{0:T(128)S(1)}, f32[64]{0:T(128)}, u32[]{:S(2)}) copy-start(f32[64]{0:T(128)} %param.13) | copy-start | bytes 772
  38.6 43.8 %copy-start.8 = (f32[64]{0:T(128)S(1)}, f32[64]{0:T(128)}, u32[]{:S(2)}) copy-start(f32[64]{0:T(128)} %param.12) | copy-start | bytes 772
  75.8 7.2 %collective-permute-start.2 = (f32[2,128]{1,0:T(2,128)}, f32[2,128]{1,0:T(2,128)S(1)}, u32[]{:S(2)}, u32[]{:S(2)}) collective-permute-start(f32[2,128]{1,0:T(2,128)} %get-tuple-element.29), channel_id=1, source_target_pairs={{0,1},{1,2},{2,3},{3,0},{4,5},{5,6},{6,7},{7,4},{8,9},{9,10},{10,1... | collective-permute-start | bytes 3080 | tf_op jit(solution)/shard_map/ppermute | solution.py:993
  78.4 4.7 %collective-permute-start.3 = (f32[2,128]{1,0:T(2,128)}, f32[2,128]{1,0:T(2,128)S(1)}, u32[]{:S(2)}, u32[]{:S(2)}) collective-permute-start(f32[2,128]{1,0:T(2,128)} %get-tuple-element.29), channel_id=1, source_target_pairs={{0,2},{1,3},{2,0},{3,1},{4,6},{5,7},{6,4},{7,5},{8,10},{9,11},{10,... | collective-permute-start | bytes 3080 | tf_op jit(solution)/shard_map/ppermute | solution.py:993
  81.0 3.8 %collective-permute-start.4 = (f32[2,128]{1,0:T(2,128)}, f32[2,128]{1,0:T(2,128)S(1)}, u32[]{:S(2)}, u32[]{:S(2)}) collective-permute-start(f32[2,128]{1,0:T(2,128)} %get-tuple-element.29), channel_id=1, source_target_pairs={{0,3},{1,0},{2,1},{3,2},{4,7},{5,4},{6,5},{7,6},{8,11},{9,8},{10,9... | collective-permute-start | bytes 3080 | tf_op jit(solution)/shard_map/ppermute | solution.py:993
  94.1 10.1 %collective-permute-start.5 = (bf16[4,16,16,128]{3,2,1,0:T(8,128)(2,1)S(1)}, bf16[4,16,16,128]{3,2,1,0:T(8,128)(2,1)S(1)}, u32[]{:S(2)}, u32[]{:S(2)}) collective-permute-start(bf16[4,16,16,128]{3,2,1,0:T(8,128)(2,1)S(1)} %get-tuple-element.59), channel_id=1, source_target_pairs={{0,1},{1,2},{2,3},{4,5},{5,6},{6,7},{8,9},{9,10},{10,11},{12,13},{... | collective-permute-start | bytes 786440 | tf_op jit(solution)/shard_map/ppermute | solution.py:1023
  96.1 8.3 %collective-permute-start.6 = (bf16[4,16,16,128]{3,2,1,0:T(8,128)(2,1)S(1)}, bf16[4,16,16,128]{3,2,1,0:T(8,128)(2,1)S(1)}, u32[]{:S(2)}, u32[]{:S(2)}) collective-permute-start(bf16[4,16,16,128]{3,2,1,0:T(8,128)(2,1)S(1)} %get-tuple-element.58), channel_id=1, source_target_pairs={{1,0},{2,1},{3,2},{5,4},{6,5},{7,6},{9,8},{10,9},{11,10},{13,12},{... | collective-permute-start | bytes 786440 | tf_op jit(solution)/shard_map/ppermute | solution.py:1024
  105.0 24.4 %copy-start.6 = (bf16[128,4]{0,1:T(4,128)(2,1)S(1)}, bf16[128,4]{0,1:T(4,128)(2,1)}, u32[]{:S(2)}) copy-start(bf16[128,4]{0,1:T(4,128)(2,1)} %param.16) | copy-start | bytes 3076
  122.4 7.6 %collective-permute-start.7 = (f32[16,128]{1,0:T(8,128)}, f32[16,128]{1,0:T(8,128)S(1)}, u32[]{:S(2)}, u32[]{:S(2)}) collective-permute-start(f32[16,128]{1,0:T(8,128)} %get-tuple-element.33), channel_id=1, source_target_pairs={{0,1},{1,2},{2,3},{3,0},{4,5},{5,6},{6,7},{7,4},{8,9},{9,10},{10,1... | collective-permute-start | bytes 24584 | tf_op jit(solution)/shard_map/ppermute | solution.py:993
  124.9 5.5 %collective-permute-start.8 = (f32[16,128]{1,0:T(8,128)}, f32[16,128]{1,0:T(8,128)S(1)}, u32[]{:S(2)}, u32[]{:S(2)}) collective-permute-start(f32[16,128]{1,0:T(8,128)} %get-tuple-element.33), channel_id=1, source_target_pairs={{0,2},{1,3},{2,0},{3,1},{4,6},{5,7},{6,4},{7,5},{8,10},{9,11},{10,... | collective-permute-start | bytes 24584 | tf_op jit(solution)/shard_map/ppermute | solution.py:993
  128.5 3.9 %collective-permute-start.9 = (f32[16,128]{1,0:T(8,128)}, f32[16,128]{1,0:T(8,128)S(1)}, u32[]{:S(2)}, u32[]{:S(2)}) collective-permute-start(f32[16,128]{1,0:T(8,128)} %get-tuple-element.33), channel_id=1, source_target_pairs={{0,3},{1,0},{2,1},{3,2},{4,7},{5,4},{6,5},{7,6},{8,11},{9,8},{10,9... | collective-permute-start | bytes 24584 | tf_op jit(solution)/shard_map/ppermute | solution.py:993
  146.3 8.9 %collective-permute-start.10 = (bf16[8,16,16,128]{3,2,1,0:T(8,128)(2,1)S(1)}, bf16[8,16,16,128]{3,2,1,0:T(8,128)(2,1)S(1)}, u32[]{:S(2)}, u32[]{:S(2)}) collective-permute-start(bf16[8,16,16,128]{3,2,1,0:T(8,128)(2,1)S(1)} %get-tuple-element.57), channel_id=1, source_target_pairs={{0,1},{1,2},{2,3},{4,5},{5,6},{6,7},{8,9},{9,10},{10,11},{12,13},{... | collective-permute-start | bytes 1572872 | tf_op jit(solution)/shard_map/ppermute | solution.py:1023
  148.3 11.1 %collective-permute-start.11 = (bf16[8,16,16,128]{3,2,1,0:T(8,128)(2,1)S(1)}, bf16[8,16,16,128]{3,2,1,0:T(8,128)(2,1)S(1)}, u32[]{:S(2)}, u32[]{:S(2)}) collective-permute-start(bf16[8,16,16,128]{3,2,1,0:T(8,128)(2,1)S(1)} %get-tuple-element.56), channel_id=1, source_target_pairs={{1,0},{2,1},{3,2},{5,4},{6,5},{7,6},{9,8},{10,9},{11,10},{13,12},{... | collective-permute-start | bytes 1572872 | tf_op jit(solution)/shard_map/ppermute | solution.py:1024
  185.2 6.1 %collective-permute-start.12 = (f32[2,128]{1,0:T(2,128)}, f32[2,128]{1,0:T(2,128)S(1)}, u32[]{:S(2)}, u32[]{:S(2)}) collective-permute-start(f32[2,128]{1,0:T(2,128)} %norm_sums.1.refs_5_), channel_id=1, source_target_pairs={{0,1},{1,2},{2,3},{3,0},{4,5},{5,6},{6,7},{7,4},{8,9},{9,10},{10,1... | collective-permute-start | bytes 3080 | tf_op jit(solution)/shard_map/ppermute | solution.py:993
  187.2 4.7 %collective-permute-start.13 = (f32[2,128]{1,0:T(2,128)}, f32[2,128]{1,0:T(2,128)S(1)}, u32[]{:S(2)}, u32[]{:S(2)}) collective-permute-start(f32[2,128]{1,0:T(2,128)} %norm_sums.1.refs_5_), channel_id=1, source_target_pairs={{0,2},{1,3},{2,0},{3,1},{4,6},{5,7},{6,4},{7,5},{8,10},{9,11},{10,... | collective-permute-start | bytes 3080 | tf_op jit(solution)/shard_map/ppermute | solution.py:993
  188.4 4.4 %collective-permute-start.14 = (f32[2,128]{1,0:T(2,128)}, f32[2,128]{1,0:T(2,128)S(1)}, u32[]{:S(2)}, u32[]{:S(2)}) collective-permute-start(f32[2,128]{1,0:T(2,128)} %norm_sums.1.refs_5_), channel_id=1, source_target_pairs={{0,3},{1,0},{2,1},{3,2},{4,7},{5,4},{6,5},{7,6},{8,11},{9,8},{10,9... | collective-permute-start | bytes 3080 | tf_op jit(solution)/shard_map/ppermute | solution.py:993
  227.6 17.3 %all-to-all-start = ((f32[32,16,128]{2,1,0:T(8,128)}), f32[32,16,128]{2,1,0:T(8,128)S(1)}, u32[]{:S(2)}, u32[]{:S(2)}) async-start(f32[32,16,128]{2,1,0:T(8,128)} %bitcast.35), calls=%async_computation | async-start | bytes 524288 | tf_op jit(solution)/shard_map/all_to_all | solution.py:1000
  244.8 26.5 %all-to-all-start.2 = ((bf16[32,104,128]{2,1,0:T(8,128)(2,1)}), bf16[32,104,128]{2,1,0:T(8,128)(2,1)S(1)}, u32[]{:S(2)}, u32[]{:S(2)}) async-start(bf16[32,104,128]{2,1,0:T(8,128)(2,1)} %second_grad.1), calls=%async_computation.2 | async-start | bytes 1703936 | tf_op jit(solution)/shard_map/all_to_all | solution.py:1000
  271.3 12.9 %all-to-all-start.1 = ((bf16[32,16,128]{2,1,0:T(8,128)(2,1)}), bf16[32,16,128]{2,1,0:T(8,128)(2,1)S(1)}, u32[]{:S(2)}, u32[]{:S(2)}) async-start(bf16[32,16,128]{2,1,0:T(8,128)(2,1)} %add_parts.1), calls=%async_computation.1 | async-start | bytes 262144 | tf_op jit(solution)/shard_map/all_to_all | solution.py:1000
  284.2 15.6 %all-to-all-start.3 = ((bf16[32,56,128]{2,1,0:T(8,128)(2,1)}), bf16[32,56,128]{2,1,0:T(8,128)(2,1)S(1)}, u32[]{:S(2)}, u32[]{:S(2)}) async-start(bf16[32,56,128]{2,1,0:T(8,128)(2,1)} %get-tuple-element.44), calls=%async_computation.3 | async-start | bytes 917504 | tf_op jit(solution)/shard_map/all_to_all | solution.py:1000
  (8 other events, 20.0 us)

commit v3 on v2

--- a/solution.py
+++ b/solution.py
@@ -64,16 +64,16 @@
     return pl.BlockSpec(shape, lambda *_: (0,) * len(shape), pipeline_mode=pl.Buffered(1))
 
 
-def weights_kernel(c_in, c_mid, ci_ref, co_ref, w1_ref, w2_ref, v3_ref, t1, t2):
-    def offset(a, b, d):
-        return (a * 3 + b) * 3 + d
-
-    for k in range(ci_ref.shape[1] // LANES):
+def offset(a, b, d):
+    return (a * 3 + b) * 3 + d
+
+
+def first_weights_kernel(c_in, ci_ref, w1_ref, t0, t1):
+    t0[...] = jnp.zeros_like(t0)
+    t0[0 : ci_ref.shape[0], 0 : ci_ref.shape[1]] = ci_ref[...].astype(F32)
+    for k in range(t0.shape[1] // LANES):
         lanes = slice(k * LANES, (k + 1) * LANES)
-        t1[lanes, :] = both_halves(ci_ref[:, lanes].astype(F32).T)
-    for k in range(co_ref.shape[1] // LANES):
-        lanes = slice(k * LANES, (k + 1) * LANES)
-        t2[lanes, :] = co_ref[:, lanes].astype(F32).T
+        t1[lanes, :] = both_halves(t0[:, lanes].T)
     mask = low_half((c_in, LANES))
     zero = jnp.zeros((c_in, LANES), F32)
     row = 0
@@ -96,6 +96,15 @@
                                 mask, parts[0], parts[1]
                             ).astype(BF16)
                         row += c_in
+
+
+def second_weights_kernel(c_mid, co_ref, w2_ref, v3_ref, t0, t2):
+    columns = co_ref.shape[0]
+    t2[0:columns] = co_ref[...].astype(F32)
+    t2[columns:] = jnp.zeros((t2.shape[0] - columns, LANES), F32)
+    for k in range(t0.shape[1] // LANES):
+        lanes = slice(k * LANES, (k + 1) * LANES)
+        t0[:, lanes] = t2[lanes, :].T
     row = 0
     for b in range(3):
         for d in range(3):
@@ -119,31 +128,38 @@
                     b = yw - py
                     if 0 <= b <= 2:
                         o = offset(2 - a, 2 - b, 2 - d)
-                        v = co_ref[:, o // 2 * LANES : (o // 2 + 1) * LANES].astype(F32)
+                        v = t0[:, o // 2 * LANES : (o // 2 + 1) * LANES]
                         parts.append(v if o % 2 == py else roll_half(v))
                     else:
                         parts.append(zero)
                 v3_ref[d, a, yw] = jnp.where(mask, parts[0], parts[1]).astype(BF16)
 
 
-def make_weights(conv_in, conv_out):
+def first_weights(conv_in):
     c_in = conv_in.shape[1] // 27
+    width = -(-conv_in.shape[1] // LANES) * LANES
+    return call(
+        lambda *refs: first_weights_kernel(c_in, *refs),
+        jax.ShapeDtypeStruct((48 * c_in, 2 * LANES), BF16),
+        2.0,
+        scratch_shapes=[pltpu.VMEM((LANES, width), F32), pltpu.VMEM((width, LANES), F32)],
+        name="first_weights",
+    )(conv_in)
+
+
+def second_weights(conv_out):
     c_mid = conv_out.shape[1] // 27
-    wide_in = -(-conv_in.shape[1] // LANES) * LANES
-    wide_out = -(-conv_out.shape[1] // LANES) * LANES
-    ci = jnp.pad(conv_in, ((0, LANES - conv_in.shape[0]), (0, wide_in - conv_in.shape[1])))
-    co = jnp.pad(conv_out, ((0, 0), (0, wide_out - conv_out.shape[1])))
+    width = -(-conv_out.shape[1] // LANES) * LANES
     return call(
-        lambda *refs: weights_kernel(c_in, c_mid, *refs),
+        lambda *refs: second_weights_kernel(c_mid, *refs),
         (
-            jax.ShapeDtypeStruct((48 * c_in, 2 * LANES), BF16),
             jax.ShapeDtypeStruct((36 * c_mid, 2 * LANES), BF16),
             jax.ShapeDtypeStruct((3, 3, 4, LANES, LANES), BF16),
         ),
-        5.0,
-        scratch_shapes=[pltpu.VMEM((wide_in, LANES), F32), pltpu.VMEM((wide_out, LANES), F32)],
-        name="weights",
-    )(ci, co)
+        3.0,
+        scratch_shapes=[pltpu.VMEM((LANES, width), F32), pltpu.VMEM((width, LANES), F32)],
+        name="second_weights",
+    )(conv_out.T)
 
 
 def half_pads(before, after):
@@ -154,126 +170,225 @@
     )
 
 
-def gather_rows(src_ref, sel_ref, z_ref, samples):
+def split_sample(read, sel_ref, ub_ref, s, samples):
     half_y = GRID // HALVES
-    chunks = z_ref.shape[0]
+    last = half_y // 2
+    width = ub_ref.shape[3]
+    half = LANES // 2
+    per_group = LANES // GRID
+
+    def put(h, m, part, value):
+        for k in range(width // LANES):
+            at = k * LANES + part * half
+            ub_ref[h * samples + s, m, :, at : at + half] = value[:, at : at + half]
+
+    for g in range(GRID * GRID // LANES):
+        val = dot_rows(read(slice(g * LANES, (g + 1) * LANES)), sel_ref[...]).astype(BF16)
+        for r in range(per_group):
+            y = g * per_group + r
+            h, local = y // half_y, y % half_y
+            v = val[r * GRID : (r + 1) * GRID]
+            if y % 2:
+                put(h, (local + 1) // 2, 0, v)
+                if local == half_y - 1 and h + 1 < HALVES:
+                    put(h + 1, 0, 0, v)
+            else:
+                put(h, local // 2, 1, v)
+                if local == 0 and h > 0:
+                    put(h - 1, last, 1, v)
+    zero = jnp.zeros((GRID, width), BF16)
+    put(0, 0, 0, zero)
+    put(HALVES - 1, last, 1, zero)
+
+
+def weave(ub_ref, perm_ref, m, part):
+    slots = ub_ref.shape[0]
+    rows = jnp.concatenate(
+        [ub_ref[t, m, part * slots : (part + 1) * slots, :] for t in range(slots)], axis=0
+    )
+    return dot(perm_ref[...], rows).astype(BF16)
+
+
+def weave_matrix(slots):
+    perm = np.zeros((slots * slots, slots * slots), np.float32)
+    for z in range(slots):
+        for t in range(slots):
+            perm[z * slots + t, t * slots + z] = 1.0
+    return jnp.asarray(perm, BF16)
+
+
+def prepare_kernel(steps, x_ref, pa_ref, perm_ref, xb_ref, ub_ref):
+    i = pl.program_id(0)
+    batch = x_ref.shape[0]
+    samples = batch * steps
     inner = HALVES * samples
-    groups = GRID * GRID // LANES
-    per_group = LANES // GRID
-
-    def gather(t, carry):
-        s = t % samples
-        q = t // samples
-        for h in range(HALVES):
-            g = q + h * (groups // HALVES)
-            lanes = pl.ds(pl.multiple_of(g * LANES, LANES), LANES)
-            val = dot_rows(src_ref[s, :, lanes], sel_ref[...])
-            start = (per_group * q + 1) * GRID * inner + h * samples + s
-            for k in range(chunks):
-                z_ref[k, pl.ds(start, LANES, stride=inner), :] = val[:, k * LANES : (k + 1) * LANES]
-        return carry
-
-    lax.fori_loop(0, samples * groups // HALVES, gather, 0)
-    row = GRID * inner
-    for k in range(chunks):
-        last = plane_of(z_ref, k, half_y, row).reshape(GRID, inner, LANES)
-        head = plane_of(z_ref, k, 1, row).reshape(GRID, inner, LANES)
-        lo, hi = half_pads(last, head)
-        z_ref[k, 0:row, :] = lo.reshape(row, LANES)
-        z_ref[k, (half_y + 1) * row : (half_y + 2) * row, :] = hi.reshape(row, LANES)
-
-
-def plane_of(z_ref, k, y, row):
-    return z_ref[k, pl.ds(pl.multiple_of(y * row, row), row), :]
-
-
-def prepare_kernel(planes, samples, x_ref, pa_ref, xb_ref, z_ref):
-    pairs = planes // 2 + 1
-    half_y = GRID // HALVES
-    inner = HALVES * samples
-    row = GRID * inner
-    gather_rows(x_ref, pa_ref, z_ref, samples)
-
-    def assemble(m, carry):
-        mask = low_half((row, LANES))
-        for k in range(pairs):
-            a = plane_of(z_ref, k // 2, 2 * m, row)
-            b = plane_of(z_ref, k // 2, 2 * m + 1, row)
-            if k % 2 == 0:
-                b = roll_half(b)
-            else:
-                a = roll_half(a)
-            both = jnp.where(mask, a, b).astype(BF16)
-            xb_ref[k, m, 1 : GRID + 1] = both.reshape(GRID, inner, LANES)
-            zero = jnp.zeros((inner, LANES), BF16)
-            xb_ref[k, m, 0] = zero
-            xb_ref[k, m, GRID + 1] = zero
-        return carry
-
-    lax.fori_loop(0, half_y // 2 + 1, assemble, 0)
+    per_step = xb_ref.shape[1]
+
+    @pl.when(i < steps)
+    def _():
+        def split(t, carry):
+            split_sample(
+                lambda lanes: x_ref[t, :, lanes], pa_ref, ub_ref, i * batch + t, samples
+            )
+            return carry
+
+        lax.fori_loop(0, batch, split, 0)
+
+    @pl.when(i >= steps)
+    def _():
+        zero = jnp.zeros((inner, LANES), BF16)
+
+        def join(t, carry):
+            m = (i - steps) * per_step + t
+            for part in range(GRID // inner):
+                out = weave(ub_ref, perm_ref, m, part)
+                for k in range(xb_ref.shape[0]):
+                    at = 1 + part * inner
+                    xb_ref[k, t, at : at + inner] = out[:, k * LANES : (k + 1) * LANES].reshape(
+                        inner, inner, LANES
+                    )
+            for k in range(xb_ref.shape[0]):
+                xb_ref[k, t, 0] = zero
+                xb_ref[k, t, GRID + 1] = zero
+            return carry
+
+        lax.fori_loop(0, per_step, join, 0)
 
 
 def prepare(x, planes, c):
     samples = x.shape[0]
     pairs = planes // 2 + 1
-    chunks = -(-pairs * 2 * c // LANES)
     inner = HALVES * samples
-    half_y = GRID // HALVES
-    pa = np.zeros((c * planes, chunks * LANES), np.float32)
+    ms = GRID // HALVES // 2 + 1
+    batch, per_step = samples // 4, ms // 3
+    pa = np.zeros((c * planes, pairs * LANES), np.float32)
     for ch in range(c):
-        for p in range(planes):
-            pa[ch * planes + p, (p + 1) * c + ch] = 1.0
+        for k in range(pairs):
+            for yo in range(2):
+                for xo in range(2):
+                    p = 2 * k - 1 + xo
+                    if 0 <= p < planes:
+                        pa[ch * planes + p, k * LANES + yo * 2 * c + xo * c + ch] = 1.0
+    pa = jnp.asarray(pa, BF16)
+    perm = weave_matrix(inner)
+    block = (pairs, per_step, GRID + 2, inner, LANES)
     return call(
-        lambda *refs: prepare_kernel(planes, samples, *refs),
-        jax.ShapeDtypeStruct((pairs, half_y // 2 + 1, GRID + 2, inner, LANES), BF16),
-        20.0,
-        scratch_shapes=[pltpu.VMEM((chunks, (half_y + 2) * GRID * inner, LANES), F32)],
+        lambda *refs: prepare_kernel(4, *refs),
+        jax.ShapeDtypeStruct((pairs, ms, GRID + 2, inner, LANES), BF16),
+        11.0,
+        grid=(4 + 3,),
+        in_specs=[
+            pl.BlockSpec((batch,) + x.shape[1:], lambda i: (jnp.minimum(i, 3), 0, 0)),
+            whole_spec(pa.shape),
+            whole_spec(perm.shape),
+        ],
+        out_specs=pl.BlockSpec(block, lambda i: (0, jnp.maximum(i - 4, 0), 0, 0, 0)),
+        scratch_shapes=[pltpu.VMEM((inner, ms, GRID, pairs * LANES), BF16)],
         name="prepare",
-    )(x, jnp.asarray(pa, BF16))
+    )(x, pa, perm)
+
+
+def edge_kernel(x_ref, sel_ref, lo_ref, hi_ref):
+    c = lo_ref.shape[1]
+    for t in range(x_ref.shape[0]):
+        out = dot(sel_ref[...], x_ref[t]).astype(BF16)
+        lo_ref[t] = out[0:c]
+        hi_ref[t] = out[c:]
+
+
+def edge_planes(x, planes, c):
+    samples, rows, cells = x.shape
+    sel = np.zeros((2 * c, rows), np.float32)
+    for ch in range(c):
+        sel[ch, ch * planes] = 1.0
+        sel[c + ch, ch * planes + planes - 1] = 1.0
+    sel = jnp.asarray(sel, BF16)
+    out = jax.ShapeDtypeStruct((samples, c, cells), BF16)
+    batch = samples // 2
+    spec = pl.BlockSpec((batch, c, cells), lambda i: (i, 0, 0))
+    return call(
+        edge_kernel,
+        (out, out),
+        2.5,
+        grid=(2,),
+        in_specs=[pl.BlockSpec((batch, rows, cells), lambda i: (i, 0, 0)), whole_spec(sel.shape)],
+        out_specs=(spec, spec),
+        name="edge_planes",
+    )(x, sel)
 
 
 def first_kernel(planes, samples, refs):
-    (xi_ref, halo_ref, pb_ref, w_ref, f_ref, xb_ref, st_ref, z_ref, w_acc) = refs
+    (xa_ref, xc_ref, lo_ref, hi_ref, pb_ref, perm_ref, w_ref,
+     f_ref, xe_ref, st_ref, cur, ub, eb, w_acc) = refs
     i = pl.program_id(0)
-    pairs = planes // 2 + 1
     half_y = GRID // HALVES
     inner = HALVES * samples
     rows = GRID * inner
     blocks = half_y // 2
     per_block = rows // 8
+    end = pl.num_programs(0) - 1
 
     @pl.when(i == 0)
     def _():
-        gather_rows(halo_ref, pb_ref, z_ref, samples)
-
-        def patch(m, carry):
+        def split(s, carry):
+            split_sample(
+                lambda lanes: jnp.concatenate([lo_ref[s, :, lanes], hi_ref[s, :, lanes]], axis=0),
+                pb_ref, ub, s, samples,
+            )
+            return carry
+
+        lax.fori_loop(0, samples, split, 0)
+
+        def join(m, carry):
+            for part in range(GRID // inner):
+                at = part * inner
+                eb[m, at : at + inner] = weave(ub, perm_ref, m, part).reshape(inner, inner, LANES)
+            return carry
+
+        lax.fori_loop(0, blocks + 1, join, 0)
+        w_acc[...] = jnp.zeros_like(w_acc)
+
+    def patched(k, x_ref):
+        def body(m, carry):
             lane = lax.broadcasted_iota(jnp.int32, (rows, LANES), 1)
-            a = plane_of(z_ref, 0, 2 * m, rows)
-            b = plane_of(z_ref, 0, 2 * m + 1, rows)
-            edge = jnp.where(lane < LANES // 2, a, b)
-            first = lane % (LANES // 2) < LANES // 4
-            for k in range(pairs):
-                xb_ref[k, m] = xi_ref[k, m]
-            for k in (0, pairs - 1):
-                own = xi_ref[k, m, 1 : GRID + 1].astype(F32).reshape(rows, LANES)
-                both = jnp.where(first, edge, own) if k == 0 else jnp.where(first, own, edge)
-                xb_ref[k, m, 1 : GRID + 1] = both.astype(BF16).reshape(GRID, inner, LANES)
+            halo = (lane % (LANES // 2) < LANES // 4) == (k == 0)
+            own = x_ref[0, m, 1 : GRID + 1].astype(F32).reshape(rows, LANES)
+            edge = eb[m].astype(F32).reshape(rows, LANES)
+            both = jnp.where(halo, edge, own).astype(BF16).reshape(GRID, inner, LANES)
+            zero = jnp.zeros((inner, LANES), BF16)
+            for ref, at in ((cur, k), (xe_ref, k)):
+                ref[at, m, 0] = zero
+                ref[at, m, 1 : GRID + 1] = both
+                ref[at, m, GRID + 1] = zero
             return carry
 
-        lax.fori_loop(0, blocks + 1, patch, 0)
-        w_acc[...] = jnp.zeros_like(w_acc)
-
-    def conv(yb, carry):
+        lax.fori_loop(0, blocks + 1, body, 0)
+
+    def copied(k, x_ref):
+        def body(m, carry):
+            cur[k, m] = x_ref[0, m]
+            return carry
+
+        lax.fori_loop(0, blocks + 1, body, 0)
+
+    pl.when(i == 0)(lambda: patched(0, xa_ref))
+    pl.when(i > 0)(lambda: copied(0, xa_ref))
+    pl.when(i == end)(lambda: patched(1, xc_ref))
+    pl.when(i < end)(lambda: copied(1, xc_ref))
+
+    def conv(yb):
         pieces = []
         for dz in range(3):
             for kk in range(2):
                 for mm in range(2):
                     pieces.append(
-                        xb_ref[i + kk, yb + mm, dz : dz + GRID].reshape(rows, LANES)
+                        cur[kk, yb + mm, dz : dz + GRID].reshape(rows, LANES)
                     )
         out = dot(jnp.concatenate(pieces, axis=1), w_ref[...])
         f_ref[0, yb] = out.reshape(GRID, inner, 2 * LANES)
-        stacked = out.reshape(per_block, 8, 2 * LANES)
+
+    def stats(yb):
+        stacked = f_ref[0, yb].reshape(per_block, 8, 2 * LANES)
         mean = jnp.sum(stacked, axis=0) * (1.0 / per_block)
         dev = stacked - mean[None]
         square = jnp.sum(dev * dev, axis=0)
@@ -281,9 +396,15 @@
         delta = mean - w_acc[0]
         w_acc[0] = w_acc[0] + delta / (done + 1.0)
         w_acc[1] = w_acc[1] + square + delta * delta * (per_block * done / (done + 1.0))
+
+    def step(yb, carry):
+        stats(yb - 1)
+        conv(yb)
         return carry
 
-    lax.fori_loop(0, blocks, conv, 0)
+    conv(0)
+    lax.fori_loop(1, blocks, step, 0)
+    stats(blocks - 1)
 
     @pl.when(i == pl.num_programs(0) - 1)
     def _():
@@ -298,9 +419,8 @@
         st_ref[...] = st
 
 
-def first_conv(xi, halo, w1, planes):
-    samples = halo.shape[0]
-    c = halo.shape[1] // 2
+def first_conv(xi, lo, hi, w1, planes):
+    samples, c, _ = lo.shape
     inner = HALVES * samples
     half_y = GRID // HALVES
     pb = np.zeros((2 * c, LANES), np.float32)
@@ -308,36 +428,46 @@
         pb[ch, ch] = 1.0
         pb[ch, LANES // 2 + ch] = 1.0
     pb = jnp.asarray(pb, BF16)
+    perm = weave_matrix(inner)
     nxb = planes // 2
     f_shape = (nxb, half_y // 2, GRID, inner, 2 * LANES)
+    x_block = (1,) + xi.shape[1:]
+    xe_shape = (2,) + xi.shape[1:]
     return call(
         lambda *refs: first_kernel(planes, samples, refs),
         (
             jax.ShapeDtypeStruct(f_shape, F32),
-            jax.ShapeDtypeStruct(xi.shape, BF16),
+            jax.ShapeDtypeStruct(xe_shape, BF16),
             jax.ShapeDtypeStruct((2, LANES), F32),
         ),
         25.0,
         grid=(nxb,),
-        in_specs=[whole_spec(a.shape) for a in (xi, halo, pb, w1)],
+        in_specs=[
+            pl.BlockSpec(x_block, lambda i: (i, 0, 0, 0, 0)),
+            pl.BlockSpec(x_block, lambda i: (i + 1, 0, 0, 0, 0)),
+        ] + [whole_spec(a.shape) for a in (lo, hi, pb, perm, w1)],
         out_specs=(
             pl.BlockSpec((1,) + f_shape[1:], lambda i: (i, 0, 0, 0, 0)),
-            whole_spec(xi.shape),
+            whole_spec(xe_shape),
             whole_spec((2, LANES)),
         ),
         scratch_shapes=[
-            pltpu.VMEM((1, (half_y + 2) * GRID * inner, LANES), F32),
+            pltpu.VMEM(xe_shape, BF16),
+            pltpu.VMEM((inner, half_y // 2 + 1, GRID, LANES), BF16),
+            pltpu.VMEM((half_y // 2 + 1, GRID, inner, LANES), BF16),
             pltpu.VMEM((2, 8, 2 * LANES), F32),
         ],
         name="first_conv",
-    )(xi, halo, pb, w1)
-
-
-def group_stats(st, local_count, total_count):
-    means = st[:, 0]
-    mean = jnp.mean(means, axis=0, keepdims=True)
-    dev = means - mean
-    square = jnp.sum(st[:, 1] + local_count * dev * dev, axis=0, keepdims=True)
+    )(xi, xi, lo, hi, pb, perm, w1)
+
+
+def group_stats(refs, local_count, total_count):
+    count = len(refs)
+    mean = sum(ref[0:1] for ref in refs) * (1.0 / count)
+    square = sum(ref[1:2] for ref in refs)
+    for ref in refs:
+        dev = ref[0:1] - mean
+        square = square + local_count * dev * dev
     inverse = lax.rsqrt(square / total_count + norm_epsilon)
     return mean, inverse
 
@@ -346,65 +476,85 @@
     return jnp.concatenate([row, row], axis=1)
 
 
-def pool_kernel(local_count, total_count, f_ref, st_ref, gs_ref, pd_ref, edge_ref=None):
-    mean, inverse = group_stats(st_ref[...], local_count, total_count)
-    mean = wide(mean)
-    inverse = wide(inverse)
-    gain = wide(gs_ref[0:1])
-    shift = wide(gs_ref[1:2])
+def pool_kernel(local_count, total_count, count, refs):
+    f_ref, gs_ref, *st_refs = refs[: count + 2]
+    pd_ref, *edge_refs = refs[count + 2 :]
+    mean, inverse = group_stats(st_refs, local_count, total_count)
+    scale = gs_ref[0:1] * inverse
+    mean, scale, shift = wide(mean), wide(scale), wide(gs_ref[1:2])
     nyb = f_ref.shape[1]
     nz = f_ref.shape[2]
     inner = f_ref.shape[3]
 
+    size = 4
+
     def step(yb, carry):
-        f = f_ref[0, yb].reshape(nz * inner, 2 * LANES)
-        act = leaky_relu(gain * ((f - mean) * inverse) + shift)
-        act = act[:, :LANES] + act[:, LANES:]
-        act = act.reshape(nz // 2, 2, inner, LANES)
-        act = act[:, 0] + act[:, 1]
-        pooled = both_halves(act) * 0.125
-        pd_ref[0, yb] = pooled.astype(BF16)
+        for z in range(0, nz, size):
+            f = f_ref[0, yb, z : z + size].reshape(size * inner, 2 * LANES)
+            act = leaky_relu((f - mean) * scale + shift)
+            act = act[:, :LANES] + act[:, LANES:]
+            act = act.reshape(size // 2, 2, inner, LANES)
+            act = act[:, 0] + act[:, 1]
+            pooled = both_halves(act) * 0.125
+            pd_ref[0, yb, z // 2 : (z + size) // 2] = pooled.astype(BF16)
         return carry
 
     lax.fori_loop(0, nyb, step, 0)
-    if edge_ref is not None:
-        half = nyb // 2
+    half = nyb // 2
+
+    def pack(ref):
         mask = low_half((nz // 2, inner, LANES))
         for y in range(half):
-            edge_ref[0, y] = jnp.where(
+            ref[y] = jnp.where(
                 mask, pd_ref[0, y].astype(F32), pd_ref[0, y + half].astype(F32)
             ).astype(BF16)
 
-
-def normalise_pool(f, st, gs, local_count, total_count, edges):
+    for t, ref in enumerate(edge_refs):
+        pl.when(pl.program_id(0) == t)(lambda ref=ref: pack(ref))
+
+
+def normalise_pool(f, stats, gs, local_count, total_count, edges):
     nxb, nyb, nz, inner, _ = f.shape
     count = 2 if edges else nxb - 2
     stride, base = (nxb - 1, 0) if edges else (1, 1)
     pd_shape = (count, nyb, nz // 2, inner, LANES)
-    edge = (2, nyb // 2, nz // 2, inner, LANES)
+    edge = (nyb // 2, nz // 2, inner, LANES)
     shapes = [jax.ShapeDtypeStruct(pd_shape, BF16)]
     specs = [pl.BlockSpec((1,) + pd_shape[1:], lambda i: (i, 0, 0, 0, 0))]
     if edges:
-        shapes.append(jax.ShapeDtypeStruct(edge, BF16))
-        specs.append(pl.BlockSpec((1,) + edge[1:], lambda i: (i, 0, 0, 0, 0)))
+        shapes += [jax.ShapeDtypeStruct(edge, BF16)] * 2
+        specs += [whole_spec(edge)] * 2
     return call(
-        lambda *refs: pool_kernel(local_count, total_count, *refs),
+        lambda *refs: pool_kernel(local_count, total_count, len(stats), refs),
         shapes,
         3.0 * count,
         grid=(count,),
         in_specs=[
             pl.BlockSpec((1,) + f.shape[1:], lambda i: (i * stride + base, 0, 0, 0, 0)),
-            whole_spec(st.shape),
             whole_spec(gs.shape),
-        ],
+        ] + [whole_spec(st.shape) for st in stats],
         out_specs=specs,
         name="pool_edges" if edges else "pool_inside",
-    )(f, st, gs)
+    )(f, gs, *stats)
+
+
+def dense_copies(d_ref, j_ref, dbuf, sems):
+    parts = sems.shape[0]
+    size = dbuf.shape[0] // parts
+    return [
+        pltpu.make_async_copy(
+            d_ref.at[pl.ds(p * size, size), j_ref[0]], dbuf.at[pl.ds(p * size, size)], sems.at[p]
+        )
+        for p in range(parts)
+    ]
 
 
 def second_kernel(samples, refs):
     (j_ref, pe_ref, *mid, lo_ref, hi_ref, w_ref, d_ref, tg_ref,
-     pp_ref, sec_ref, fc_ref, hid_ref, ft, fcs) = refs
+     pp_ref, sec_ref, fc_ref, hid_ref, ft, fcs, dbuf, sems) = refs
+    copies = dense_copies(d_ref, j_ref, dbuf, sems)
+    for copy in copies:
+        copy.start()
     edges, ny, nz, inner, _ = pe_ref.shape
     planes = edges + (mid[0].shape[0] if mid else 0)
 
@@ -492,11 +642,15 @@
     def dense(t, acc):
         for u in range(8):
             ch = t * 8 + u
-            acc[u % 4] = acc[u % 4] + dot(fc_ref[ch], d_ref[ch, 0])
+            acc[u % 4] = acc[u % 4] + dot(fc_ref[ch], dbuf[ch])
         return acc
 
     zeros = [jnp.zeros((samples, LANES), F32) for _ in range(4)]
-    acc = lax.fori_loop(0, channels // 8, dense, zeros)
+    acc = zeros
+    size = channels // 8 // len(copies)
+    for p, copy in enumerate(copies):
+        copy.wait()
+        acc = lax.fori_loop(p * size, (p + 1) * size, dense, acc)
     total = (acc[0] + acc[1]) + (acc[2] + acc[3])
     own, targets_n = tg_ref.shape
     hid_ref[0:samples] = total
@@ -532,26 +686,30 @@
             num_scalar_prefetch=1,
             grid=(1,),
             in_specs=[const(p.shape) for p in pds] + [const(lo.shape), const(hi.shape), const(w2.shape),
-                      pl.BlockSpec((channels, 1, cells, units), lambda i, j_ref: (0, j_ref[0], 0, 0), pipeline_mode=pl.Buffered(1)),
-                      const(targets.shape)],
+                      pl.BlockSpec(memory_space=pl.ANY), const(targets.shape)],
             out_specs=(const(pp_shape), const(sec_shape), const(fc_shape), const((2 * samples, units))),
             scratch_shapes=[
                 pltpu.VMEM((nxb * (ny // 2) * (nz // 2) * inner, LANES), F32),
                 pltpu.VMEM((channels * samples, LANES), F32),
+                pltpu.VMEM((channels, cells, units), BF16),
+                pltpu.SemaphoreType.DMA((4,)),
             ],
         ),
         name="second_conv",
     )(j, *pds, lo, hi, w2, dense4, targets)
 
 
-def dense_kernel(samples, own, targets_n, j_ref, hp_ref, do_ref, d_ref, sec_ref,
-                 pred_ref, bh_ref, gdo_ref, bs_ref, bfc, bf):
+def dense_kernel(samples, own, targets_n, refs):
+    (j_ref, *hp_refs, do_ref, d_ref, sec_hbm, pred_ref, bh_ref, gdo_ref, bs_ref, lo_ref, hi_ref,
+     bfc, bf, dbuf, sec_ref, sems, sec_sem) = refs
+    copies = dense_copies(d_ref, j_ref, dbuf, sems)
+    for copy in copies:
+        copy.start()
+    sec_copy = pltpu.make_async_copy(sec_hbm, sec_ref, sec_sem)
+    sec_copy.start()
     nxb, ny, nz, inner, _ = sec_ref.shape
-    channels = d_ref.shape[0]
-    cells = d_ref.shape[2]
-    both = hp_ref[0]
-    for t in range(1, hp_ref.shape[0]):
-        both = both + hp_ref[t]
+    channels, cells, _ = dbuf.shape
+    both = sum(ref[...] for ref in hp_refs)
     hp = both[0:samples]
     goals = both[samples:]
     hidden = leaky_relu(hp).astype(BF16).astype(F32)
@@ -577,11 +735,14 @@
     def features(t, carry):
         for u in range(8):
             ch = t * 8 + u
-            out = dot_lanes(bh, d_ref[ch, 0])
+            out = dot_lanes(bh, dbuf[ch])
             bfc[pl.ds(pl.multiple_of(ch * samples, samples), samples), 0:cells] = out
         return carry
 
-    lax.fori_loop(0, channels // 8, features, 0)
+    size = channels // 8 // len(copies)
+    for p, copy in enumerate(copies):
+        copy.wait()
+        lax.fori_loop(p * size, (p + 1) * size, features, 0)
     half = ny // 2
     per_half = half * (nz // 2)
 
@@ -596,6 +757,7 @@
 
     lax.fori_loop(0, samples, turn, 0)
     count = nz // 2 * inner
+    sec_copy.wait()
 
     def spread(t, carry):
         xb = t // half
@@ -611,12 +773,14 @@
         return carry
 
     lax.fori_loop(0, nxb * half, spread, 0)
-
-
-def dense_layers(j, hp, dense_out_t, dense4, sec, own):
+    lo_ref[...] = bs_ref[0]
+    hi_ref[...] = bs_ref[2 * nxb - 1]
+
+
+def dense_layers(j, hps, dense_out_t, dense4, sec, own):
     nxb, ny, nz, inner, _ = sec.shape
     channels, _, cells, units = dense4.shape
-    samples = hp.shape[1] // 2
+    samples = hps[0].shape[0] // 2
     targets_n = dense_out_t.shape[0]
     bs_shape = (2 * nxb, ny, nz, inner, LANES)
 
@@ -624,28 +788,35 @@
         return pl.BlockSpec(shape, lambda i, j_ref: (0,) * len(shape), pipeline_mode=pl.Buffered(1))
 
     return call(
-        lambda *refs: dense_kernel(samples, own, targets_n, *refs),
+        lambda *refs: dense_kernel(samples, own, targets_n, refs),
         (
             jax.ShapeDtypeStruct((own, targets_n), F32),
             jax.ShapeDtypeStruct((samples, units), BF16),
             jax.ShapeDtypeStruct((8, units), F32),
             jax.ShapeDtypeStruct(bs_shape, BF16),
+            jax.ShapeDtypeStruct(bs_shape[1:], BF16),
+            jax.ShapeDtypeStruct(bs_shape[1:], BF16),
         ),
         11.0,
         grid_spec=pltpu.PrefetchScalarGridSpec(
             num_scalar_prefetch=1,
             grid=(1,),
-            in_specs=[const(hp.shape), const(dense_out_t.shape),
-                      pl.BlockSpec((channels, 1, cells, units), lambda i, j_ref: (0, j_ref[0], 0, 0), pipeline_mode=pl.Buffered(1)),
-                      const(sec.shape)],
-            out_specs=(const((own, targets_n)), const((samples, units)), const((8, units)), const(bs_shape)),
+            in_specs=[const(hp.shape) for hp in hps]
+            + [const(dense_out_t.shape)]
+            + [pl.BlockSpec(memory_space=pl.ANY)] * 2,
+            out_specs=(const((own, targets_n)), const((samples, units)), const((8, units)),
+                       const(bs_shape), const(bs_shape[1:]), const(bs_shape[1:])),
             scratch_shapes=[
                 pltpu.VMEM((channels * samples, LANES), F32),
                 pltpu.VMEM((nxb * (ny // 2) * (nz // 2) * inner, LANES), F32),
+                pltpu.VMEM((channels, cells, units), BF16),
+                pltpu.VMEM(sec.shape, F32),
+                pltpu.SemaphoreType.DMA((4,)),
+                pltpu.SemaphoreType.DMA(()),
             ],
         ),
         name="dense_layers",
-    )(j, hp, dense_out_t, dense4, sec)
+    )(j, *hps, dense_out_t, dense4, sec)
 
 
 def collect_kernel(spaces, samples, at_bh, at_grad, r_ref, t_ref, o_ref):
@@ -817,7 +988,7 @@
                 ]
                 sides.append(jnp.concatenate(blocks, axis=0))
             out = out + dot(jnp.concatenate(pieces, axis=1), jnp.concatenate(sides, axis=1))
-        out = out.astype(BF16).astype(F32)
+        out = out.astype(BF16).astype(F32) * 0.125
         mask = low_half((2 * rows, LANES))
         for px in range(2):
             v = out[:, px * LANES : (px + 1) * LANES]
@@ -843,29 +1014,36 @@
     )(bs, lo, hi, w3)
 
 
-def active_of(f, bp, mean, inverse, gain, shift):
-    nz, inner, _ = f.shape
-    w = (f.reshape(nz * inner, 2 * LANES) - mean) * inverse
-    slope = slope_of(gain * w + shift)
-    g = bp.astype(F32).reshape(nz // 2, 1, inner, LANES) * 0.125
-    g = jnp.broadcast_to(g, (nz // 2, 2, inner, LANES)).reshape(nz * inner, LANES)
-    return w, slope * jnp.concatenate([g, g], axis=1)
-
-
-def sums_kernel(local_count, total_count, f_ref, bp_ref, st_ref, gs_ref, o_ref, acc):
+def sums_kernel(local_count, total_count, count, refs):
+    f_ref, bp_ref, gs_ref, *st_refs = refs[: count + 3]
+    o_ref, act_ref, acc = refs[count + 3 :]
     i = pl.program_id(0)
-    mean, inverse = group_stats(st_ref[...], local_count, total_count)
-    mean, inverse = wide(mean), wide(inverse)
-    gain, shift = wide(gs_ref[0:1]), wide(gs_ref[1:2])
+    mean, inverse = group_stats(st_refs, local_count, total_count)
+    scale = wide(gs_ref[0:1] * inverse)
+    mean, shift = wide(mean), wide(gs_ref[1:2])
+    nz, inner = f_ref.shape[2:4]
 
     @pl.when(i == 0)
     def _():
         acc[...] = jnp.zeros_like(acc)
 
+    size = 4
+
     def step(yb, carry):
-        w, active = active_of(f_ref[0, yb], bp_ref[0, yb], mean, inverse, gain, shift)
-        acc[0] = acc[0] + jnp.sum((active * w).reshape(-1, 8, 2 * LANES), axis=0)
-        acc[1] = acc[1] + jnp.sum(active.reshape(-1, 8, 2 * LANES), axis=0)
+        cross = acc[0]
+        plain = acc[1]
+        for z in range(0, nz, size):
+            dev = f_ref[0, yb, z : z + size].reshape(size * inner, 2 * LANES) - mean
+            slope = slope_of(dev * scale + shift)
+            g = bp_ref[0, yb, z // 2 : (z + size) // 2].astype(F32)
+            g = jnp.broadcast_to(g.reshape(size // 2, 1, inner, LANES), (size // 2, 2, inner, LANES))
+            g = g.reshape(size * inner, LANES)
+            active = slope * jnp.concatenate([g, g], axis=1)
+            cross = cross + jnp.sum((active * dev).reshape(-1, 8, 2 * LANES), axis=0)
+            plain = plain + jnp.sum(active.reshape(-1, 8, 2 * LANES), axis=0)
+            act_ref[0, yb, z : z + size] = active.reshape(size, inner, 2 * LANES)
+        acc[0] = cross
+        acc[1] = plain
         return carry
 
     lax.fori_loop(0, f_ref.shape[1], step, 0)
@@ -874,36 +1052,42 @@
     def _():
         rows = [jnp.sum(acc[k], axis=0, keepdims=True) for k in range(2)]
         rows = [both_halves(r[:, :LANES] + r[:, LANES:]) for r in rows]
-        o_ref[...] = jnp.concatenate(rows, axis=0)
-
-
-def norm_sums(f, bp, st, gs, local_count, total_count):
+        o_ref[...] = jnp.concatenate([rows[0] * inverse, rows[1]], axis=0)
+
+
+def norm_sums(f, bp, stats, gs, local_count, total_count):
     return call(
-        lambda *refs: sums_kernel(local_count, total_count, *refs),
-        jax.ShapeDtypeStruct((2, LANES), F32),
+        lambda *refs: sums_kernel(local_count, total_count, len(stats), refs),
+        (jax.ShapeDtypeStruct((2, LANES), F32), jax.ShapeDtypeStruct(f.shape, F32)),
         13.0,
         grid=(f.shape[0],),
         in_specs=[
             pl.BlockSpec((1,) + f.shape[1:], lambda i: (i, 0, 0, 0, 0)),
             pl.BlockSpec((1,) + bp.shape[1:], lambda i: (i, 0, 0, 0, 0)),
-            whole_spec(st.shape),
             whole_spec(gs.shape),
-        ],
-        out_specs=whole_spec((2, LANES)),
+        ] + [whole_spec(st.shape) for st in stats],
+        out_specs=(
+            whole_spec((2, LANES)),
+            pl.BlockSpec((1,) + f.shape[1:], lambda i: (i, 0, 0, 0, 0)),
+        ),
         scratch_shapes=[pltpu.VMEM((2, 8, 2 * LANES), F32)],
         name="norm_sums",
-    )(f, bp, st, gs)
-
-
-def first_grad_kernel(local_count, total_count, c, f_ref, bp_ref, st_ref, gs_ref, sum_ref, own_ref, gdo_ref, xa_ref, xc_ref, g_ref, acc):
+    )(f, bp, gs, *stats)
+
+
+def first_grad_kernel(local_count, total_count, c, count, refs):
+    f_ref, act_ref, xa_ref, xc_ref, xe_ref, gs_ref, gdo_ref = refs[:7]
+    st_refs = refs[7 : 7 + count]
+    sum_refs = refs[7 + count : 7 + 2 * count]
+    g_ref, acc, cur, left_a, left_b = refs[7 + 2 * count :]
     i = pl.program_id(0)
-    mean, inverse = group_stats(st_ref[...], local_count, total_count)
-    mean, inverse = wide(mean), wide(inverse)
-    gain, shift = wide(gs_ref[0:1]), wide(gs_ref[1:2])
-    group_sums = jnp.sum(sum_ref[...], axis=0)
-    cross = wide(group_sums[0:1]) * (1.0 / total_count)
-    plain = wide(group_sums[1:2]) * (1.0 / total_count)
-    scale = gain * inverse
+    end = pl.num_programs(0) - 1
+    mean, inverse = group_stats(st_refs, local_count, total_count)
+    group_sums = sum(ref[...] for ref in sum_refs) * (1.0 / total_count)
+    scale = gs_ref[0:1] * inverse
+    cross = wide(scale * inverse * group_sums[0:1])
+    plain = wide(scale * group_sums[1:2])
+    scale, mean = wide(scale), wide(mean)
     nz = f_ref.shape[2]
     inner = f_ref.shape[3]
     rows = nz * inner
@@ -912,26 +1096,50 @@
     def _():
         acc[...] = jnp.zeros_like(acc)
 
-    def step(yb, carry):
-        w, active = active_of(f_ref[0, yb], bp_ref[0, yb], mean, inverse, gain, shift)
-        left = (scale * (active - plain - w * cross)).astype(BF16).T
+    def load(k, ref, at):
+        def body(m, carry):
+            cur[k, m] = ref[at, m]
+            return carry
+
+        lax.fori_loop(0, cur.shape[1], body, 0)
+
+    pl.when(i == 0)(lambda: load(0, xe_ref, 0))
+    pl.when(i > 0)(lambda: load(0, xa_ref, 0))
+    pl.when(i == end)(lambda: load(1, xe_ref, 1))
+    pl.when(i < end)(lambda: load(1, xc_ref, 0))
+
+    def left(yb, ref):
+        dev = f_ref[0, yb].reshape(rows, 2 * LANES) - mean
+        active = act_ref[0, yb].reshape(rows, 2 * LANES)
+        ref[...] = (active * scale - (dev * cross + plain)).astype(BF16).T
+
+    def add(yb, ref):
         for dz in range(3):
-            for kk, x_ref in enumerate((xa_ref, xc_ref)):
+            for kk in range(2):
                 right = jnp.concatenate(
-                    [x_ref[0, yb + mm, dz : dz + nz].reshape(rows, LANES) for mm in range(2)],
+                    [cur[kk, yb + mm, dz : dz + nz].reshape(rows, LANES) for mm in range(2)],
                     axis=1,
                 )
-                acc[dz * 2 + kk] = acc[dz * 2 + kk] + dot(left, right)
+                acc[dz * 2 + kk] = acc[dz * 2 + kk] + dot(ref[...], right)
+
+    blocks = f_ref.shape[1]
+
+    def step(t, carry):
+        left(2 * t + 1, left_b)
+        add(2 * t, left_a)
+        left(jnp.minimum(2 * t + 2, blocks - 1), left_a)
+        add(2 * t + 1, left_b)
         return carry
 
-    lax.fori_loop(0, f_ref.shape[1], step, 0)
-
-    @pl.when(i == pl.num_programs(0) - 1)
+    left(0, left_a)
+    lax.fori_loop(0, blocks // 2, step, 0)
+
+    @pl.when(i == end)
     def _():
         co = LANES // 2
         blocks = -(-27 * c // LANES)
         g_ref[(blocks - 1) * co :, :] = jnp.zeros((g_ref.shape[0] - (blocks - 1) * co, LANES), F32)
-        g_ref[blocks * co : blocks * co + 2, :] = own_ref[...]
+        g_ref[blocks * co : blocks * co + 2, :] = sum_refs[0][...]
         g_ref[blocks * co + 8 : blocks * co + 16, :] = gdo_ref[...]
         for a in range(3):
             for b in range(3):
@@ -944,34 +1152,34 @@
                             top = (px * 2 + py) * co
                             part = acc[d * 2 + xw // 2, top : top + co, at : at + c]
                             total = part if total is None else total + part
-                    at = ((a * 3 + b) * 3 + d) * c
+                    at = offset(a, b, d) * c
                     row = at // LANES * co
                     g_ref[row : row + co, at % LANES : at % LANES + c] = total
 
 
-def first_grad(f, bp, st, gs, sums, own, gdo, xb, c, local_count, total_count, rows):
-    x_block = (1,) + xb.shape[1:]
+def first_grad(f, active, xi, xe, gs, gdo, stats, sums, c, local_count, total_count, rows):
+    x_block = (1,) + xi.shape[1:]
     out = (rows, LANES)
     return call(
-        lambda *refs: first_grad_kernel(local_count, total_count, c, *refs),
+        lambda *refs: first_grad_kernel(local_count, total_count, c, len(stats), refs),
         jax.ShapeDtypeStruct(out, F32),
-        33.0,
+        30.0,
         grid=(f.shape[0],),
         in_specs=[
             pl.BlockSpec((1,) + f.shape[1:], lambda i: (i, 0, 0, 0, 0)),
-            pl.BlockSpec((1,) + bp.shape[1:], lambda i: (i, 0, 0, 0, 0)),
-            whole_spec(st.shape),
-            whole_spec(gs.shape),
-            whole_spec(sums.shape),
-            whole_spec(own.shape),
-            whole_spec(gdo.shape),
+            pl.BlockSpec((1,) + f.shape[1:], lambda i: (i, 0, 0, 0, 0)),
             pl.BlockSpec(x_block, lambda i: (i, 0, 0, 0, 0)),
             pl.BlockSpec(x_block, lambda i: (i + 1, 0, 0, 0, 0)),
+        ] + [whole_spec(a.shape) for a in (xe, gs, gdo, *stats, *sums)],
+        out_specs=whole_spec(out),
+        scratch_shapes=[
+            pltpu.VMEM((6, 2 * LANES, 2 * LANES), F32),
+            pltpu.VMEM(xe.shape, BF16),
+            pltpu.VMEM((2 * LANES, f.shape[2] * f.shape[3]), BF16),
+            pltpu.VMEM((2 * LANES, f.shape[2] * f.shape[3]), BF16),
         ],
-        out_specs=whole_spec(out),
-        scratch_shapes=[pltpu.VMEM((6, 2 * LANES, 2 * LANES), F32)],
         name="first_grad",
-    )(f, bp, st, gs, sums, own, gdo, xb, xb)
+    )(f, active, xi, xi, xe, gs, gdo, *stats, *sums)
 
 
 def add_kernel(r_ref, o_ref):
@@ -993,7 +1201,7 @@
         lax.ppermute(value, axis, [(i, (i + k) % count) for i in range(count)])
         for k in range(1, count)
     ]
-    return jnp.stack([value] + others)
+    return [value] + others
 
 
 def swap(parts, axes):
@@ -1001,10 +1209,10 @@
 
 
 def finish_second_kernel(r_ref, g_ref):
-    columns = g_ref.shape[1]
+    columns = g_ref.shape[0]
     for k in range(r_ref.shape[0]):
         width = min(LANES, columns - k * LANES)
-        g_ref[:, k * LANES : k * LANES + width] = r_ref[k].astype(F32)[:, 0:width]
+        g_ref[k * LANES : k * LANES + width, :] = r_ref[k].astype(F32).T[0:width]
 
 
 def finish_first_kernel(r_ref, g_ref, n_ref, gdo_ref):
@@ -1015,7 +1223,7 @@
         g_ref[:, k * LANES : k * LANES + width] = r_ref[k * co : (k + 1) * co].astype(F32)[:, 0:width]
     tail = r_ref[blocks * co : blocks * co + 16].astype(F32)
     n_ref[...] = tail[0:2, 0 : n_ref.shape[1]]
-    gdo_ref[...] = tail[8:16].T[:, 0 : gdo_ref.shape[1]]
+    gdo_ref[...] = tail[8 : 8 + gdo_ref.shape[0]]
 
 
 def swap_edges(first, last, axis):
@@ -1038,30 +1246,34 @@
     everyone = groups * spaces
     world = ("dp", "space")
 
-    before, after = swap_edges(inputs[:, :, :1], inputs[:, :, planes - 1 :], "space")
-    w1, w2, v3 = make_weights(conv_in, conv_out)
-    xi = prepare(inputs.reshape(samples, c * planes, cells), planes, c)
+    x = inputs.reshape(samples, c * planes, cells)
+    first, last = edge_planes(x, planes, c)
+    before, after = swap_edges(first, last, "space")
+    w1 = first_weights(conv_in)
+    xi = prepare(x, planes, c)
     gs = jnp.stack([norm_gain, norm_shift])
     gs = jnp.concatenate([gs, gs], axis=1)
     j = lax.axis_index("space").astype(jnp.int32).reshape(1)
     dense4 = dense_in.reshape(channels, spaces, dense_in.shape[0] // (channels * spaces), units)
-    halo = jnp.concatenate([before, after], axis=1).reshape(samples, 2 * c, cells)
-
-    f, xb, st = first_conv(xi, halo, w1, planes)
+
+    f, xe, st = first_conv(xi, before, after, w1, planes)
     stats = gather_all(st, "space")
-    outer, edge = normalise_pool(f, stats, gs, local_count, total_count, True)
-    lo, hi = swap_edges(edge[0], edge[1], "space")
+    w2, v3 = second_weights(conv_out)
+    outer, edge_lo, edge_hi = normalise_pool(f, stats, gs, local_count, total_count, True)
+    lo, hi = swap_edges(edge_lo, edge_hi, "space")
     pds = [outer]
     if planes > 4:
         pds += normalise_pool(f, stats, gs, local_count, total_count, False)
     pp, sec, fc, partial = second_conv(j, pds, lo, hi, w2, dense4, targets, samples)
-    hp = gather_all(partial, "space")
-    predictions, bh, gdo, bs = dense_layers(j, hp, dense_out.astype(F32).T, dense4, sec, own)
-    bs_lo, bs_hi = swap_edges(bs[0], bs[-1], "space")
+    hps = gather_all(partial, "space")
+    predictions, bh, gdo, bs, bs_first, bs_last = dense_layers(
+        j, hps, dense_out.astype(F32).T, dense4, sec, own
+    )
+    bs_lo, bs_hi = swap_edges(bs_first, bs_last, "space")
     message = second_grad(bs, pp, fc, bh, everyone)
     received = swap(message, world)
     bp = second_back(bs, bs_lo, bs_hi, v3)
-    own_sums = norm_sums(f, bp, stats, gs, local_count, total_count)
+    own_sums, active = norm_sums(f, bp, stats, gs, local_count, total_count)
     sums = gather_all(own_sums, "space")
     totals, grad_dense_in = collect(received, spaces, fc.shape)
     totals = swap(totals, world)
@@ -1069,12 +1281,12 @@
     rows = -(-used // everyone)
     rows = (-(-rows // 8) * 8 if rows > 8 else rows) * everyone
     local_in = first_grad(
-        f, bp, stats, gs, sums, own_sums, gdo, xb, c, local_count, total_count, rows
+        f, active, xi, xe, gs, gdo, stats, sums, c, local_count, total_count, rows
     )
     parts = swap(local_in.reshape(everyone, -1, LANES), world)
     grad_conv_out = call(
         finish_second_kernel,
-        jax.ShapeDtypeStruct(conv_out.shape, F32),
+        jax.ShapeDtypeStruct(conv_out.shape[::-1], F32),
         2.0,
         name="finish_second",
     )(totals.reshape(14, LANES, LANES))
@@ -1085,16 +1297,16 @@
         (
             jax.ShapeDtypeStruct(conv_in.shape, F32),
             jax.ShapeDtypeStruct((2, norm_gain.shape[0]), F32),
-            jax.ShapeDtypeStruct(dense_out.shape, F32),
+            jax.ShapeDtypeStruct(dense_out.shape[::-1], F32),
         ),
         name="finish_first",
     )(totals.reshape(rows, LANES))
     return (
         grad_conv_in,
         grad_norm,
-        grad_conv_out,
+        grad_conv_out.T,
         grad_dense_in.reshape(-1, units),
-        grad_dense_out,
+        grad_dense_out.T,
         predictions,
     )
 

time: 307 us -> 273 us (0.89)
  Pallas kernels: 180 us -> 162 us
  local copies, waits for them, and re-layouts: 16.1 us -> 5.61 us
  starting transfers between devices: 51.8 us -> 42.5 us
  waiting for transfers between devices: 50.5 us -> 59.3 us
  other arithmetic: 6.14 us -> 1.24 us
    pallas_call x8 -> x10, Pallas kernels: 96.6 us -> 87.7 us  [the longest x1 26.5 us: first_grad(): call(lambda *refs: first_grad_kernel(local_count, total_count, c, len(sta...]
    pallas_call x1, Pallas kernels: 37.2 us -> 29.9 us  [first_conv(): call(lambda *refs: first_kernel(planes, samples, refs), (jax.ShapeDtypeSt...]
    ppermute x9, waiting for transfers between devices: 5.72 us -> 12.1 us  [gather_all(): lax.ppermute(value, axis, [(i, (i + k) % count) for i in range(count)])]
    slice x1 -> x0, local copies, waits for them, and re-layouts: 5.45 us -> none  [shards(): inputs[:, :, planes - 1:]]
    ppermute x9, starting transfers between devices: 19.7 us -> 14.5 us  [gather_all(): lax.ppermute(value, axis, [(i, (i + k) % count) for i in range(count)])]
    another operation x3 -> x0, other arithmetic: 3.86 us -> none  [gather_all(): return jnp.stack([value] + others)]
    all_to_all x4, starting transfers between devices: 19.2 us -> 15.7 us  [swap(): return lax.all_to_all(parts, axes, split_axis=0, concat_axis=0, tiled=True)]
    unnamed x31 -> x44, local copies, waits for them, and re-layouts: 6.73 us -> 5.61 us
  transfers between devices with their start and end apart: 19 -> 19, of which waited for: 12 -> 13; matrix products, arithmetic and copies ran while one was open for 2% -> 0% of each run, Pallas kernels for 15% -> 15%
where the time goes in v3:
time: 273 us; the launch traced here: 271 us
  Pallas kernels  162 us (59%)
  waiting for transfers between devices  59.3 us (22%)
  starting transfers between devices  42.5 us (16%)
  local copies, waits for them, and re-layouts  5.61 us (2%)
    all_to_all x4, waiting for transfers between devices, swap(): return lax.all_to_all(parts, axes, split_axis=0, concat_axis=0, tiled=True)  36.3 us
    pallas_call x1, Pallas kernels, first_conv(): call(lambda *refs: first_kernel(planes, samples, refs), (jax.ShapeDtypeSt...  29.9 us
    pallas_call x1, Pallas kernels, first_grad(): call(lambda *refs: first_grad_kernel(local_count, total_count, c, len(sta...  26.5 us
    pallas_call x1, Pallas kernels, second_conv(): call(lambda *refs: second_kernel(samples, refs), (jax.ShapeDtypeStruct(pp...  16.1 us
    pallas_call x1, Pallas kernels, norm_sums(): call(lambda *refs: sums_kernel(local_count, total_count, len(stats), refs...  15.9 us
    all_to_all x4, starting transfers between devices, swap(): return lax.all_to_all(parts, axes, split_axis=0, concat_axis=0, tiled=True)  15.7 us
    ppermute x9, starting transfers between devices, gather_all(): lax.ppermute(value, axis, [(i, (i + k) % count) for i in range(count)])  14.5 us
    pallas_call x2, Pallas kernels, normalise_pool(): call(lambda *refs: pool_kernel(local_count, total_count, len(stats), refs...  13.3 us
  transfers between devices with their start and end apart: 19, of which 13 were waited for; matrix products, arithmetic and copies ran while one was open for 0% of the time, Pallas kernels for 15%

profile of v3, /device:TPU:0, one launch (start us, length us, event | category | flops | bytes accessed | tf_op | source)
XLA Modules:
  0.0 271.5 jit_solution(7579152282060921166)
XLA Ops:
  0.6 3.5 %edge_planes.1 = (bf16[8,32,1024]{2,1,0:T(8,128)(2,1)}, bf16[8,32,1024]{2,1,0:T(8,128)(2,1)}) custom-call(bf16[8,256,1024]{2,1,0:T(8,128)(2,1)} %bitcast.21, bf16[64,256]{1,0:T(8,128)(2,1)} %constant.12.clone.sel_ref), custom_call_target="tpu_custom_call" | custom-call | flops 2500000000 | bytes 7500000 | tf_op jit(solution)/shard_map/edge_planes/pallas_call | solution.py:309
  4.1 5.0 %collective-permute-start = (bf16[8,32,1024]{2,1,0:T(8,128)(2,1)}, bf16[8,32,1024]{2,1,0:T(8,128)(2,1)S(1)}, u32[]{:S(2)}, u32[]{:S(2)}) collective-permute-start(bf16[8,32,1024]{2,1,0:T(8,128)(2,1)} %get-tuple-element.33), channel_id=1, source_target_pairs={{0,1},{1,2},{2,3},{4,5},{5,6},{6,7},{8,9},{9,10},{10,11},{12,13},{... | collective-permute-start | bytes 1572872 | tf_op jit(solution)/shard_map/ppermute | solution.py:1231
  10.4 11.3 %prepare.1.refs_0_.refs_1_.refs_2_.refs_3_ = bf16[5,9,34,16,128]{4,3,2,1,0:T(8,128)(2,1)} custom-call(bf16[8,256,1024]{2,1,0:T(8,128)(2,1)} %bitcast.22, bf16[256,640]{1,0:T(8,128)(2,1)} %constant.13.clone.refs_1_, bf16[256,256]{1,0:T(8,128)(2,1)} %constant.14.clone.refs_2_.refs_5_), custom_call_target="tpu_custom_call" | custom-call | flops 11000000512 | bytes 33000000 | tf_op jit(solution)/shard_map/prepare/pallas_call | solution.py:275
  28.4 29.9 %first_conv.1 = (f32[4,8,32,16,256]{4,3,2,1,0:T(8,128)}, bf16[2,9,34,16,128]{4,3,2,1,0:T(8,128)(2,1)}, f32[2,128]{1,0:T(2,128)}) custom-call(bf16[5,9,34,16,128]{4,3,2,1,0:T(8,128)(2,1)} %prepare.1.refs_0_.refs_1_.refs_2_.refs_3_, bf16[5,9,34,16,128]{4,3,2,1,0:T(8,128)(2,1)} %prepare.1.refs_0_.refs_1_.refs_2_.refs_3_, bf16[8,32,1024]{2,1,0:T(8,128)(2,1)} %copy-done.7, ...), custom_call_target="tpu_custom_call" | custom-call | flops 24999999488 | bytes 75000000 | tf_op jit(solution)/shard_map/first_conv/pallas_call | solution.py:436
  58.4 4.7 %collective-permute-start.4 = (f32[2,128]{1,0:T(2,128)}, f32[2,128]{1,0:T(2,128)S(1)}, u32[]{:S(2)}, u32[]{:S(2)}) collective-permute-start(f32[2,128]{1,0:T(2,128)} %get-tuple-element.36.refs_2_.refs_3_.refs_7_), channel_id=1, source_target_pairs={{0,3},{1,0},{2,1},{3,2},{4,7},{5,4},{6,5},{7,6},{8,11},{9,8},{10,9... | collective-permute-start | bytes 3080 | tf_op jit(solution)/shard_map/ppermute | solution.py:1201
  64.7 3.0 %collective-permute-done.3.refs_4_.refs_5_.refs_9_ = f32[2,128]{1,0:T(2,128)S(1)} collective-permute-done((f32[2,128]{1,0:T(2,128)}, f32[2,128]{1,0:T(2,128)S(1)}, u32[]{:S(2)}, u32[]{:S(2)}) %collective-permute-start.3) | collective-permute-done | bytes 1056 | tf_op jit(solution)/shard_map/ppermute | solution.py:1201
  69.3 6.8 %pool_edges.1 = (bf16[2,8,16,16,128]{4,3,2,1,0:T(8,128)(2,1)}, bf16[4,16,16,128]{3,2,1,0:T(8,128)(2,1)}, bf16[4,16,16,128]{3,2,1,0:T(8,128)(2,1)}) custom-call(f32[4,8,32,16,256]{4,3,2,1,0:T(8,128)} %get-tuple-element.35.refs_0_, f32[2,128]{1,0:T(2,128)} %maximum_maximum_fusion.refs_1_.refs_2_.refs_5_, f32[2,128]{1,0:T(2,128)} %get-tuple-element.36.refs_2_.refs_3_.refs_7_, ...), custom_call_target="tpu_custom_call" | custom-call | flops 6000000000 | bytes 18000000 | tf_op jit(solution)/shard_map/pool_edges/pallas_call | solution.py:527
  78.7 6.5 %pool_inside.1.refs_2_ = bf16[2,8,16,16,128]{4,3,2,1,0:T(8,128)(2,1)} custom-call(f32[4,8,32,16,256]{4,3,2,1,0:T(8,128)} %get-tuple-element.35.refs_0_, f32[2,128]{1,0:T(2,128)} %maximum_maximum_fusion.refs_1_.refs_2_.refs_5_, f32[2,128]{1,0:T(2,128)} %get-tuple-element.36.refs_2_.refs_3_.refs_7_, f32[2,128]{1,0:T(2,128)} %copy-done.18, ...), custom_call_target="tpu_custom_call" | custom-call | flops 6000000000 | bytes 18000000 | tf_op jit(solution)/shard_map/pool_inside/pallas_call | solution.py:527
  86.8 16.1 %second_conv.1 = (bf16[3,10,18,16,128]{4,3,2,1,0:T(8,128)(2,1)}, f32[2,8,16,16,256]{4,3,2,1,0:T(8,128)}, bf16[128,8,128]{2,1,0:T(8,128)(2,1)}, f32[16,128]{1,0:T(8,128)}) custom-call(s32[1]{0:T(128)} %bitcast.1.refs_0_, bf16[2,8,16,16,128]{4,3,2,1,0:T(8,128)(2,1)} %get-tuple-element.37.refs_1_, bf16[2,8,16,16,128]{4,3,2,1,0:T(8,128)(2,1)} %pool_inside.1.refs_2_, ...), custom_call_target="tpu_custom_call" | custom-call | flops 16999999488 | bytes 51000000 | tf_op jit(solution)/shard_map/second_conv/pallas_call | solution.py:676
  102.9 3.1 %collective-permute-start.9 = (f32[16,128]{1,0:T(8,128)}, f32[16,128]{1,0:T(8,128)S(1)}, u32[]{:S(2)}, u32[]{:S(2)}) collective-permute-start(f32[16,128]{1,0:T(8,128)} %get-tuple-element.41.refs_1_), channel_id=1, source_target_pairs={{0,3},{1,0},{2,1},{3,2},{4,7},{5,4},{6,5},{7,6},{8,11},{9,8},{10,9... | collective-permute-start | bytes 24584 | tf_op jit(solution)/shard_map/ppermute | solution.py:1201
  112.9 10.0 %dense_layers.1 = (f32[2,4]{1,0:T(2,128)}, bf16[8,128]{1,0:T(8,128)(2,1)}, f32[8,128]{1,0:T(8,128)}, bf16[4,8,16,16,128]{4,3,2,1,0:T(8,128)(2,1)}, bf16[8,16,16,...) custom-call(s32[1]{0:T(128)} %bitcast.1.refs_0_, f32[16,128]{1,0:T(8,128)} %get-tuple-element.41.refs_1_, ...), custom_call_target="tpu_custom_call" | custom-call | flops 11000000512 | bytes 33000000 | tf_op jit(solution)/shard_map/dense_layers/pallas_call | solution.py:790
  126.3 5.9 %collective-permute-done.10.lo_ref = bf16[8,16,16,128]{3,2,1,0:T(8,128)(2,1)S(1)} collective-permute-done((bf16[8,16,16,128]{3,2,1,0:T(8,128)(2,1)}, bf16[8,16,16,128]{3,2,1,0:T(8,128)(2,1)S(1)}, u32[]{:S(2)}, u32[]{:S(2)}) %collective-permute-start.10) | collective-permute-done | bytes 524320 | tf_op jit(solution)/shard_map/ppermute | solution.py:1231
  132.2 4.1 %collective-permute-done.11.hi_ref = bf16[8,16,16,128]{3,2,1,0:T(8,128)(2,1)S(1)} collective-permute-done((bf16[8,16,16,128]{3,2,1,0:T(8,128)(2,1)}, bf16[8,16,16,128]{3,2,1,0:T(8,128)(2,1)S(1)}, u32[]{:S(2)}, u32[]{:S(2)}) %collective-permute-start.11) | collective-permute-done | bytes 524320 | tf_op jit(solution)/shard_map/ppermute | solution.py:1232
  137.0 11.7 %second_back.1.refs_1_ = bf16[4,8,16,16,128]{4,3,2,1,0:T(8,128)(2,1)} custom-call(bf16[4,8,16,16,128]{4,3,2,1,0:T(8,128)(2,1)} %get-tuple-element.43.bs_ref, bf16[8,16,16,128]{3,2,1,0:T(8,128)(2,1)} %copy-done.9, bf16[8,16,16,128]{3,2,1,0:T(8,128)(2,1)} %copy-done.10, bf16[3,3,4,128,128]{4,3,2,1,0:T(8,128)(2,1)} %get-tuple-element.46.w_ref), custom_call_target="tpu_custom_call" | custom-call | flops 12000000000 | bytes 36000000 | tf_op jit(solution)/shard_map/second_back/pallas_call | solution.py:1008
  148.7 15.9 %norm_sums.1 = (f32[2,128]{1,0:T(2,128)}, f32[4,8,32,16,256]{4,3,2,1,0:T(8,128)}) custom-call(f32[4,8,32,16,256]{4,3,2,1,0:T(8,128)} %get-tuple-element.35.refs_0_, bf16[4,8,16,16,128]{4,3,2,1,0:T(8,128)(2,1)} %second_back.1.refs_1_, f32[2,128]{1,0:T(2,128)} %maximum_maximum_fusion.refs_1_.refs_2_.refs_5_, ...), custom_call_target="tpu_custom_call" | custom-call | flops 12999999488 | bytes 39000000 | tf_op jit(solution)/shard_map/norm_sums/pallas_call | solution.py:1059
  169.5 3.3 %collective-permute-done.12.refs_12_ = f32[2,128]{1,0:T(2,128)S(1)} collective-permute-done((f32[2,128]{1,0:T(2,128)}, f32[2,128]{1,0:T(2,128)S(1)}, u32[]{:S(2)}, u32[]{:S(2)}) %collective-permute-start.12) | collective-permute-done | bytes 1056 | tf_op jit(solution)/shard_map/ppermute | solution.py:1201
  173.3 26.5 %first_grad.1 = f32[512,128]{1,0:T(8,128)} custom-call(f32[4,8,32,16,256]{4,3,2,1,0:T(8,128)} %get-tuple-element.35.refs_0_, f32[4,8,32,16,256]{4,3,2,1,0:T(8,128)} %get-tuple-element.47.refs_1_, bf16[5,9,34,16,128]{4,3,2,1,0:T(8,128)(2,1)} %prepare.1.refs_0_.refs_1_.refs_2_.refs_3_, bf16[5,9,34,16,128]{4,3,2,1,0:T(8,128)(2,1)} %prepare.1.refs_0_.refs_1_.refs_2_.refs_3_, ...), custom_call_target="tpu_custom_call" | custom-call | flops 30000001024 | bytes 90000000 | tf_op jit(solution)/shard_map/first_grad/pallas_call | solution.py:1163
  199.8 3.0 %all-to-all-start = ((f32[32,16,128]{2,1,0:T(8,128)}), f32[32,16,128]{2,1,0:T(8,128)S(1)}, u32[]{:S(2)}, u32[]{:S(2)}) async-start(f32[32,16,128]{2,1,0:T(8,128)} %bitcast.15), calls=%async_computation | async-start | bytes 524288 | tf_op jit(solution)/shard_map/all_to_all | solution.py:1208
  202.8 10.8 %second_grad.1 = bf16[32,104,128]{2,1,0:T(8,128)(2,1)} custom-call(bf16[4,8,16,16,128]{4,3,2,1,0:T(8,128)(2,1)} %get-tuple-element.43.bs_ref, bf16[3,10,18,16,128]{4,3,2,1,0:T(8,128)(2,1)} %get-tuple-element.53.pp_ref, bf16[128,8,128]{2,1,0:T(8,128)(2,1)} %get-tuple-element.54.fc_ref, bf16[8,128]{1,0:T(8,128)(2,1)} %get-tuple-element.55.bh_ref), custom_call_target="tpu_custom_call" | custom-call | flops 12000000000 | bytes 36000000 | tf_op jit(solution)/shard_map/second_grad/pallas_call | solution.py:918
  213.6 5.7 %all-to-all-start.2 = ((bf16[32,104,128]{2,1,0:T(8,128)(2,1)}), bf16[32,104,128]{2,1,0:T(8,128)(2,1)S(1)}, u32[]{:S(2)}, u32[]{:S(2)}) async-start(bf16[32,104,128]{2,1,0:T(8,128)(2,1)} %second_grad.1), calls=%async_computation.2 | async-start | bytes 1703936 | tf_op jit(solution)/shard_map/all_to_all | solution.py:1208
  220.9 19.2 %all-to-all-done.2.refs_0_ = bf16[32,104,128]{2,1,0:T(8,128)(2,1)S(1)} async-done(((bf16[32,104,128]{2,1,0:T(8,128)(2,1)}), bf16[32,104,128]{2,1,0:T(8,128)(2,1)S(1)}, u32[]{:S(2)}, u32[]{:S(2)}) %all-to-all-start.2) | async-done | bytes 852000 | tf_op jit(solution)/shard_map/all_to_all | solution.py:1208
  240.1 4.5 %all-to-all-start.1 = ((bf16[32,16,128]{2,1,0:T(8,128)(2,1)}), bf16[32,16,128]{2,1,0:T(8,128)(2,1)S(1)}, u32[]{:S(2)}, u32[]{:S(2)}) async-start(bf16[32,16,128]{2,1,0:T(8,128)(2,1)} %add_parts.1), calls=%async_computation.1 | async-start | bytes 262144 | tf_op jit(solution)/shard_map/all_to_all | solution.py:1208
  247.2 5.8 %all-to-all-done.1 = bf16[32,16,128]{2,1,0:T(8,128)(2,1)S(1)} async-done(((bf16[32,16,128]{2,1,0:T(8,128)(2,1)}), bf16[32,16,128]{2,1,0:T(8,128)(2,1)S(1)}, u32[]{:S(2)}, u32[]{:S(2)}) %all-to-all-start.1) | async-done | bytes 131104 | tf_op jit(solution)/shard_map/all_to_all | solution.py:1208
  257.2 11.4 %all-to-all-done.3 = bf16[32,56,128]{2,1,0:T(8,128)(2,1)S(1)} async-done(((bf16[32,56,128]{2,1,0:T(8,128)(2,1)}), bf16[32,56,128]{2,1,0:T(8,128)(2,1)S(1)}, u32[]{:S(2)}, u32[]{:S(2)}) %all-to-all-start.3) | async-done | bytes 458784 | tf_op jit(solution)/shard_map/all_to_all | solution.py:1208
  (77 shorter events, 43.1 us)
Async XLA Ops:
  4.1 22.7 %collective-permute-start = (bf16[8,32,1024]{2,1,0:T(8,128)(2,1)}, bf16[8,32,1024]{2,1,0:T(8,128)(2,1)S(1)}, u32[]{:S(2)}, u32[]{:S(2)}) collective-permute-start(bf16[8,32,1024]{2,1,0:T(8,128)(2,1)} %get-tuple-element.33), channel_id=1, source_target_pairs={{0,1},{1,2},{2,3},{4,5},{5,6},{6,7},{8,9},{9,10},{10,11},{12,13},{... | collective-permute-start | bytes 1572872 | tf_op jit(solution)/shard_map/ppermute | solution.py:1231
  9.1 17.7 %collective-permute-start.1 = (bf16[8,32,1024]{2,1,0:T(8,128)(2,1)}, bf16[8,32,1024]{2,1,0:T(8,128)(2,1)S(1)}, u32[]{:S(2)}, u32[]{:S(2)}) collective-permute-start(bf16[8,32,1024]{2,1,0:T(8,128)(2,1)} %get-tuple-element.34), channel_id=1, source_target_pairs={{1,0},{2,1},{3,2},{5,4},{6,5},{7,6},{9,8},{10,9},{11,10},{13,12},{... | collective-permute-start | bytes 1572872 | tf_op jit(solution)/shard_map/ppermute | solution.py:1232
  26.8 37.2 %copy-start.5 = (f32[64]{0:T(128)S(1)}, f32[64]{0:T(128)}, u32[]{:S(2)}) copy-start(f32[64]{0:T(128)} %param.16) | copy-start | bytes 772
  26.8 37.2 %copy-start.6 = (f32[64]{0:T(128)S(1)}, f32[64]{0:T(128)}, u32[]{:S(2)}) copy-start(f32[64]{0:T(128)} %param.15) | copy-start | bytes 772
  58.4 6.4 %collective-permute-start.4 = (f32[2,128]{1,0:T(2,128)}, f32[2,128]{1,0:T(2,128)S(1)}, u32[]{:S(2)}, u32[]{:S(2)}) collective-permute-start(f32[2,128]{1,0:T(2,128)} %get-tuple-element.36.refs_2_.refs_3_.refs_7_), channel_id=1, source_target_pairs={{0,3},{1,0},{2,1},{3,2},{4,7},{5,4},{6,5},{7,6},{8,11},{9,8},{10,9... | collective-permute-start | bytes 3080 | tf_op jit(solution)/shard_map/ppermute | solution.py:1201
  63.1 4.7 %collective-permute-start.3 = (f32[2,128]{1,0:T(2,128)}, f32[2,128]{1,0:T(2,128)S(1)}, u32[]{:S(2)}, u32[]{:S(2)}) collective-permute-start(f32[2,128]{1,0:T(2,128)} %get-tuple-element.36.refs_2_.refs_3_.refs_7_), channel_id=1, source_target_pairs={{0,2},{1,3},{2,0},{3,1},{4,6},{5,7},{6,4},{7,5},{8,10},{9,11},{10,... | collective-permute-start | bytes 3080 | tf_op jit(solution)/shard_map/ppermute | solution.py:1201
  63.1 5.6 %collective-permute-start.2 = (f32[2,128]{1,0:T(2,128)}, f32[2,128]{1,0:T(2,128)S(1)}, u32[]{:S(2)}, u32[]{:S(2)}) collective-permute-start(f32[2,128]{1,0:T(2,128)} %get-tuple-element.36.refs_2_.refs_3_.refs_7_), channel_id=1, source_target_pairs={{0,1},{1,2},{2,3},{3,0},{4,5},{5,6},{6,7},{7,4},{8,9},{9,10},{10,1... | collective-permute-start | bytes 3080 | tf_op jit(solution)/shard_map/ppermute | solution.py:1201
  76.0 9.2 %collective-permute-start.5 = (bf16[4,16,16,128]{3,2,1,0:T(8,128)(2,1)}, bf16[4,16,16,128]{3,2,1,0:T(8,128)(2,1)S(1)}, u32[]{:S(2)}, u32[]{:S(2)}) collective-permute-start(bf16[4,16,16,128]{3,2,1,0:T(8,128)(2,1)} %get-tuple-element.38), channel_id=1, source_target_pairs={{0,1},{1,2},{2,3},{4,5},{5,6},{6,7},{8,9},{9,10},{10,11},{12,13},{... | collective-permute-start | bytes 786440 | tf_op jit(solution)/shard_map/ppermute | solution.py:1231
  77.4 8.7 %collective-permute-start.6 = (bf16[4,16,16,128]{3,2,1,0:T(8,128)(2,1)}, bf16[4,16,16,128]{3,2,1,0:T(8,128)(2,1)S(1)}, u32[]{:S(2)}, u32[]{:S(2)}) collective-permute-start(bf16[4,16,16,128]{3,2,1,0:T(8,128)(2,1)} %get-tuple-element.39), channel_id=1, source_target_pairs={{1,0},{2,1},{3,2},{5,4},{6,5},{7,6},{9,8},{10,9},{11,10},{13,12},{... | collective-permute-start | bytes 786440 | tf_op jit(solution)/shard_map/ppermute | solution.py:1232
  86.8 21.8 %copy-start.4 = (bf16[128,4]{0,1:T(4,128)(2,1)S(1)}, bf16[128,4]{0,1:T(4,128)(2,1)}, u32[]{:S(2)}) copy-start(bf16[128,4]{0,1:T(4,128)(2,1)} %param.19) | copy-start | bytes 3076
  102.9 6.2 %collective-permute-start.9 = (f32[16,128]{1,0:T(8,128)}, f32[16,128]{1,0:T(8,128)S(1)}, u32[]{:S(2)}, u32[]{:S(2)}) collective-permute-start(f32[16,128]{1,0:T(8,128)} %get-tuple-element.41.refs_1_), channel_id=1, source_target_pairs={{0,3},{1,0},{2,1},{3,2},{4,7},{5,4},{6,5},{7,6},{8,11},{9,8},{10,9... | collective-permute-start | bytes 24584 | tf_op jit(solution)/shard_map/ppermute | solution.py:1201
  106.0 4.8 %collective-permute-start.8 = (f32[16,128]{1,0:T(8,128)}, f32[16,128]{1,0:T(8,128)S(1)}, u32[]{:S(2)}, u32[]{:S(2)}) collective-permute-start(f32[16,128]{1,0:T(8,128)} %get-tuple-element.41.refs_1_), channel_id=1, source_target_pairs={{0,2},{1,3},{2,0},{3,1},{4,6},{5,7},{6,4},{7,5},{8,10},{9,11},{10,... | collective-permute-start | bytes 24584 | tf_op jit(solution)/shard_map/ppermute | solution.py:1201
  106.6 5.7 %collective-permute-start.7 = (f32[16,128]{1,0:T(8,128)}, f32[16,128]{1,0:T(8,128)S(1)}, u32[]{:S(2)}, u32[]{:S(2)}) collective-permute-start(f32[16,128]{1,0:T(8,128)} %get-tuple-element.41.refs_1_), channel_id=1, source_target_pairs={{0,1},{1,2},{2,3},{3,0},{4,5},{5,6},{6,7},{7,4},{8,9},{9,10},{10,1... | collective-permute-start | bytes 24584 | tf_op jit(solution)/shard_map/ppermute | solution.py:1201
  122.9 9.3 %collective-permute-start.10 = (bf16[8,16,16,128]{3,2,1,0:T(8,128)(2,1)}, bf16[8,16,16,128]{3,2,1,0:T(8,128)(2,1)S(1)}, u32[]{:S(2)}, u32[]{:S(2)}) collective-permute-start(bf16[8,16,16,128]{3,2,1,0:T(8,128)(2,1)} %get-tuple-element.44), channel_id=1, source_target_pairs={{0,1},{1,2},{2,3},{4,5},{5,6},{6,7},{8,9},{9,10},{10,11},{12,13},{... | collective-permute-start | bytes 1572872 | tf_op jit(solution)/shard_map/ppermute | solution.py:1231
  125.0 11.3 %collective-permute-start.11 = (bf16[8,16,16,128]{3,2,1,0:T(8,128)(2,1)}, bf16[8,16,16,128]{3,2,1,0:T(8,128)(2,1)S(1)}, u32[]{:S(2)}, u32[]{:S(2)}) collective-permute-start(bf16[8,16,16,128]{3,2,1,0:T(8,128)(2,1)} %get-tuple-element.45), channel_id=1, source_target_pairs={{1,0},{2,1},{3,2},{5,4},{6,5},{7,6},{9,8},{10,9},{11,10},{13,12},{... | collective-permute-start | bytes 1572872 | tf_op jit(solution)/shard_map/ppermute | solution.py:1232
  164.6 3.8 %collective-permute-start.14 = (f32[2,128]{1,0:T(2,128)}, f32[2,128]{1,0:T(2,128)S(1)}, u32[]{:S(2)}, u32[]{:S(2)}) collective-permute-start(f32[2,128]{1,0:T(2,128)} %get-tuple-element.50.refs_11_), channel_id=1, source_target_pairs={{0,3},{1,0},{2,1},{3,2},{4,7},{5,4},{6,5},{7,6},{8,11},{9,8},{10,9... | collective-permute-start | bytes 3080 | tf_op jit(solution)/shard_map/ppermute | solution.py:1201
  164.8 4.7 %collective-permute-start.13 = (f32[2,128]{1,0:T(2,128)}, f32[2,128]{1,0:T(2,128)S(1)}, u32[]{:S(2)}, u32[]{:S(2)}) collective-permute-start(f32[2,128]{1,0:T(2,128)} %get-tuple-element.50.refs_11_), channel_id=1, source_target_pairs={{0,2},{1,3},{2,0},{3,1},{4,6},{5,7},{6,4},{7,5},{8,10},{9,11},{10,... | collective-permute-start | bytes 3080 | tf_op jit(solution)/shard_map/ppermute | solution.py:1201
  167.2 5.6 %collective-permute-start.12 = (f32[2,128]{1,0:T(2,128)}, f32[2,128]{1,0:T(2,128)S(1)}, u32[]{:S(2)}, u32[]{:S(2)}) collective-permute-start(f32[2,128]{1,0:T(2,128)} %get-tuple-element.50.refs_11_), channel_id=1, source_target_pairs={{0,1},{1,2},{2,3},{3,0},{4,5},{5,6},{6,7},{7,4},{8,9},{9,10},{10,1... | collective-permute-start | bytes 3080 | tf_op jit(solution)/shard_map/ppermute | solution.py:1201
  199.8 13.8 %all-to-all-start = ((f32[32,16,128]{2,1,0:T(8,128)}), f32[32,16,128]{2,1,0:T(8,128)S(1)}, u32[]{:S(2)}, u32[]{:S(2)}) async-start(f32[32,16,128]{2,1,0:T(8,128)} %bitcast.15), calls=%async_computation | async-start | bytes 524288 | tf_op jit(solution)/shard_map/all_to_all | solution.py:1208
  213.6 5.7 %copy-start.2 = (f32[32,16,128]{2,1,0:T(8,128)}, f32[32,16,128]{2,1,0:T(8,128)S(1)}, u32[]{:S(2)}) copy-start(f32[32,16,128]{2,1,0:T(8,128)S(1)} %all-to-all-done.r_ref) | copy-start | bytes 786436
  213.6 26.5 %all-to-all-start.2 = ((bf16[32,104,128]{2,1,0:T(8,128)(2,1)}), bf16[32,104,128]{2,1,0:T(8,128)(2,1)S(1)}, u32[]{:S(2)}, u32[]{:S(2)}) async-start(bf16[32,104,128]{2,1,0:T(8,128)(2,1)} %second_grad.1), calls=%async_computation.2 | async-start | bytes 1703936 | tf_op jit(solution)/shard_map/all_to_all | solution.py:1208
  240.1 4.5 %copy-start = (bf16[32,104,128]{2,1,0:T(8,128)(2,1)}, bf16[32,104,128]{2,1,0:T(8,128)(2,1)S(1)}, u32[]{:S(2)}) copy-start(bf16[32,104,128]{2,1,0:T(8,128)(2,1)S(1)} %all-to-all-done.2.refs_0_) | copy-start | bytes 2555908
  240.1 12.9 %all-to-all-start.1 = ((bf16[32,16,128]{2,1,0:T(8,128)(2,1)}), bf16[32,16,128]{2,1,0:T(8,128)(2,1)S(1)}, u32[]{:S(2)}, u32[]{:S(2)}) async-start(bf16[32,16,128]{2,1,0:T(8,128)(2,1)} %add_parts.1), calls=%async_computation.1 | async-start | bytes 262144 | tf_op jit(solution)/shard_map/all_to_all | solution.py:1208
  253.0 15.6 %all-to-all-start.3 = ((bf16[32,56,128]{2,1,0:T(8,128)(2,1)}), bf16[32,56,128]{2,1,0:T(8,128)(2,1)S(1)}, u32[]{:S(2)}, u32[]{:S(2)}) async-start(bf16[32,56,128]{2,1,0:T(8,128)(2,1)} %get-tuple-element.56), calls=%async_computation.3 | async-start | bytes 917504 | tf_op jit(solution)/shard_map/all_to_all | solution.py:1208
  (17 other events, 30.4 us)
